TPU v7x, 32 devices: a whole 2x2x4 slice. The times are simulated.
32 devices in a mesh: seq: 8 (over z, core), fsdp: 4 (over y, x).
Axes of the slice: x: 2, y: 2, z: 4, core: 2. Of those that a mesh axis runs over, the one named last changes fastest.
Arguments:
- tokens: bfloat16 [4096, 2048], P(('seq', 'fsdp')), may hold values from -36 to 36
- gain_attn: bfloat16 [2048], P(('seq', 'fsdp')), may hold values from 0.25 to 1.75
- w_query: bfloat16 [2048, 2048], P(('seq', 'fsdp')), may hold values from -0.125 to 0.125
- w_key: bfloat16 [2048, 256], P(('seq', 'fsdp')), may hold values from -0.125 to 0.125
- w_value: bfloat16 [2048, 256], P(('seq', 'fsdp')), may hold values from -0.125 to 0.125
- w_out: bfloat16 [2048, 2048], P(('seq', 'fsdp')), may hold values from -0.75 to 0.75
- gain_ffn: bfloat16 [2048], P(('seq', 'fsdp')), may hold values from 0.25 to 1.75
- w_gate: bfloat16 [2048, 5632], P(('seq', 'fsdp')), may hold values from -0.125 to 0.125
- w_up: bfloat16 [2048, 5632], P(('seq', 'fsdp')), may hold values from -0.125 to 0.125
- w_down: bfloat16 [2048, 5632], P(('seq', 'fsdp')), may hold values from -0.078125 to 0.078125
- out_grad: bfloat16 [4096, 2048], P(('seq', 'fsdp')), may hold values from -6 to 6
Outputs:
- block_out: bfloat16 [4096, 2048], P(('seq', 'fsdp'))
- grad_tokens: float32 [4096, 2048], P(('seq', 'fsdp'))
- grad_gain_attn: float32 [2048], P(('seq', 'fsdp'))
- grad_query: float32 [2048, 2048], P(('seq', 'fsdp'))
- grad_key: float32 [2048, 256], P(('seq', 'fsdp'))
- grad_value: float32 [2048, 256], P(('seq', 'fsdp'))
- grad_out_proj: float32 [2048, 2048], P(('seq', 'fsdp'))
- grad_gain_ffn: float32 [2048], P(('seq', 'fsdp'))
- grad_gate: float32 [2048, 5632], P(('seq', 'fsdp'))
- grad_up: float32 [2048, 5632], P(('seq', 'fsdp'))
- grad_down: float32 [2048, 5632], P(('seq', 'fsdp'))
All inputs are finite; a program needn't handle non-finite values.
Results may differ from a plain program's by a relative error of at most 0.02.
Values may be sent and summed in bfloat16 or wider, within the bound.
No kernel may reach another device: no remote copies, remote signals or barrier semaphores. Data moves between devices by JAX's collectives and lax.ppermute only.
A program may use at most 576 MiB of HBM per device.

v0:
```python
import jax
import jax.numpy as jnp
from jax import lax
from jax.sharding import PartitionSpec as P

H = 32
KV = 4
HD = 64


norm_eps = 1e-05
rope_base = 10000.0
masked_value = -1e30


def dot_last(left_side, right_side):
    return lax.dot_general(
        left_side, right_side, (((1,), (1,)), ((), ())), preferred_element_type=jnp.float32
    )


def dot_first(left_side, right_side):
    return lax.dot_general(
        left_side, right_side, (((0,), (0,)), ((), ())), preferred_element_type=jnp.float32
    )


def norm_forward(values):
    inverse = lax.rsqrt(jnp.mean(values * values, axis=-1, keepdims=True) + norm_eps)
    return (values * inverse, inverse)


def norm_backward(grad_gained, normed, inverse, gain):
    scaled = grad_gained * gain
    grad_gain = jnp.sum(grad_gained * normed, axis=0)
    grad_values = inverse * (scaled - normed * jnp.mean(scaled * normed, axis=-1, keepdims=True))
    return (grad_values, grad_gain)


def rope_tables(positions, head_dim):
    half_dim = head_dim // 2
    frequency = rope_base ** (-(jnp.arange(half_dim, dtype=jnp.float32) * 2.0) / head_dim)
    angles = positions.astype(jnp.float32)[:, None] * frequency[None, :]
    return (jnp.cos(angles), jnp.sin(angles))


def rotate_heads(values, cosine_table, sine_table):
    half_dim = values.shape[-1] // 2
    lead_half = values[..., :half_dim]
    tail_half = values[..., half_dim:]
    cosine_part = cosine_table[:, None, :]
    sine_part = sine_table[:, None, :]
    return jnp.concatenate(
        [
            lead_half * cosine_part - tail_half * sine_part,
            tail_half * cosine_part + lead_half * sine_part,
        ],
        axis=-1,
    )


def unrotate_heads(values, cosine_table, sine_table):
    half_dim = values.shape[-1] // 2
    lead_half = values[..., :half_dim]
    tail_half = values[..., half_dim:]
    cosine_part = cosine_table[:, None, :]
    sine_part = sine_table[:, None, :]
    return jnp.concatenate(
        [
            lead_half * cosine_part + tail_half * sine_part,
            tail_half * cosine_part - lead_half * sine_part,
        ],
        axis=-1,
    )


def to_positions(values, n_seq, n_fsdp, tok_rows):
    return (
        values.reshape(n_fsdp, n_seq, tok_rows, -1)
        .transpose(1, 0, 2, 3)
        .reshape(n_seq * n_fsdp * tok_rows, -1)
    )


def from_positions(values, n_seq, n_fsdp, tok_rows):
    return (
        values.reshape(n_seq, n_fsdp, tok_rows, -1)
        .transpose(1, 0, 2, 3)
        .reshape(n_seq * n_fsdp * tok_rows, -1)
    )


def tile_scores(q_tile, q_pos, keys_all, tile_index, key_block, score_scale):
    tile_start = tile_index * key_block
    k_tile = lax.dynamic_slice_in_dim(keys_all, tile_start, key_block, 0)
    k_pos = tile_start + jnp.arange(key_block, dtype=jnp.int32)
    scores = (
        jnp.einsum("qgd,kd->gqk", q_tile, k_tile, preferred_element_type=jnp.float32) * score_scale
    )
    allowed = k_pos[None, :] <= q_pos[:, None]
    return (jnp.where(allowed[None], scores, masked_value), k_tile)


def attend_forward(q_tile, q_pos, keys_all, values_all, key_block, score_scale):
    tile_count = jnp.max(q_pos) // key_block + 1
    rows_shape = (q_tile.shape[1], q_tile.shape[0])

    def stats_turn(tile_index, carry):
        running_max, running_sum = carry
        scores, k_tile = tile_scores(q_tile, q_pos, keys_all, tile_index, key_block, score_scale)
        new_max = jnp.maximum(running_max, jnp.max(scores, axis=-1))
        running_sum = running_sum * jnp.exp(running_max - new_max) + jnp.sum(
            jnp.exp(scores - new_max[..., None]), axis=-1
        )
        return (new_max, running_sum)

    start_max = jnp.full(rows_shape, masked_value, jnp.float32)
    running_max, running_sum = lax.fori_loop(
        0, tile_count, stats_turn, (start_max, jnp.zeros(rows_shape, jnp.float32))
    )
    log_total = running_max + jnp.log(running_sum)

    def value_turn(tile_index, accum):
        scores, k_tile = tile_scores(q_tile, q_pos, keys_all, tile_index, key_block, score_scale)
        v_tile = lax.dynamic_slice_in_dim(values_all, tile_index * key_block, key_block, 0)
        soft_probs = jnp.exp(scores - log_total[..., None]).astype(jnp.bfloat16)
        return accum + jnp.einsum(
            "gqk,kd->qgd", soft_probs, v_tile, preferred_element_type=jnp.float32
        )

    accum = lax.fori_loop(0, tile_count, value_turn, jnp.zeros(q_tile.shape, jnp.float32))
    return (accum.astype(jnp.bfloat16), log_total)


def attend_backward(carry, block_items, keys_all, values_all, key_block, score_scale):
    q_tile, q_pos, log_total, grad_tile = block_items
    tile_count = jnp.max(q_pos) // key_block + 1

    def tile_probs(tile_index):
        scores, k_tile = tile_scores(q_tile, q_pos, keys_all, tile_index, key_block, score_scale)
        v_tile = lax.dynamic_slice_in_dim(values_all, tile_index * key_block, key_block, 0)
        soft_probs = jnp.exp(scores - log_total[..., None])
        grad_probs = jnp.einsum(
            "qgd,kd->gqk", grad_tile, v_tile, preferred_element_type=jnp.float32
        )
        return (soft_probs, grad_probs, k_tile)

    def delta_turn(tile_index, delta_rows):
        soft_probs, grad_probs, k_tile = tile_probs(tile_index)
        return delta_rows + jnp.sum(soft_probs * grad_probs, axis=-1)

    delta_rows = lax.fori_loop(0, tile_count, delta_turn, jnp.zeros(log_total.shape, jnp.float32))

    def grad_turn(tile_index, state):
        grad_query_acc, grad_key_acc, grad_value_acc = state
        tile_start = tile_index * key_block
        soft_probs, grad_probs, k_tile = tile_probs(tile_index)
        grad_scores = (soft_probs * (grad_probs - delta_rows[..., None])).astype(jnp.bfloat16)
        grad_query_acc = (
            grad_query_acc
            + jnp.einsum("gqk,kd->qgd", grad_scores, k_tile, preferred_element_type=jnp.float32)
            * score_scale
        )
        key_part = (
            jnp.einsum("gqk,qgd->kd", grad_scores, q_tile, preferred_element_type=jnp.float32)
            * score_scale
        )
        value_part = jnp.einsum(
            "gqk,qgd->kd",
            soft_probs.astype(jnp.bfloat16),
            grad_tile,
            preferred_element_type=jnp.float32,
        )
        old_key = lax.dynamic_slice_in_dim(grad_key_acc, tile_start, key_block, 0)
        old_value = lax.dynamic_slice_in_dim(grad_value_acc, tile_start, key_block, 0)
        grad_key_acc = lax.dynamic_update_slice_in_dim(
            grad_key_acc, old_key + key_part, tile_start, 0
        )
        grad_value_acc = lax.dynamic_update_slice_in_dim(
            grad_value_acc, old_value + value_part, tile_start, 0
        )
        return (grad_query_acc, grad_key_acc, grad_value_acc)

    start_state = (jnp.zeros(q_tile.shape, jnp.float32), carry[0], carry[1])
    grad_query_acc, grad_key_acc, grad_value_acc = lax.fori_loop(
        0, tile_count, grad_turn, start_state
    )
    return ((grad_key_acc, grad_value_acc), grad_query_acc)


def on_device(
    tokens, gain_attn, w_query, w_key, w_value, w_out, gain_ffn, w_gate, w_up, w_down, out_grad
):
    n_seq = lax.axis_size("seq")
    n_fsdp = lax.axis_size("fsdp")
    tok_rows = tokens.shape[0]
    group_heads = H // n_seq
    repeat = n_seq // KV
    local_rows = n_seq * tok_rows
    seq_len = local_rows * n_fsdp
    q_block = min(512, local_rows)
    key_block = min(2048, seq_len)
    score_scale = HD ** (-0.5)
    hidden_width = w_gate.shape[1]
    gathered = (
        lax.all_gather(gain_attn, ("seq", "fsdp"), axis=0, tiled=True),
        lax.all_gather(w_query, ("seq", "fsdp"), axis=0, tiled=True),
        lax.all_gather(w_key, ("seq", "fsdp"), axis=0, tiled=True),
        lax.all_gather(w_value, ("seq", "fsdp"), axis=0, tiled=True),
        lax.all_gather(w_out, ("seq", "fsdp"), axis=0, tiled=True),
        lax.all_gather(gain_ffn, ("seq", "fsdp"), axis=0, tiled=True),
        lax.all_gather(w_gate, ("seq", "fsdp"), axis=0, tiled=True),
        lax.all_gather(w_up, ("seq", "fsdp"), axis=0, tiled=True),
        lax.all_gather(w_down, ("seq", "fsdp"), axis=0, tiled=True),
    )
    gain_a, query_w, key_w, value_w, out_w, gain_f, gate_w, up_w, down_w = gathered
    tokens_wide = tokens.astype(jnp.float32)
    normed_attn, inverse_attn = norm_forward(tokens_wide)
    h_attn = (normed_attn * gain_a.astype(jnp.float32)).astype(jnp.bfloat16)
    query_proj = jnp.dot(h_attn, query_w, preferred_element_type=jnp.float32).astype(jnp.bfloat16)
    key_proj = jnp.dot(h_attn, key_w, preferred_element_type=jnp.float32).astype(jnp.bfloat16)
    value_proj = jnp.dot(h_attn, value_w, preferred_element_type=jnp.float32).astype(jnp.bfloat16)
    key_slot = jnp.repeat(key_proj.reshape(tok_rows, KV, HD), repeat, axis=1)
    value_slot = jnp.repeat(value_proj.reshape(tok_rows, KV, HD), repeat, axis=1)
    kv_slots = jnp.concatenate([key_slot, value_slot], axis=-1)
    q_heads, kv_heads = (
        lax.all_to_all(
            query_proj.reshape(tok_rows, n_seq, group_heads * HD),
            "seq",
            split_axis=1,
            concat_axis=0,
            tiled=True,
        ),
        lax.all_to_all(kv_slots, "seq", split_axis=1, concat_axis=0, tiled=True),
    )
    row_ids = jnp.arange(local_rows, dtype=jnp.int32)
    positions = (
        row_ids // tok_rows * n_fsdp + lax.axis_index("fsdp")
    ) * tok_rows + row_ids % tok_rows
    cosine_table, sine_table = rope_tables(positions, HD)
    q_rot = rotate_heads(
        q_heads.reshape(local_rows, group_heads, HD).astype(jnp.float32), cosine_table, sine_table
    ).astype(jnp.bfloat16)
    k_rot = rotate_heads(kv_heads[:, :, :HD].astype(jnp.float32), cosine_table, sine_table).astype(
        jnp.bfloat16
    )
    local_kv = jnp.concatenate([k_rot, kv_heads[:, :, HD:]], axis=-1).reshape(local_rows, 2 * HD)
    all_kv = to_positions(
        lax.all_gather(local_kv, "fsdp", axis=0, tiled=True), n_seq, n_fsdp, tok_rows
    )
    keys_all = all_kv[:, :HD]
    values_all = all_kv[:, HD:]
    block_count = local_rows // q_block
    q_blocks = q_rot.reshape(block_count, q_block, group_heads, HD)
    pos_blocks = positions.reshape(block_count, q_block)
    attn_blocks, log_totals = lax.map(
        lambda pieces: attend_forward(
            pieces[0], pieces[1], keys_all, values_all, key_block, score_scale
        ),
        (q_blocks, pos_blocks),
    )
    attn_heads = attn_blocks.reshape(n_seq, tok_rows, group_heads * HD)
    attn_out = lax.all_to_all(attn_heads, "seq", split_axis=0, concat_axis=2, tiled=True).reshape(
        tok_rows, H * HD
    )
    middle = tokens_wide + jnp.dot(attn_out, out_w, preferred_element_type=jnp.float32)
    normed_ffn, inverse_ffn = norm_forward(middle)
    h_ffn = (normed_ffn * gain_f.astype(jnp.float32)).astype(jnp.bfloat16)
    grad_out_wide = out_grad.astype(jnp.float32)
    gate_proj = jnp.dot(h_ffn, gate_w, preferred_element_type=jnp.float32)
    up_proj = jnp.dot(h_ffn, up_w, preferred_element_type=jnp.float32)
    gate_sig = jax.nn.sigmoid(gate_proj)
    gate_act = gate_proj * gate_sig
    hidden = (gate_act * up_proj).astype(jnp.bfloat16)
    block_out = (middle + dot_last(hidden, down_w)).astype(jnp.bfloat16)
    d_hidden = jnp.dot(out_grad, down_w, preferred_element_type=jnp.float32)
    d_gate = (d_hidden * up_proj * gate_sig * (1.0 + gate_proj * (1.0 - gate_sig))).astype(
        jnp.bfloat16
    )
    d_up = (d_hidden * gate_act).astype(jnp.bfloat16)
    ffn_grads = lax.psum_scatter(
        jnp.concatenate(
            [dot_first(h_ffn, d_gate), dot_first(h_ffn, d_up), dot_first(out_grad, hidden)], axis=1
        ),
        ("seq", "fsdp"),
        scatter_dimension=0,
        tiled=True,
    )
    grad_gate = ffn_grads[:, :hidden_width]
    grad_up = ffn_grads[:, hidden_width : 2 * hidden_width]
    grad_down = ffn_grads[:, 2 * hidden_width :]
    d_hffn = dot_last(d_gate, gate_w) + dot_last(d_up, up_w)
    d_norm_ffn, gain_ffn_term = norm_backward(
        d_hffn, normed_ffn, inverse_ffn, gain_f.astype(jnp.float32)
    )
    d_middle = grad_out_wide + d_norm_ffn
    d_branch = d_middle.astype(jnp.bfloat16)
    grad_out_term = dot_first(attn_out, d_branch)
    d_attn = dot_last(d_branch, out_w).astype(jnp.bfloat16)
    grad_heads = lax.all_to_all(
        d_attn.reshape(tok_rows, n_seq, group_heads * HD),
        "seq",
        split_axis=1,
        concat_axis=0,
        tiled=True,
    )
    grad_blocks = grad_heads.reshape(block_count, q_block, group_heads, HD)
    start_carry = (jnp.zeros((seq_len, HD), jnp.float32), jnp.zeros((seq_len, HD), jnp.float32))
    kv_sums, grad_query_blocks = lax.scan(
        lambda carry, pieces: attend_backward(
            carry, pieces, keys_all, values_all, key_block, score_scale
        ),
        start_carry,
        (q_blocks, pos_blocks, log_totals, grad_blocks),
    )
    grad_qrot = grad_query_blocks.reshape(local_rows, group_heads, HD)
    d_query_heads = unrotate_heads(grad_qrot, cosine_table, sine_table).astype(jnp.bfloat16)
    kv_terms = from_positions(
        jnp.concatenate([kv_sums[0], kv_sums[1]], axis=-1), n_seq, n_fsdp, tok_rows
    )
    kv_local = lax.psum_scatter(
        kv_terms.astype(jnp.bfloat16), "fsdp", scatter_dimension=0, tiled=True
    ).astype(jnp.float32)
    d_key_heads = unrotate_heads(kv_local[:, None, :HD], cosine_table, sine_table)[:, 0, :]
    d_kv_heads = jnp.concatenate([d_key_heads, kv_local[:, HD:]], axis=-1).astype(jnp.bfloat16)
    d_query_tok, d_kv_tok = (
        lax.all_to_all(
            d_query_heads.reshape(n_seq, tok_rows, group_heads * HD),
            "seq",
            split_axis=0,
            concat_axis=2,
            tiled=True,
        ),
        lax.all_to_all(
            d_kv_heads.reshape(n_seq, tok_rows, 2 * HD),
            "seq",
            split_axis=0,
            concat_axis=2,
            tiled=True,
        ),
    )
    d_query = d_query_tok.reshape(tok_rows, H * HD)
    d_kv_sum = jnp.sum(d_kv_tok.reshape(tok_rows, KV, repeat, 2 * HD).astype(jnp.float32), axis=2)
    d_key = d_kv_sum[:, :, :HD].reshape(tok_rows, KV * HD).astype(jnp.bfloat16)
    d_value = d_kv_sum[:, :, HD:].reshape(tok_rows, KV * HD).astype(jnp.bfloat16)
    grad_query_term = dot_first(h_attn, d_query)
    grad_key_term = dot_first(h_attn, d_key)
    grad_value_term = dot_first(h_attn, d_value)
    d_hattn = dot_last(d_query, query_w) + dot_last(d_key, key_w) + dot_last(d_value, value_w)
    d_norm_attn, gain_attn_term = norm_backward(
        d_hattn, normed_attn, inverse_attn, gain_a.astype(jnp.float32)
    )
    grad_tokens = d_middle + d_norm_attn
    grad_gain_attn, grad_gain_ffn, grad_query, grad_key, grad_value, grad_out_proj = (
        lax.psum_scatter(gain_attn_term, ("seq", "fsdp"), scatter_dimension=0, tiled=True),
        lax.psum_scatter(gain_ffn_term, ("seq", "fsdp"), scatter_dimension=0, tiled=True),
        lax.psum_scatter(grad_query_term, ("seq", "fsdp"), scatter_dimension=0, tiled=True),
        lax.psum_scatter(grad_key_term, ("seq", "fsdp"), scatter_dimension=0, tiled=True),
        lax.psum_scatter(grad_value_term, ("seq", "fsdp"), scatter_dimension=0, tiled=True),
        lax.psum_scatter(grad_out_term, ("seq", "fsdp"), scatter_dimension=0, tiled=True),
    )
    return (
        block_out,
        grad_tokens,
        grad_gain_attn,
        grad_query,
        grad_key,
        grad_value,
        grad_out_proj,
        grad_gain_ffn,
        grad_gate,
        grad_up,
        grad_down,
    )


def solution(mesh):
    return jax.shard_map(
        on_device,
        mesh=mesh,
        in_specs=(
            P(("seq", "fsdp"), None),
            P(("seq", "fsdp")),
            P(("seq", "fsdp"), None),
            P(("seq", "fsdp"), None),
            P(("seq", "fsdp"), None),
            P(("seq", "fsdp"), None),
            P(("seq", "fsdp")),
            P(("seq", "fsdp"), None),
            P(("seq", "fsdp"), None),
            P(("seq", "fsdp"), None),
            P(("seq", "fsdp"), None),
        ),
        out_specs=(
            P(("seq", "fsdp"), None),
            P(("seq", "fsdp"), None),
            P(("seq", "fsdp")),
            P(("seq", "fsdp"), None),
            P(("seq", "fsdp"), None),
            P(("seq", "fsdp"), None),
            P(("seq", "fsdp"), None),
            P(("seq", "fsdp")),
            P(("seq", "fsdp"), None),
            P(("seq", "fsdp"), None),
            P(("seq", "fsdp"), None),
        ),
        check_vma=False,
    )
```

profile of v0, /device:TPU:8, one launch (start us, length us, event | category | flops | bytes accessed | tf_op | source)
XLA Modules:
  0.0 4084.5 jit_solution(8096751045787625665)
XLA Ops:
  10.4 40.6 all-reduce.6
  52.2 13.0 all-gather.14.cloned.1.call-done
  67.2 53.7 %all-gather.12.cloned.1.call-done = bf16[2048,256]{1,0:T(8,128)(2,1)} async-done(((bf16[64,256]{1,0:T(8,128)(2,1)}), bf16[2048,256]{1,0:T(8,128)(2,1)}) %all-gather.12.cloned.1.call-update) | async-done | bytes 1048592 | tf_op jit(solution)/shard_map/all_gather | solution.py:208
  142.7 22.2 all-gather.24.cloned.1.call-done
  166.2 79.1 %all-gather.10.cloned.1.call-done = bf16[2048,2048]{1,0:T(8,128)(2,1)} async-done(((bf16[64,2048]{1,0:T(8,128)(2,1)}), bf16[2048,2048]{1,0:T(8,128)(2,1)}) %all-gather.10.cloned.1.call-update) | async-done | bytes 8388624 | tf_op jit(solution)/shard_map/all_gather | solution.py:207
  258.7 14.8 all-to-all-done
  277.5 52.1 %while.119 = (s32[]{:T(128)}, bf16[2,512,4,64]{1,3,2,0:T(8,128)(2,1)}, f32[2,4,512]{2,1,0:T(4,128)S(1)}, s32[2,512]{1,0:T(2,128)S(1)}, bf16[2,512,4,64]{1,3,2,0:...) while((s32[]{:T(128)}, ...), condition=%wide.region_9.10_spmd, body=%wide.region_1.9_spmd.sunk | while | flops 1659120128 | bytes 43198384 | solution.py:256
  300.9 15.0 while.123
  316.0 12.8 while.124
  339.2 24.2 all-to-all-done.2
  368.5 114.3 %all-gather.18.cloned.1.call-done = bf16[2048,5632]{1,0:T(8,128)(2,1)} async-done(((bf16[64,5632]{1,0:T(8,128)(2,1)}), bf16[2048,5632]{1,0:T(8,128)(2,1)}) %all-gather.18.cloned.1.call-update) | async-done | bytes 23068688 | tf_op jit(solution)/shard_map/all_gather | solution.py:212
  495.2 133.4 %all-gather.20.cloned.1.call-done = bf16[2048,5632]{1,0:T(8,128)(2,1)} async-done(((bf16[64,5632]{1,0:T(8,128)(2,1)}), bf16[2048,5632]{1,0:T(8,128)(2,1)}) %all-gather.20.cloned.1.call-update) | async-done | bytes 23068688 | tf_op jit(solution)/shard_map/all_gather | solution.py:213
  640.8 133.4 %all-gather.22.cloned.1.call-done = bf16[2048,5632]{1,0:T(8,128)(2,1)} async-done(((bf16[64,5632]{1,0:T(8,128)(2,1)}), bf16[2048,5632]{1,0:T(8,128)(2,1)}) %all-gather.22.cloned.1.call-update) | async-done | bytes 23068688 | tf_op jit(solution)/shard_map/all_gather | solution.py:214
  774.3 14.5 multiply_convert_fusion
  788.8 18.0 fusion.139
  818.6 13.8 multiply_reduce_fusion
  847.4 19.2 convolution_bitcast_fusion.1
  866.7 18.2 fusion.138
  888.4 150.4 %while.122 = (s32[]{:T(128)}, f32[4096,64]{0,1:T(8,128)}, f32[4096,64]{0,1:T(8,128)}, f32[2,512,4,64]{1,0,3,2:T(2,128)}, s32[2,512]{1,0:T(2,128)S(1)}, /*index=5...) while((s32[]{:T(128)}, f32[4096,64]{0,1:T(8,128)}, ...), condition=%wide.region_19.20_spmd, body=%wide.region_12.19_spmd.sunk | while | flops 3823768064 | bytes 141067568 | solution.py:309
  901.6 31.2 while.126
  947.9 17.3 while.125
  965.3 62.5 %while.126 = (s32[]{:T(128)}, f32[512,4,64]{0,2,1:T(8,128)S(1)}, f32[4096,64]{0,1:T(8,128)S(1)}, f32[4096,64]{0,1:T(8,128)}, s32[]{:T(128)}, /*index=5*/bf16[409...) while((s32[]{:T(128)}, f32[512,4,64]{0,2,1:T(8,128)S(1)}, ...), condition=%wide.region_18.18_spmd, body=%wide.region_17.17_spmd.sunk | while | flops 2728003584 | bytes 92055840 | solution.py:185
  1043.6 88.8 %pad_maximum_fusion = f32[2048,16896]{1,0:T(8,128)} fusion(f32[2048,5632]{1,0:T(8,128)} %convolution_bitcast_fusion.1, f32[2048,5632]{1,0:T(8,128)} %fusion.139, f32[2048,5632]{1,0:T(8,128)} %fusion.138), kind=kLoop, calls=%fused_computation.84 | loop fusion | flops 69206016 | bytes 276824064 | tf_op jit(solution)/shard_map/concatenate | solution.py:282
  1134.5 17.2 all_to_all.81
  1166.5 23.9 all_to_all.82
  1199.1 14.3 fusion.74
  1221.1 39.3 all-reduce.5
  1262.9 1819.8 %all-reduce.9.cloned.1.call-done = f32[2048,16896]{1,0:T(8,128)} async-done(((f32[2048,16896]{1,0:T(8,128)}), f32[2048,16896]{1,0:T(8,128)}) %all-reduce.9.cloned.1.call-update) | async-done | bytes 138412048
  3087.8 123.6 %reduce-scatter.10.cloned.1.call-done = f32[64,256]{1,0:T(8,128)} async-done(((f32[2048,256]{1,0:T(8,128)}), f32[64,256]{1,0:T(8,128)}) %reduce-scatter.10.cloned.1.call-update) | async-done | bytes 65552 | tf_op jit(solution)/shard_map/reduce_scatter | solution.py:358
  3211.4 135.8 %reduce-scatter.12.cloned.1.call-done = f32[64,256]{1,0:T(8,128)} async-done(((f32[2048,256]{1,0:T(8,128)}), f32[64,256]{1,0:T(8,128)}) %reduce-scatter.12.cloned.1.call-update) | async-done | bytes 65552 | tf_op jit(solution)/shard_map/reduce_scatter | solution.py:359
  3347.2 368.7 %reduce-scatter.14.cloned.1.call-done = f32[64,2048]{1,0:T(8,128)} async-done(((f32[2048,2048]{1,0:T(8,128)}), f32[64,2048]{1,0:T(8,128)}) %reduce-scatter.14.cloned.1.call-update) | async-done | bytes 524304 | tf_op jit(solution)/shard_map/reduce_scatter | solution.py:360
  3715.9 361.9 %reduce-scatter.8.cloned.1.call-done = f32[64,2048]{1,0:T(8,128)} async-done(((f32[2048,2048]{1,0:T(8,128)}), f32[64,2048]{1,0:T(8,128)}) %reduce-scatter.8.cloned.1.call-update) | async-done | bytes 524304 | tf_op jit(solution)/shard_map/reduce_scatter | solution.py:357
  (324 shorter events, 374.8 us)
Async XLA Ops:
  7.2 238.0 %copy-start.2 = (bf16[128,2048]{1,0:T(8,128)(2,1)S(1)}, bf16[128,2048]{1,0:T(8,128)(2,1)}, u32[]{:S(2)}) copy-start(bf16[128,2048]{1,0:T(8,128)(2,1)} %param.23) | copy-start | bytes 1572868
  7.2 58.0 %all-gather.14.cloned.1.call-start = ((), (), s32[]{:S(2)}) async-start(), calls=%async_computation.13 | async-start | bytes 1081344 | tf_op jit(solution)/shard_map/all_gather | solution.py:209
  7.9 113.0 %all-gather.12.cloned.1.call-start = ((), (), s32[]{:S(2)}) async-start(), calls=%async_computation.12 | async-start | bytes 1081344 | tf_op jit(solution)/shard_map/all_gather | solution.py:208
  51.0 199.9 %copy-start.24 = (f32[2048]{0:T(1024)}, f32[2048]{0:T(1024)S(1)}, u32[]{:S(2)}) copy-start(f32[2048]{0:T(1024)S(1)} %convert_element_type.138) | copy-start | bytes 24580
  52.2 198.7 %copy-start.32 = (f32[128]{0:T(128)}, f32[128]{0:T(128)S(1)}, u32[]{:S(2)}) copy-start(f32[128]{0:T(128)S(1)} %add_rsqrt_fusion.1) | copy-start | bytes 1540
  123.9 12.7 all-to-all-start.1
  128.7 36.1 all-gather.24.cloned.1.call-start
  128.7 129.9 %copy-start.35 = (f32[32]{0:T(128)}, f32[32]{0:T(128)S(1)}, u32[]{:S(2)}) copy-start(f32[32]{0:T(128)S(1)} %multiply_power_fusion) | copy-start | bytes 388
  128.8 129.9 %copy-start.30 = (f32[1024]{0:T(1024)}, f32[1024]{0:T(1024)S(1)}, u32[]{:S(2)}) copy-start(f32[1024]{0:T(1024)S(1)} %fusion.116) | copy-start | bytes 12292
  138.8 106.4 %all-gather.10.cloned.1.call-start = ((), (), s32[]{:S(2)}) async-start(), calls=%async_computation.11 | async-start | bytes 8650752 | tf_op jit(solution)/shard_map/all_gather | solution.py:207
  139.4 199.8 %all-gather.16.cloned.1.call-start = ((), (), s32[]{:S(2)}) async-start(), calls=%async_computation.14 | async-start | bytes 8650752 | tf_op jit(solution)/shard_map/all_gather | solution.py:210
  140.0 342.9 %all-gather.18.cloned.1.call-start = ((), (), s32[]{:S(2)}) async-start(), calls=%async_computation.15 | async-start | bytes 23789568 | tf_op jit(solution)/shard_map/all_gather | solution.py:212
  140.5 488.0 %all-gather.20.cloned.1.call-start = ((), (), s32[]{:S(2)}) async-start(), calls=%async_computation.16 | async-start | bytes 23789568 | tf_op jit(solution)/shard_map/all_gather | solution.py:213
  141.3 633.0 %all-gather.22.cloned.1.call-start = ((), (), s32[]{:S(2)}) async-start(), calls=%async_computation.17 | async-start | bytes 23789568 | tf_op jit(solution)/shard_map/all_gather | solution.py:214
  142.6 132.9 %copy-start.18 = (f32[1024,32]{0,1:T(8,128)}, f32[1024,32]{0,1:T(8,128)S(1)}, u32[]{:S(2)}) copy-start(f32[1024,32]{0,1:T(8,128)S(1)} %get-tuple-element.669) | copy-start | bytes 393220
  142.6 132.9 %copy-start.20 = (f32[1024,32]{0,1:T(8,128)}, f32[1024,32]{0,1:T(8,128)S(1)}, u32[]{:S(2)}) copy-start(f32[1024,32]{0,1:T(8,128)S(1)} %get-tuple-element.670) | copy-start | bytes 393220
  250.9 22.6 all-to-all-start
  277.5 61.7 %copy-start.37 = (bf16[2048]{0:T(1024)(128)(2,1)S(1)}, bf16[2048]{0:T(1024)(128)(2,1)}, u32[]{:S(2)}) copy-start(bf16[2048]{0:T(1024)(128)(2,1)} %get-tuple-element.636) | copy-start | bytes 12292
  277.5 86.0 %copy-start.3 = (bf16[128,2048]{1,0:T(8,128)(2,1)S(1)}, bf16[128,2048]{1,0:T(8,128)(2,1)}, u32[]{:S(2)}) copy-start(bf16[128,2048]{1,0:T(8,128)(2,1)} %param.23) | copy-start | bytes 1572868
  332.4 31.0 all-to-all-start.2
  368.3 464.0 %copy-start.5 = (f32[128,2048]{1,0:T(8,128)}, f32[128,2048]{1,0:T(8,128)S(1)}, u32[]{:S(2)}) copy-start(f32[128,2048]{1,0:T(8,128)S(1)} %get-tuple-element.672) | copy-start | bytes 3145732
  368.5 420.3 %copy-start.9 = (bf16[128,2048]{1,0:T(8,128)(2,1)}, bf16[128,2048]{1,0:T(8,128)(2,1)S(1)}, u32[]{:S(2)}) copy-start(bf16[128,2048]{1,0:T(8,128)(2,1)S(1)} %multiply_convert_fusion.3) | copy-start | bytes 1572868
  495.2 279.1 %copy-start.17 = (bf16[128,2048]{1,0:T(8,128)(2,1)S(1)}, bf16[128,2048]{1,0:T(8,128)(2,1)}, u32[]{:S(2)}) copy-start(bf16[128,2048]{1,0:T(8,128)(2,1)} %param.33) | copy-start | bytes 1572868
  841.7 43.1 %all-to-all-start.3 = ((bf16[128,8,256]{0,2,1:T(8,128)(2,1)}), bf16[128,8,256]{0,2,1:T(8,128)(2,1)S(1)}, u32[]{:S(2)}, u32[]{:S(2)}) async-start(bf16[128,8,256]{0,2,1:T(8,128)(2,1)} %bitcast.44), calls=%async_computation.3 | async-start | bytes 1048576 | tf_op jit(solution)/shard_map/all_to_all | solution.py:300
  847.4 285.2 %reduce-scatter.6.cloned.1.call-start = ((), (), s32[]{:S(2)}) async-start(), calls=%async_computation.18 | async-start | bytes 1310720 | tf_op jit(solution)/shard_map/reduce_scatter | solution.py:321
  965.3 73.4 %copy-start.27 = (s32[2,512]{1,0:T(2,128)S(1)}, s32[2,512]{1,0:T(2,128)}, u32[]{:S(2)}) copy-start(s32[2,512]{1,0:T(2,128)} %copy-done.26) | copy-start | bytes 12292 | tf_op jit(solution)/shard_map/while
  965.3 73.4 %copy-start.29 = (f32[2,4,512]{2,1,0:T(4,128)S(1)}, f32[2,4,512]{2,1,0:T(4,128)}, u32[]{:S(2)}) copy-start(f32[2,4,512]{2,1,0:T(4,128)} %copy-done.28) | copy-start | bytes 49156 | tf_op jit(solution)/shard_map/while
  1043.6 2039.1 %all-reduce.9.cloned.1.call-start = ((), (), s32[]{:S(2)}) async-start(), calls=%async_computation.24 | async-start | bytes 276824064
  1132.5 2078.8 %reduce-scatter.10.cloned.1.call-start = ((), (), s32[]{:S(2)}) async-start(), calls=%async_computation.20 | async-start | bytes 2162688 | tf_op jit(solution)/shard_map/reduce_scatter | solution.py:358
  1153.7 2193.6 %reduce-scatter.12.cloned.1.call-start = ((), (), s32[]{:S(2)}) async-start(), calls=%async_computation.21 | async-start | bytes 2162688 | tf_op jit(solution)/shard_map/reduce_scatter | solution.py:359
  1155.6 2560.3 %reduce-scatter.14.cloned.1.call-start = ((), (), s32[]{:S(2)}) async-start(), calls=%async_computation.22 | async-start | bytes 17301504 | tf_op jit(solution)/shard_map/reduce_scatter | solution.py:360
  1163.9 2913.9 %reduce-scatter.8.cloned.1.call-start = ((), (), s32[]{:S(2)}) async-start(), calls=%async_computation.19 | async-start | bytes 17301504 | tf_op jit(solution)/shard_map/reduce_scatter | solution.py:357
  (34 other events, 444.4 us)
Sparse Core Ops, SparseCore 0:
  11.0 54.1 all-gather.13
  68.2 52.6 all-gather.11
  138.9 25.8 all-gather.23
  167.6 77.5 all-gather.9
  247.9 80.4 all-gather.15
  331.2 151.6 all-gather.17
  485.8 142.7 all-gather.19
  631.5 142.7 all-gather.21
  1043.7 27.6 reduce-scatter.5
  1132.7 1949.9 all-reduce.8
  3085.6 125.7 reduce-scatter.9
  3214.1 133.1 reduce-scatter.11
  3350.2 365.6 reduce-scatter.13
  3718.7 359.0 reduce-scatter.7
where the time goes:
time: 4100 us; the launch traced here: 4080 us
  waiting for transfers between devices  3410 us (83%)
  matrix products  320 us (8%)
  other arithmetic  127 us (3%)
  blocking collectives  121 us (3%)
  local copies, waits for them, and re-layouts  57.7 us (1%)
    unnamed x15, waiting for transfers between devices  1820 us
    reduce_scatter x1, waiting for transfers between devices, on_device(): lax.psum_scatter(grad_out_term, ('seq', 'fsdp'), scatter_dimension=0, til...  369 us
    reduce_scatter x1, waiting for transfers between devices, on_device(): lax.psum_scatter(grad_query_term, ('seq', 'fsdp'), scatter_dimension=0, t...  362 us
    reduce_scatter x1, waiting for transfers between devices, on_device(): lax.psum_scatter(grad_value_term, ('seq', 'fsdp'), scatter_dimension=0, t...  136 us
    all_gather x1, waiting for transfers between devices, on_device(): lax.all_gather(w_down, ('seq', 'fsdp'), axis=0, tiled=True)  133 us
    all_gather x1, waiting for transfers between devices, on_device(): lax.all_gather(w_up, ('seq', 'fsdp'), axis=0, tiled=True)  133 us
    reduce_scatter x1, waiting for transfers between devices, on_device(): lax.psum_scatter(grad_key_term, ('seq', 'fsdp'), scatter_dimension=0, til...  124 us
    all_gather x1, waiting for transfers between devices, on_device(): lax.all_gather(w_gate, ('seq', 'fsdp'), axis=0, tiled=True)  114 us
  transfers between devices with their start and end apart: 18, of which 15 were waited for; matrix products, arithmetic and copies ran while one was open for 7% of the time, Pallas kernels for 0%

commit v1 on v0

v1 whole, which is shorter than its diff:
```python
import functools
import math

import jax
import jax.numpy as jnp
from jax import lax
from jax.experimental import pallas as pl
from jax.experimental.pallas import tpu as pltpu
from jax.sharding import PartitionSpec as P

H = 32
KV = 4
HD = 64
AXES = ("seq", "fsdp")
norm_eps = 1e-05
rope_base = 10000.0
masked_value = -1e30
score_scale = HD ** (-0.5)
to_log2 = score_scale * math.log2(math.e)
bf16 = jnp.bfloat16
f32 = jnp.float32
KEY_TILE = 512
Q_ROWS = 512


def dot(a, b):
    return lax.dot_general(a, b, (((1,), (0,)), ((), ())), preferred_element_type=f32)


def dot_last(a, b):
    return lax.dot_general(a, b, (((1,), (1,)), ((), ())), preferred_element_type=f32)


def dot_first(a, b):
    return lax.dot_general(a, b, (((0,), (0,)), ((), ())), preferred_element_type=f32)


def inverse_rms(values):
    return lax.rsqrt(jnp.mean(values * values, axis=-1, keepdims=True) + norm_eps)


def rope_tables(positions):
    half = HD // 2
    frequency = rope_base ** (-(jnp.arange(half, dtype=f32) * 2.0) / HD)
    angles = positions.astype(f32)[..., None] * frequency
    return (jnp.cos(angles), jnp.sin(angles))


def rotate(values, cosine, sine):
    a, b = jnp.split(values, 2, axis=-1)
    return jnp.concatenate([a * cosine - b * sine, b * cosine + a * sine], axis=-1)


def unrotate(values, cosine, sine):
    a, b = jnp.split(values, 2, axis=-1)
    return jnp.concatenate([a * cosine + b * sine, b * cosine - a * sine], axis=-1)


def block_position(me, i, x_mask, z_mask):
    return me ^ (((i // 2) % 2) * x_mask + (i // 4) * z_mask)


def forward_kernel(x_mask, z_mask, rows, me_ref, q_ref, kv_ref, o_ref, ones_ref):
    me = me_ref[0]
    per_tile = KEY_TILE // rows
    lanes = lax.broadcasted_iota(jnp.int32, (KEY_TILE, 2 * HD), 1)

    def fill(j, carry):
        where = pl.ds(pl.multiple_of(j * KEY_TILE, KEY_TILE), KEY_TILE)
        ones_ref[where, :] = jnp.where(lanes < HD, jnp.ones((), bf16), kv_ref[where, :])
        return carry

    lax.fori_loop(0, kv_ref.shape[0] // KEY_TILE, fill, 0)

    def block(i, carry):
        position = block_position(me, i, x_mask, z_mask)
        last = position // per_tile
        q = q_ref[i]

        def scores(kt):
            physical = kt ^ (me // per_tile)
            where = pl.ds(pl.multiple_of(physical * KEY_TILE, KEY_TILE), KEY_TILE)
            return dot_last(q, kv_ref[where, :]), ones_ref[where, :]

        s, ones_v = scores(last)
        row = lax.broadcasted_iota(jnp.int32, s.shape, 0) % rows + (position % per_tile) * rows
        col = lax.broadcasted_iota(jnp.int32, s.shape, 1)
        key = ((col // rows) ^ (me % per_tile)) * rows + col % rows
        s = jnp.where(key <= row, s, masked_value)
        top = jnp.max(s, axis=-1, keepdims=True)
        p = jnp.exp2((s - top) * to_log2).astype(bf16)
        total = dot(p, ones_v)

        def turn(kt, state):
            top, total = state
            s, ones_v = scores(kt)
            new_top = jnp.maximum(top, jnp.max(s, axis=-1, keepdims=True))
            p = jnp.exp2((s - new_top) * to_log2).astype(bf16)
            total = total * jnp.exp2((top - new_top) * to_log2) + dot(p, ones_v)
            return new_top, total

        top, total = lax.fori_loop(0, last, turn, (top, total))
        weight = total[:, :1]
        lane = lax.broadcasted_iota(jnp.int32, total.shape, 1)
        o_ref[i] = jnp.where(lane < HD, top * to_log2 + jnp.log2(weight), total / weight)
        return carry

    lax.fori_loop(0, q_ref.shape[0], block, 0)


def backward_kernel(
    x_mask, z_mask, rows, me_ref, q_ref, g_ref, kv_ref, log_ref, delta_ref, dq_ref, dkv_ref
):
    me = me_ref[0]
    per_tile = KEY_TILE // rows

    def clear(j, carry):
        where = pl.ds(pl.multiple_of(j * KEY_TILE, KEY_TILE), KEY_TILE)
        dkv_ref[where, :] = jnp.zeros((KEY_TILE, 2 * HD), f32)
        return carry

    lax.fori_loop(0, kv_ref.shape[0] // KEY_TILE, clear, 0)

    def block(i, carry):
        position = block_position(me, i, x_mask, z_mask)
        last = position // per_tile
        q = q_ref[i]
        g = g_ref[i]
        log_total = log_ref[i]
        delta = delta_ref[i]

        def tile(kt, keep):
            physical = kt ^ (me // per_tile)
            where = pl.ds(pl.multiple_of(physical * KEY_TILE, KEY_TILE), KEY_TILE)
            kv = kv_ref[where, :]
            p = jnp.exp2(dot_last(kv, q) * to_log2 - log_total)
            if keep is not None:
                p = jnp.where(keep, p, 0.0)
            ds = (p * (dot_last(kv, g) - delta)).astype(bf16)
            dkv_ref[where, :] += dot(p.astype(bf16), g) + dot(ds, q)
            return dot_first(ds, kv)

        shape = (KEY_TILE, q.shape[0])
        col = lax.broadcasted_iota(jnp.int32, shape, 0)
        row = lax.broadcasted_iota(jnp.int32, shape, 1) % rows + (position % per_tile) * rows
        key = ((col // rows) ^ (me % per_tile)) * rows + col % rows
        dq = tile(last, key <= row)
        dq = lax.fori_loop(0, last, lambda kt, dq: dq + tile(kt, None), dq)
        dq_ref[i] = dq
        return carry

    lax.fori_loop(0, q_ref.shape[0], block, 0)


SMEM_SPEC = pl.BlockSpec(memory_space=pltpu.SMEM)
VMEM_SPEC = pl.BlockSpec(memory_space=pltpu.VMEM)


def attention_forward(me, q, kv, x_mask, z_mask, rows):
    tiles = q.shape[0] * kv.shape[0] // KEY_TILE // 2
    cost = pl.CostEstimate(
        flops=tiles * 4 * Q_ROWS * KEY_TILE * 2 * HD * 2,
        bytes_accessed=2 * (q.size * 3 + kv.size),
        transcendentals=tiles * Q_ROWS * KEY_TILE,
    )
    return pl.pallas_call(
        functools.partial(forward_kernel, x_mask, z_mask, rows),
        out_shape=jax.ShapeDtypeStruct(q.shape, f32),
        in_specs=[SMEM_SPEC, VMEM_SPEC, VMEM_SPEC],
        out_specs=VMEM_SPEC,
        scratch_shapes=[pltpu.VMEM(kv.shape, bf16)],
        compiler_params=pltpu.CompilerParams(vmem_limit_bytes=40 << 20),
        cost_estimate=cost,
        name="attention_forward",
    )(me, q, kv)


def attention_backward(me, q, g, kv, log_total, delta, x_mask, z_mask, rows):
    tiles = q.shape[0] * kv.shape[0] // KEY_TILE // 2
    cost = pl.CostEstimate(
        flops=tiles * 10 * Q_ROWS * KEY_TILE * 2 * HD * 2,
        bytes_accessed=2 * (q.size * 4 + kv.size * 3),
        transcendentals=tiles * Q_ROWS * KEY_TILE,
    )
    return pl.pallas_call(
        functools.partial(backward_kernel, x_mask, z_mask, rows),
        out_shape=(
            jax.ShapeDtypeStruct(q.shape, f32),
            jax.ShapeDtypeStruct(kv.shape, f32),
        ),
        in_specs=[SMEM_SPEC] + [VMEM_SPEC] * 5,
        out_specs=(VMEM_SPEC, VMEM_SPEC),
        compiler_params=pltpu.CompilerParams(vmem_limit_bytes=48 << 20),
        cost_estimate=cost,
        name="attention_backward",
    )(me, q, g, kv, log_total, delta)


def on_device(
    tokens, gain_attn, w_query, w_key, w_value, w_out, gain_ffn, w_gate, w_up, w_down, out_grad
):
    n_seq = lax.axis_size("seq")
    n_fsdp = lax.axis_size("fsdp")
    n = n_seq * n_fsdp
    me = lax.axis_index(AXES)
    rows = tokens.shape[0]
    width = tokens.shape[1]
    slab = w_gate.shape[0]
    hidden_width = w_gate.shape[1]
    group_heads = H // KV
    x_mask, z_mask, core = 1, 2 * n_fsdp, n_fsdp
    t_masks = [0, x_mask, z_mask, x_mask | z_mask]
    far = [n_fsdp << k for k in range(2, n_seq.bit_length() - 1)]
    near = [1 << k for k in range(1, n_fsdp.bit_length() - 1)]
    d_bits = far + near + [core]
    d_masks = [0]
    for bit in d_bits:
        d_masks = d_masks + [m | bit for m in d_masks]
    d_all = sum(d_bits)
    x_bit = me % 2
    z_bit = (me // z_mask) % 2
    t = 2 * z_bit + x_bit
    tok = 4 * rows

    def swap(value, mask):
        return lax.ppermute(value, AXES, [(i, i ^ mask) for i in range(n)])

    def order_t(p):
        q = [
            jnp.where(x_bit == 1, p[1], p[0]),
            jnp.where(x_bit == 1, p[0], p[1]),
            jnp.where(x_bit == 1, p[3], p[2]),
            jnp.where(x_bit == 1, p[2], p[3]),
        ]
        return [
            jnp.where(z_bit == 1, q[2], q[0]),
            jnp.where(z_bit == 1, q[3], q[1]),
            jnp.where(z_bit == 1, q[0], q[2]),
            jnp.where(z_bit == 1, q[1], q[3]),
        ]

    def exchange_t(piece):
        return order_t([piece(t)] + [swap(piece(t ^ r), t_masks[r]) for r in (1, 2, 3)])

    def gather_t(value):
        return jnp.concatenate([value] + [swap(value, m) for m in t_masks[1:]], axis=0)

    def scatter_t(partial):
        mine = partial[:rows]
        for r in (1, 2, 3):
            sent = swap(partial[r * rows : (r + 1) * rows].astype(bf16), t_masks[r])
            mine = mine + sent.astype(f32)
        return mine

    def gather_d(value):
        pieces = [value]
        for bit in far + near:
            pieces = pieces + [swap(p, bit) for p in pieces]
        half = jnp.concatenate(pieces, axis=0)
        return jnp.concatenate([half, swap(half, core)], axis=0)

    def scatter_d(own, other):
        total = own + swap(other.astype(bf16), core).astype(f32)
        for bit in reversed(far + near):
            half = total.shape[0] // 2
            total = total[:half] + swap(total[half:].astype(bf16), bit).astype(f32)
        return total

    unit = 2 * slab

    def place(mask):
        return sum(((mask // bit) % 2) << k for k, bit in enumerate(d_bits))

    def to_relative(value):
        parts = []
        for m in d_masks:
            for z in (0, z_mask):
                start = (((me & d_all) ^ m) + z) // 2 * unit
                parts.append(lax.dynamic_slice_in_dim(value, start, unit, value.ndim - 1))
        return jnp.concatenate(parts, axis=-1)

    def to_natural(value):
        parts = []
        for b in range(0, n, 2):
            start = ((place(b) ^ place(me)) * 2 + (1 if b & z_mask else 0)) * unit
            parts.append(lax.dynamic_slice_in_dim(value, start, unit, value.ndim - 1))
        return jnp.concatenate(parts, axis=-1)

    gains = jnp.stack([gain_attn, gain_ffn])
    natural_gains = gains
    for bit in [x_mask, z_mask] + d_bits:
        gains = jnp.stack([gains, swap(gains, bit)])
    lead = len(d_bits)
    gains = jnp.where(z_bit == 1, jnp.flip(gains, lead), gains)
    gains = jnp.where(x_bit == 1, jnp.flip(gains, lead + 1), gains)
    gains = jnp.moveaxis(gains, -2, 0).reshape(2, width).astype(f32)
    gain_a, gain_f = gains[0:1], gains[1:2]

    q_cols = group_heads * HD
    group_tokens = gather_t(to_relative(tokens))

    def qkv_piece(j):
        return jnp.concatenate(
            [
                lax.dynamic_slice_in_dim(w_query, j * q_cols, q_cols, 1),
                lax.dynamic_slice_in_dim(w_key, j * HD, HD, 1),
                lax.dynamic_slice_in_dim(w_value, j * HD, HD, 1),
            ],
            axis=1,
        )

    qkv_w = gather_d(jnp.concatenate(exchange_t(qkv_piece), axis=0))

    cols = hidden_width // 4

    def ffn_weight(w):
        return gather_d(
            jnp.concatenate(
                exchange_t(lambda j: lax.dynamic_slice_in_dim(w, j * cols, cols, 1)), axis=0
            )
        )

    gate_w, up_w, down_w = ffn_weight(w_gate), ffn_weight(w_up), ffn_weight(w_down)

    bits = n.bit_length() - 1
    z_place, x_place = z_mask.bit_length() - 1, 0
    source = {z_place: bits - 1, x_place: bits - 2}
    free = [b for b in range(bits - 2)]
    open_places = [b for b in range(bits) if b not in source]
    for b in list(open_places):
        if b in free:
            source[b] = b
            free.remove(b)
            open_places.remove(b)
    for b, s in zip(open_places, free):
        source[b] = s

    def goes_to(i):
        return sum(((i >> s) & 1) << b for b, s in source.items())

    def came_from(i):
        return sum(((i >> b) & 1) << s for b, s in source.items())

    per_group = n // 4
    out_pieces = [lax.ppermute(w_out, AXES, [(i, goes_to(i)) for i in range(n)])]
    for bit in far + near:
        out_pieces = out_pieces + [swap(p, bit) for p in out_pieces]
    out_half = jnp.concatenate(out_pieces, axis=0)
    out_both = jnp.concatenate([out_half, swap(out_half, core)], axis=0)
    my_row = came_from(me) % per_group
    out_places = [(my_row ^ (came_from(m) % per_group)) * slab for m in d_masks]
    out_w = jnp.zeros((per_group * slab, width), bf16)
    for k in range(per_group):
        out_w = lax.dynamic_update_slice_in_dim(
            out_w, out_both[k * slab : (k + 1) * slab], out_places[k], 0
        )

    wide = group_tokens.astype(f32)
    h_attn = (wide * inverse_rms(wide) * gain_a).astype(bf16)
    qkv = dot(h_attn, qkv_w).astype(bf16).astype(f32)
    blocks = jnp.stack([me ^ m for m in t_masks])
    positions = blocks[:, None] * rows + jnp.arange(rows, dtype=jnp.int32)
    cosine, sine = rope_tables(positions)
    cos_h, sin_h = cosine[:, None], sine[:, None]
    q = qkv[:, :q_cols].reshape(4, rows, group_heads, HD).transpose(0, 2, 1, 3)
    q = rotate(q, cos_h, sin_h).astype(bf16)
    q = jnp.concatenate([q, jnp.zeros_like(q)], axis=-1)
    per_block = Q_ROWS // rows
    n_blocks = 4 * group_heads // per_block
    q = q.reshape(n_blocks, Q_ROWS, 2 * HD)
    k = rotate(qkv[:, q_cols : q_cols + HD].reshape(4, rows, HD), cosine, sine).astype(bf16)
    v = qkv[:, q_cols + HD :].reshape(4, rows, HD).astype(bf16)
    kv = jnp.concatenate([k, v], axis=-1)
    chips = [m for m in d_masks if not m & core]
    kv = jnp.stack([kv] + [swap(kv, m) for m in chips[1:]])
    kv = jnp.concatenate([kv, swap(kv, core)], axis=0)
    order = list(reversed(d_bits)) + [z_mask, x_mask]
    axes = sorted(range(len(order)), key=lambda a: -order[a])
    kv = kv.reshape((2,) * len(order) + (rows, 2 * HD))
    kv = kv.transpose(axes + [len(order), len(order) + 1]).reshape(n * rows, 2 * HD)

    me_ref = me.reshape(1).astype(jnp.int32)
    attn = attention_forward(me_ref, q, kv, x_mask, z_mask, rows)
    log_total = attn[:, :, 0].reshape(n_blocks, 1, Q_ROWS)
    attn_wide = attn[:, :, HD:].reshape(4, group_heads, rows, HD).transpose(0, 2, 1, 3)
    attn_wide = attn_wide.reshape(tok, q_cols)
    attn_out = attn_wide.astype(bf16)
    middle = tokens.astype(f32) + scatter_t(dot(attn_out, out_w))

    inverse_ffn = inverse_rms(middle)
    normed_ffn = middle * inverse_ffn
    h_ffn = gather_t((to_relative(normed_ffn) * gain_f).astype(bf16))
    g = gather_t(to_relative(out_grad))
    gate = dot(h_ffn, gate_w)
    up = dot(h_ffn, up_w)
    sig = jax.nn.sigmoid(gate)
    act = gate * sig
    hidden = (act * up).astype(bf16)
    d_hidden = dot(g, down_w)
    d_gate = (d_hidden * up * sig * (1.0 + gate * (1.0 - sig))).astype(bf16)
    d_up = (d_hidden * act).astype(bf16)
    d_hffn = to_natural(scatter_t(dot_last(d_gate, gate_w) + dot_last(d_up, up_w)))
    block_out = (middle + to_natural(scatter_t(dot_last(hidden, down_w)))).astype(bf16)

    def weight_grad(left, right):
        half = left.shape[1] // 2
        other = dot_first(left[:, half:], right)
        own = dot_first(left[:, :half], right)
        return scatter_d(own, other)

    def give_back(shard):
        def piece(j):
            return lax.dynamic_slice_in_dim(shard, j * slab, slab, 0)

        got = [piece(t)] + [
            swap(piece(t ^ r).astype(bf16), t_masks[r]).astype(f32) for r in (1, 2, 3)
        ]
        return order_t(got)

    grad_gate = jnp.concatenate(give_back(weight_grad(h_ffn, d_gate)), axis=1)
    grad_up = jnp.concatenate(give_back(weight_grad(h_ffn, d_up)), axis=1)
    grad_down = jnp.concatenate(give_back(weight_grad(g, hidden)), axis=1)

    def natural_gain(own):
        return own

    gain_f_nat = to_natural(gain_f)
    gain_a_nat = to_natural(gain_a)
    scaled = d_hffn * gain_f_nat
    gain_ffn_term = jnp.sum(d_hffn * normed_ffn, axis=0)
    d_middle = out_grad.astype(f32) + inverse_ffn * (
        scaled - normed_ffn * jnp.mean(scaled * normed_ffn, axis=-1, keepdims=True)
    )
    d_branch = gather_t(d_middle.astype(bf16))
    d_attn = dot_last(d_branch, out_w).astype(bf16)

    out_term = dot_first(attn_out, d_branch)
    out_parts = [lax.dynamic_slice_in_dim(out_term, s, slab, 0) for s in out_places]
    half = per_group // 2
    out_shard = scatter_d(
        jnp.concatenate(out_parts[:half], axis=0), jnp.concatenate(out_parts[half:], axis=0)
    )
    grad_out_proj = lax.ppermute(
        out_shard.astype(bf16), AXES, [(goes_to(i), i) for i in range(n)]
    ).astype(f32)

    d_wide = d_attn.astype(f32)
    delta = jnp.sum((d_wide * attn_wide).reshape(4, rows, group_heads, HD), axis=-1)
    delta = delta.transpose(0, 2, 1).reshape(n_blocks, 1, Q_ROWS)
    d_heads = d_attn.reshape(4, rows, group_heads, HD).transpose(0, 2, 1, 3)
    d_heads = jnp.concatenate([jnp.zeros_like(d_heads), d_heads], axis=-1)
    d_heads = d_heads.reshape(n_blocks, Q_ROWS, 2 * HD)
    dq, dkv = attention_backward(
        me_ref, q, d_heads, kv, log_total, delta, x_mask, z_mask, rows
    )
    dq = dq[:, :, :HD].reshape(4, group_heads, rows, HD) * score_scale
    d_query = unrotate(dq, cos_h, sin_h).astype(bf16).transpose(0, 2, 1, 3).reshape(tok, q_cols)

    back = [axes.index(a) for a in range(len(order))]
    dkv = dkv.reshape((2,) * len(order) + (rows, 2 * HD))
    dkv = dkv.transpose(back + [len(order), len(order) + 1]).reshape(-1, tok, 2 * HD)
    half = dkv.shape[0] // 2
    dkv = dkv[:half] + swap(dkv[half:].astype(bf16), core).astype(f32)
    kv_sum = dkv[0]
    for k_mask, m in enumerate(chips[1:], 1):
        kv_sum = kv_sum + swap(dkv[k_mask].astype(bf16), m).astype(f32)
    dk = unrotate(kv_sum[:, :HD].reshape(4, rows, HD) * score_scale, cosine, sine)
    d_kv = jnp.concatenate([dk.reshape(tok, HD), kv_sum[:, HD:]], axis=1).astype(bf16)
    d_qkv = jnp.concatenate([d_query, d_kv], axis=1)

    d_hattn = to_natural(scatter_t(dot_last(d_qkv, qkv_w)))
    qkv_grads = give_back(weight_grad(h_attn, d_qkv))
    grad_query = jnp.concatenate([p[:, :q_cols] for p in qkv_grads], axis=1)
    grad_key = jnp.concatenate([p[:, q_cols : q_cols + HD] for p in qkv_grads], axis=1)
    grad_value = jnp.concatenate([p[:, q_cols + HD :] for p in qkv_grads], axis=1)

    own = tokens.astype(f32)
    inverse_attn = inverse_rms(own)
    normed_attn = own * inverse_attn
    scaled = d_hattn * gain_a_nat
    gain_attn_term = jnp.sum(d_hattn * normed_attn, axis=0)
    grad_tokens = d_middle + inverse_attn * (
        scaled - normed_attn * jnp.mean(scaled * normed_attn, axis=-1, keepdims=True)
    )
    gain_terms = jnp.stack([gain_attn_term, gain_ffn_term])
    for bit in t_masks[1:3] + d_bits:
        gain_terms = gain_terms + swap(gain_terms, bit)
    gain_terms = lax.dynamic_slice_in_dim(gain_terms, me * slab, slab, 1)
    return (
        block_out,
        grad_tokens,
        gain_terms[0],
        grad_query,
        grad_key,
        grad_value,
        grad_out_proj,
        gain_terms[1],
        grad_gate,
        grad_up,
        grad_down,
    )


def solution(mesh):
    spec2 = P(AXES, None)
    spec1 = P(AXES)
    return jax.shard_map(
        on_device,
        mesh=mesh,
        in_specs=(
            spec2,
            spec1,
            spec2,
            spec2,
            spec2,
            spec2,
            spec1,
            spec2,
            spec2,
            spec2,
            spec2,
        ),
        out_specs=(
            spec2,
            spec2,
            spec1,
            spec2,
            spec2,
            spec2,
            spec2,
            spec1,
            spec2,
            spec2,
            spec2,
        ),
        check_vma=False,
    )
```

time: 4100 us -> 829 us (0.20)
  waiting for transfers between devices: 3410 us -> 372 us
  matrix products: 320 us -> 73.8 us
  starting transfers between devices: 22.3 us -> 197 us
  blocking collectives: 121 us -> 0 us
  other arithmetic: 127 us -> 46.5 us
    unnamed x15 -> x0, waiting for transfers between devices: 1820 us -> none
    reduce_scatter x5 -> x0, waiting for transfers between devices: 990 us -> none  [the longest x1 369 us: on_device(): lax.psum_scatter(grad_out_term, ('seq', 'fsdp'), scatter_dimension=0, til...]
    all_gather x8 -> x0, waiting for transfers between devices: 549 us -> none  [the longest x1 133 us: on_device(): lax.all_gather(w_down, ('seq', 'fsdp'), axis=0, tiled=True)]
    ppermute x0 -> x103, waiting for transfers between devices: none -> 372 us  [the longest x101 359 us: swap(): return lax.ppermute(value, AXES, [(i, i ^ mask) for i in range(n)])]
    dot_general x48 -> x19, matrix products: 320 us -> 73.8 us  [the longest x9 26.7 us: dot_first(): lax.dot_general(a, b, (((0,), (0,)), ((), ())), preferred_element_type=f32)]
    ppermute x0 -> x103, starting transfers between devices: none -> 197 us  [the longest x101 187 us: swap(): return lax.ppermute(value, AXES, [(i, i ^ mask) for i in range(n)])]
    unnamed x2 -> x0, blocking collectives: 79.9 us -> none
    concatenate x7 -> x19, other arithmetic: 91.5 us -> 13.8 us  [the longest x2 4.62 us: gather_t(): jnp.concatenate([value] + [swap(value, m) for m in t_masks[1:]], axis=0)]
  transfers between devices with their start and end apart: 18 -> 103, of which waited for: 15 -> 45; matrix products, arithmetic and copies ran while one was open for 7% -> 20% of each run, Pallas kernels for 0% -> 4%
where the time goes in v1:
time: 829 us; the launch traced here: 818 us
  waiting for transfers between devices  372 us (45%)
  starting transfers between devices  197 us (24%)
  local copies, waits for them, and re-layouts  96.2 us (12%)
  matrix products  73.8 us (9%)
  other arithmetic  46.5 us (6%)
  Pallas kernels  29.3 us (4%)
    ppermute x101, waiting for transfers between devices, swap(): return lax.ppermute(value, AXES, [(i, i ^ mask) for i in range(n)])  359 us
    ppermute x101, starting transfers between devices, swap(): return lax.ppermute(value, AXES, [(i, i ^ mask) for i in range(n)])  187 us
    unnamed x298, local copies, waits for them, and re-layouts  50.9 us
    dot_general x9, matrix products, dot_first(): lax.dot_general(a, b, (((0,), (0,)), ((), ())), preferred_element_type=f32)  26.7 us
    dot_general x5, matrix products, dot(): lax.dot_general(a, b, (((1,), (0,)), ((), ())), preferred_element_type=f32)  25.7 us
    dot_general x5, matrix products, dot_last(): lax.dot_general(a, b, (((1,), (1,)), ((), ())), preferred_element_type=f32)  21.4 us
  transfers between devices with their start and end apart: 103, of which 45 were waited for; matrix products, arithmetic and copies ran while one was open for 20% of the time, Pallas kernels for 4%

profile of v1, /device:TPU:8, one launch (start us, length us, event | category | flops | bytes accessed | tf_op | source)
XLA Modules:
  0.0 817.9 jit_solution(1176827062889426508)
XLA Ops:
  96.6 12.8 %collective-permute-done.19 = bf16[64,2048]{1,0:T(8,128)(2,1)S(1)} collective-permute-done((bf16[64,2048]{1,0:T(8,128)(2,1)S(1)}, bf16[64,2048]{1,0:T(8,128)(2,1)S(1)}, u32[]{:S(2)}, u32[]{:S(2)}) %collective-permute-start.19) | collective-permute-done | bytes 262176 | tf_op jit(solution)/shard_map/ppermute | solution.py:345
  111.4 7.6 collective-permute-done.12
  128.7 33.3 %collective-permute-done.20 = bf16[64,2048]{1,0:T(8,128)(2,1)S(1)} collective-permute-done((bf16[64,2048]{1,0:T(8,128)(2,1)S(1)}, bf16[64,2048]{1,0:T(8,128)(2,1)S(1)}, u32[]{:S(2)}, u32[]{:S(2)}) %collective-permute-start.20) | collective-permute-done | bytes 262176 | tf_op jit(solution)/shard_map/ppermute | solution.py:226
  164.2 8.5 %collective-permute-done.13 = bf16[256,640]{1,0:T(8,128)(2,1)S(1)} collective-permute-done((bf16[256,640]{1,0:T(8,128)(2,1)S(1)}, bf16[256,640]{1,0:T(8,128)(2,1)S(1)}, u32[]{:S(2)}, u32[]{:S(2)}) %collective-permute-start.13) | collective-permute-done | bytes 327712 | tf_op jit(solution)/shard_map/ppermute | solution.py:226
  180.6 10.4 %collective-permute-done.41 = bf16[256,1408]{1,0:T(8,128)(2,1)S(1)} collective-permute-done((bf16[256,1408]{1,0:T(8,128)(2,1)S(1)}, bf16[256,1408]{1,0:T(8,128)(2,1)S(1)}, u32[]{:S(2)}, u32[]{:S(2)}) %collective-permute-start.41) | collective-permute-done | bytes 720928 | tf_op jit(solution)/shard_map/ppermute | solution.py:226
  192.0 26.0 %collective-permute-done.47 = bf16[256,1408]{1,0:T(8,128)(2,1)} collective-permute-done((bf16[256,1408]{1,0:T(8,128)(2,1)S(1)}, bf16[256,1408]{1,0:T(8,128)(2,1)}, u32[]{:S(2)}, u32[]{:S(2)}) %collective-permute-start.47) | collective-permute-done | bytes 720928 | tf_op jit(solution)/shard_map/ppermute | solution.py:226
  220.1 12.5 %collective-permute-done.33 = bf16[256,1408]{1,0:T(8,128)(2,1)S(1)} collective-permute-done((bf16[256,1408]{1,0:T(8,128)(2,1)S(1)}, bf16[256,1408]{1,0:T(8,128)(2,1)S(1)}, u32[]{:S(2)}, u32[]{:S(2)}) %collective-permute-start.33) | collective-permute-done | bytes 720928 | tf_op jit(solution)/shard_map/ppermute | solution.py:226
  252.6 5.1 collective-permute-done.16
  261.8 13.6 %attention_forward.1 = f32[8,512,128]{2,1,0:T(8,128)S(1)} custom-call(s32[1]{0:T(128)} %bitcast.me_ref, bf16[8,512,128]{2,1,0:T(8,128)(2,1)S(1)} %bitcast.135, bf16[4096,128]{1,0:T(8,128)(2,1)S(1)} %bitcast.138), custom_call_target="tpu_custom_call" | custom-call | flops 8589934592 | bytes 4194304 | tf_op jit(solution)/shard_map/attention_forward/pallas_call | solution.py:166
  294.2 14.0 %collective-permute-done.24 = bf16[128,2048]{1,0:T(8,128)(2,1)S(1)} collective-permute-done((bf16[128,2048]{1,0:T(8,128)(2,1)S(1)}, bf16[128,2048]{1,0:T(8,128)(2,1)S(1)}, u32[]{:S(2)}, u32[]{:S(2)}) %collective-permute-start.24) | collective-permute-done | bytes 524320 | tf_op jit(solution)/shard_map/ppermute | solution.py:226
  310.1 5.8 collective-permute-start.50
  319.4 7.0 collective-permute-done.34
  329.4 13.0 %collective-permute-done.54 = bf16[128,2048]{1,0:T(8,128)(2,1)S(1)} collective-permute-done((bf16[128,2048]{1,0:T(8,128)(2,1)}, bf16[128,2048]{1,0:T(8,128)(2,1)S(1)}, u32[]{:S(2)}, u32[]{:S(2)}) %collective-permute-start.54) | collective-permute-done | bytes 524320 | tf_op jit(solution)/shard_map/ppermute | solution.py:226
  366.6 6.5 fusion.78
  373.1 5.5 fusion.79
  380.9 8.7 %multiply_convert_fusion.1 = (bf16[512,1408]{1,0:T(8,128)(2,1)S(1)}, bf16[512,1408]{1,0:T(8,128)(2,1)S(1)}, bf16[512,1408]{1,0:T(8,128)(2,1)}) fusion(f32[512,1408]{1,0:T(8,128)S(1)} %fusion.78, f32[512,1408]{1,0:T(8,128)S(1)} %fusion.79, bf16[2048,1408]{1,0:T(8,128)(2,1)S(1)} %constant_dynamic-update-slice_fusion.59, ...), kind=kOutput, calls=%fused_computation.19 | convolution fusion | flops 2971992064 | bytes 17956864 | tf_op jit(solution)/shard_map/dot_general | solution.py:27
  394.6 7.2 fusion.95
  425.5 7.7 collective-permute-done.57
  440.0 13.4 %collective-permute-done.51 = bf16[128,2048]{1,0:T(8,128)(2,1)S(1)} collective-permute-done((bf16[128,2048]{1,0:T(8,128)(2,1)S(1)}, bf16[128,2048]{1,0:T(8,128)(2,1)S(1)}, u32[]{:S(2)}, u32[]{:S(2)}) %collective-permute-start.51) | collective-permute-done | bytes 524320 | tf_op jit(solution)/shard_map/ppermute | solution.py:226
  460.6 9.6 %collective-permute-done.62 = bf16[128,2048]{1,0:T(8,128)(2,1)S(1)} collective-permute-done((bf16[128,2048]{1,0:T(8,128)(2,1)S(1)}, bf16[128,2048]{1,0:T(8,128)(2,1)S(1)}, u32[]{:S(2)}, u32[]{:S(2)}) %collective-permute-start.62) | collective-permute-done | bytes 524320 | tf_op jit(solution)/shard_map/ppermute | solution.py:226
  470.3 9.4 %collective-permute-done.61 = bf16[128,2048]{1,0:T(8,128)(2,1)S(1)} collective-permute-done((bf16[128,2048]{1,0:T(8,128)(2,1)S(1)}, bf16[128,2048]{1,0:T(8,128)(2,1)S(1)}, u32[]{:S(2)}, u32[]{:S(2)}) %collective-permute-start.61) | collective-permute-done | bytes 524320 | tf_op jit(solution)/shard_map/ppermute | solution.py:226
  489.0 15.6 %attention_backward.1 = (f32[8,512,128]{2,1,0:T(8,128)S(1)}, f32[4096,128]{1,0:T(8,128)}) custom-call(s32[1]{0:T(128)} %bitcast.me_ref, bf16[8,512,128]{2,1,0:T(8,128)(2,1)S(1)} %bitcast.136, bf16[8,512,128]{2,1,0:T(8,128)(2,1)S(1)} %bitcast.137, bf16[4096,128]{1,0:T(8,128)(2,1)S(1)} %bitcast.139, f32[8,1,512]{2,1,0:T(1,128)S(1)} %bitcast.140, ...), custom_call_target="tpu_custom_call" | custom-call | flops 21474836480 | bytes 7340032 | tf_op jit(solution)/shard_map/attention_backward/pallas_call | solution.py:185
  508.9 7.0 collective-permute-start.63
  530.7 50.3 %collective-permute-start.64 = (bf16[512,128]{0,1:T(8,128)(2,1)S(1)}, bf16[512,128]{0,1:T(8,128)(2,1)S(1)}, u32[]{:S(2)}, u32[]{:S(2)}) collective-permute-start(bf16[512,128]{0,1:T(8,128)(2,1)S(1)} %get-tuple-element.144), channel_id=1, source_target_pairs={{0,16},{1,17},{2,18},{3,19},{4,20},{5,21},{6,22},{7,23},{8,24},{9,... | collective-permute-start | bytes 393224 | tf_op jit(solution)/shard_map/ppermute | solution.py:226
  583.2 5.2 collective-permute-done.64
  597.7 21.2 %collective-permute-done.67 = bf16[128,2048]{1,0:T(8,128)(2,1)S(1)} collective-permute-done((bf16[128,2048]{1,0:T(8,128)(2,1)S(1)}, bf16[128,2048]{1,0:T(8,128)(2,1)S(1)}, u32[]{:S(2)}, u32[]{:S(2)}) %collective-permute-start.67) | collective-permute-done | bytes 524320 | tf_op jit(solution)/shard_map/ppermute | solution.py:226
  636.0 9.0 %collective-permute-done.73 = f32[2,2048]{1,0:T(2,128)S(1)} collective-permute-done((f32[2,2048]{1,0:T(2,128)S(1)}, f32[2,2048]{1,0:T(2,128)S(1)}, u32[]{:S(2)}, u32[]{:S(2)}) %collective-permute-start.73) | collective-permute-done | bytes 16416 | tf_op jit(solution)/shard_map/ppermute | solution.py:226
  651.4 8.7 %collective-permute-done.83 = bf16[64,2048]{1,0:T(8,128)(2,1)S(1)} collective-permute-done((bf16[64,2048]{1,0:T(8,128)(2,1)S(1)}, bf16[64,2048]{1,0:T(8,128)(2,1)S(1)}, u32[]{:S(2)}, u32[]{:S(2)}) %collective-permute-start.83) | collective-permute-done | bytes 262176 | tf_op jit(solution)/shard_map/ppermute | solution.py:226
  676.5 9.9 %collective-permute-done.77 = bf16[256,640]{1,0:T(8,128)(2,1)S(1)} collective-permute-done((bf16[256,640]{1,0:T(8,128)(2,1)S(1)}, bf16[256,640]{1,0:T(8,128)(2,1)S(1)}, u32[]{:S(2)}, u32[]{:S(2)}) %collective-permute-start.77) | collective-permute-done | bytes 327712 | tf_op jit(solution)/shard_map/ppermute | solution.py:226
  705.8 28.4 %collective-permute-done.92 = bf16[512,1408]{1,0:T(8,128)(2,1)S(1)} collective-permute-done((bf16[512,1408]{1,0:T(8,128)(2,1)S(1)}, bf16[512,1408]{1,0:T(8,128)(2,1)S(1)}, u32[]{:S(2)}, u32[]{:S(2)}) %collective-permute-start.92) | collective-permute-done | bytes 1441824 | tf_op jit(solution)/shard_map/ppermute | solution.py:226
  736.6 27.2 %collective-permute-done.86 = bf16[512,1408]{1,0:T(8,128)(2,1)S(1)} collective-permute-done((bf16[512,1408]{1,0:T(8,128)(2,1)S(1)}, bf16[512,1408]{1,0:T(8,128)(2,1)S(1)}, u32[]{:S(2)}, u32[]{:S(2)}) %collective-permute-start.86) | collective-permute-done | bytes 1441824 | tf_op jit(solution)/shard_map/ppermute | solution.py:226
  772.2 24.0 %collective-permute-done.87 = bf16[256,1408]{1,0:T(8,128)(2,1)S(1)} collective-permute-done((bf16[256,1408]{1,0:T(8,128)(2,1)S(1)}, bf16[256,1408]{1,0:T(8,128)(2,1)S(1)}, u32[]{:S(2)}, u32[]{:S(2)}) %collective-permute-start.87) | collective-permute-done | bytes 720928 | tf_op jit(solution)/shard_map/ppermute | solution.py:226
  (694 shorter events, 370.1 us)
Async XLA Ops:
  14.4 106.2 %collective-permute-start.2 = (bf16[128,2048]{1,0:T(8,128)(2,1)S(1)}, bf16[128,2048]{1,0:T(8,128)(2,1)}, u32[]{:S(2)}, u32[]{:S(2)}) collective-permute-start(bf16[128,2048]{1,0:T(8,128)(2,1)S(1)} %constant_dynamic-update-slice_fusion), channel_id=1, source_target_pairs={{0,9},{1,8},{2,11},{3,10},{4,13},{5,12},{6,15},{7,14},{8,1},{9,0},... | collective-permute-start | bytes 1572872 | tf_op jit(solution)/shard_map/ppermute | solution.py:226
  15.8 104.8 %collective-permute-start.1 = (bf16[128,2048]{1,0:T(8,128)(2,1)S(1)}, bf16[128,2048]{1,0:T(8,128)(2,1)}, u32[]{:S(2)}, u32[]{:S(2)}) collective-permute-start(bf16[128,2048]{1,0:T(8,128)(2,1)S(1)} %constant_dynamic-update-slice_fusion), channel_id=1, source_target_pairs={{0,8},{1,9},{2,10},{3,11},{4,12},{5,13},{6,14},{7,15},{8,0},{9,1},... | collective-permute-start | bytes 1572872 | tf_op jit(solution)/shard_map/ppermute | solution.py:226
  22.3 34.3 %collective-permute-start.10 = (bf16[64,640]{1,0:T(8,128)(2,1)}, bf16[64,640]{1,0:T(8,128)(2,1)S(1)}, u32[]{:S(2)}, u32[]{:S(2)}) collective-permute-start(bf16[64,640]{1,0:T(8,128)(2,1)} %pad_maximum_fusion.23), channel_id=1, source_target_pairs={{0,1},{1,0},{2,3},{3,2},{4,5},{5,4},{6,7},{7,6},{8,9},{9,8},{10,11... | collective-permute-start | bytes 245768 | tf_op jit(solution)/shard_map/ppermute | solution.py:226
  87.0 34.2 %collective-permute-start = (bf16[128,2048]{1,0:T(8,128)(2,1)S(1)}, bf16[128,2048]{1,0:T(8,128)(2,1)S(1)}, u32[]{:S(2)}, u32[]{:S(2)}) collective-permute-start(bf16[128,2048]{1,0:T(8,128)(2,1)S(1)} %constant_dynamic-update-slice_fusion), channel_id=1, source_target_pairs={{0,1},{1,0},{2,3},{3,2},{4,5},{5,4},{6,7},{7,6},{8,9},{9,8},{10,11... | collective-permute-start | bytes 1572872 | tf_op jit(solution)/shard_map/ppermute | solution.py:226
  111.2 205.8 %collective-permute-start.56 = (bf16[128,2048]{1,0:T(8,128)(2,1)}, bf16[128,2048]{1,0:T(8,128)(2,1)}, u32[]{:S(2)}, u32[]{:S(2)}) collective-permute-start(bf16[128,2048]{1,0:T(8,128)(2,1)} %constant_dynamic-update-slice_fusion.113), channel_id=1, source_target_pairs={{0,9},{1,8},{2,11},{3,10},{4,13},{5,12},{6,15},{7,14},{8,1},{9,0},... | collective-permute-start | bytes 1572872 | tf_op jit(solution)/shard_map/ppermute | solution.py:226
  118.9 115.4 %collective-permute-start.48 = (bf16[256,1408]{1,0:T(8,128)(2,1)S(1)}, bf16[256,1408]{1,0:T(8,128)(2,1)S(1)}, u32[]{:S(2)}, u32[]{:S(2)}) collective-permute-start(bf16[256,1408]{1,0:T(8,128)(2,1)S(1)} %pad_maximum_fusion.11), channel_id=1, source_target_pairs={{0,2},{1,3},{2,0},{3,1},{4,6},{5,7},{6,4},{7,5},{8,10},{9,11},{10,... | collective-permute-start | bytes 2162696 | tf_op jit(solution)/shard_map/ppermute | solution.py:226
  120.5 56.4 %collective-permute-start.40 = (bf16[256,1408]{1,0:T(8,128)(2,1)S(1)}, bf16[256,1408]{1,0:T(8,128)(2,1)S(1)}, u32[]{:S(2)}, u32[]{:S(2)}) collective-permute-start(bf16[256,1408]{1,0:T(8,128)(2,1)S(1)} %pad_maximum_fusion.10), channel_id=1, source_target_pairs={{0,16},{1,17},{2,18},{3,19},{4,20},{5,21},{6,22},{7,23},{8,24},{9,... | collective-permute-start | bytes 2162696 | tf_op jit(solution)/shard_map/ppermute | solution.py:226
  120.6 42.0 %collective-permute-start.21 = (bf16[64,2048]{1,0:T(8,128)(2,1)S(1)}, bf16[64,2048]{1,0:T(8,128)(2,1)S(1)}, u32[]{:S(2)}, u32[]{:S(2)}) collective-permute-start(bf16[64,2048]{1,0:T(8,128)(2,1)S(1)} %collective-permute-done.19), channel_id=1, source_target_pairs={{0,2},{1,3},{2,0},{3,1},{4,6},{5,7},{6,4},{7,5},{8,10},{9,11},{10,... | collective-permute-start | bytes 786440 | tf_op jit(solution)/shard_map/ppermute | solution.py:226
  121.2 40.9 %collective-permute-start.20 = (bf16[64,2048]{1,0:T(8,128)(2,1)S(1)}, bf16[64,2048]{1,0:T(8,128)(2,1)S(1)}, u32[]{:S(2)}, u32[]{:S(2)}) collective-permute-start(bf16[64,2048]{1,0:T(8,128)(2,1)S(1)} %collective-permute-done.19), channel_id=1, source_target_pairs={{0,16},{1,17},{2,18},{3,19},{4,20},{5,21},{6,22},{7,23},{8,24},{9,... | collective-permute-start | bytes 786440 | tf_op jit(solution)/shard_map/ppermute | solution.py:226
  172.7 45.3 %collective-permute-start.47 = (bf16[256,1408]{1,0:T(8,128)(2,1)S(1)}, bf16[256,1408]{1,0:T(8,128)(2,1)}, u32[]{:S(2)}, u32[]{:S(2)}) collective-permute-start(bf16[256,1408]{1,0:T(8,128)(2,1)S(1)} %pad_maximum_fusion.11), channel_id=1, source_target_pairs={{0,16},{1,17},{2,18},{3,19},{4,20},{5,21},{6,22},{7,23},{8,24},{9,... | collective-permute-start | bytes 2162696 | tf_op jit(solution)/shard_map/ppermute | solution.py:226
  176.9 55.7 %collective-permute-start.33 = (bf16[256,1408]{1,0:T(8,128)(2,1)S(1)}, bf16[256,1408]{1,0:T(8,128)(2,1)S(1)}, u32[]{:S(2)}, u32[]{:S(2)}) collective-permute-start(bf16[256,1408]{1,0:T(8,128)(2,1)S(1)} %pad_maximum_fusion.9), channel_id=1, source_target_pairs={{0,16},{1,17},{2,18},{3,19},{4,20},{5,21},{6,22},{7,23},{8,24},{9,... | collective-permute-start | bytes 2162696 | tf_op jit(solution)/shard_map/ppermute | solution.py:226
  191.0 44.2 %collective-permute-start.23 = (bf16[256,2048]{1,0:T(8,128)(2,1)S(1)}, bf16[256,2048]{1,0:T(8,128)(2,1)S(1)}, u32[]{:S(2)}, u32[]{:S(2)}) collective-permute-start(bf16[256,2048]{1,0:T(8,128)(2,1)S(1)} %pad_maximum_fusion.7), channel_id=1, source_target_pairs={{0,4},{1,5},{2,6},{3,7},{4,0},{5,1},{6,2},{7,3},{8,12},{9,13},{10,... | collective-permute-start | bytes 3145736 | tf_op jit(solution)/shard_map/ppermute | solution.py:226
  232.6 57.2 %collective-permute-start.49 = (bf16[256,1408]{1,0:T(8,128)(2,1)}, bf16[256,1408]{1,0:T(8,128)(2,1)}, u32[]{:S(2)}, u32[]{:S(2)}) collective-permute-start(bf16[256,1408]{1,0:T(8,128)(2,1)} %collective-permute-done.47), channel_id=1, source_target_pairs={{0,2},{1,3},{2,0},{3,1},{4,6},{5,7},{6,4},{7,5},{8,10},{9,11},{10,... | collective-permute-start | bytes 2162696 | tf_op jit(solution)/shard_map/ppermute | solution.py:226
  251.7 35.8 %collective-permute-start.42 = (bf16[256,1408]{1,0:T(8,128)(2,1)}, bf16[256,1408]{1,0:T(8,128)(2,1)}, u32[]{:S(2)}, u32[]{:S(2)}) collective-permute-start(bf16[256,1408]{1,0:T(8,128)(2,1)} %copy-done.39), channel_id=1, source_target_pairs={{0,2},{1,3},{2,0},{3,1},{4,6},{5,7},{6,4},{7,5},{8,10},{9,11},{10,... | collective-permute-start | bytes 2162696 | tf_op jit(solution)/shard_map/ppermute | solution.py:226
  308.2 50.2 %collective-permute-start.43 = (bf16[1024,1408]{1,0:T(8,128)(2,1)}, bf16[1024,1408]{1,0:T(8,128)(2,1)}, u32[]{:S(2)}, u32[]{:S(2)}) collective-permute-start(bf16[1024,1408]{1,0:T(8,128)(2,1)} %get-tuple-element.131), channel_id=1, source_target_pairs={{0,4},{1,5},{2,6},{3,7},{4,0},{5,1},{6,2},{7,3},{8,12},{9,13},{10,... | collective-permute-start | bytes 8650760 | tf_op jit(solution)/shard_map/ppermute | solution.py:226
  310.1 52.7 %collective-permute-start.50 = (bf16[1024,1408]{1,0:T(8,128)(2,1)}, bf16[1024,1408]{1,0:T(8,128)(2,1)}, u32[]{:S(2)}, u32[]{:S(2)}) collective-permute-start(bf16[1024,1408]{1,0:T(8,128)(2,1)} %get-tuple-element.113), channel_id=1, source_target_pairs={{0,4},{1,5},{2,6},{3,7},{4,0},{5,1},{6,2},{7,3},{8,12},{9,13},{10,... | collective-permute-start | bytes 8650760 | tf_op jit(solution)/shard_map/ppermute | solution.py:226
  346.1 32.6 %collective-permute-start.36 = (bf16[1024,1408]{1,0:T(8,128)(2,1)}, bf16[1024,1408]{1,0:T(8,128)(2,1)}, u32[]{:S(2)}, u32[]{:S(2)}) collective-permute-start(bf16[1024,1408]{1,0:T(8,128)(2,1)} %get-tuple-element.122), channel_id=1, source_target_pairs={{0,4},{1,5},{2,6},{3,7},{4,0},{5,1},{6,2},{7,3},{8,12},{9,13},{10,... | collective-permute-start | bytes 8650760 | tf_op jit(solution)/shard_map/ppermute | solution.py:226
  418.6 34.8 %collective-permute-start.51 = (bf16[128,2048]{1,0:T(8,128)(2,1)S(1)}, bf16[128,2048]{1,0:T(8,128)(2,1)S(1)}, u32[]{:S(2)}, u32[]{:S(2)}) collective-permute-start(bf16[128,2048]{1,0:T(8,128)(2,1)S(1)} %get-tuple-element.78), channel_id=1, source_target_pairs={{0,1},{1,0},{2,3},{3,2},{4,5},{5,4},{6,7},{7,6},{8,9},{9,8},{10,11... | collective-permute-start | bytes 1572872 | tf_op jit(solution)/shard_map/ppermute | solution.py:226
  419.1 38.3 %collective-permute-start.53 = (bf16[128,2048]{1,0:T(8,128)(2,1)S(1)}, bf16[128,2048]{1,0:T(8,128)(2,1)S(1)}, u32[]{:S(2)}, u32[]{:S(2)}) collective-permute-start(bf16[128,2048]{1,0:T(8,128)(2,1)S(1)} %get-tuple-element.79), channel_id=1, source_target_pairs={{0,9},{1,8},{2,11},{3,10},{4,13},{5,12},{6,15},{7,14},{8,1},{9,0},... | collective-permute-start | bytes 1572872 | tf_op jit(solution)/shard_map/ppermute | solution.py:226
  437.5 227.2 %collective-permute-start.97 = (bf16[1024,1408]{1,0:T(8,128)(2,1)}, bf16[1024,1408]{1,0:T(8,128)(2,1)}, u32[]{:S(2)}, u32[]{:S(2)}) collective-permute-start(bf16[1024,1408]{1,0:T(8,128)(2,1)} %convolution_convert_fusion), channel_id=1, source_target_pairs={{0,4},{1,5},{2,6},{3,7},{4,0},{5,1},{6,2},{7,3},{8,12},{9,13},{10,... | collective-permute-start | bytes 8650760 | tf_op jit(solution)/shard_map/ppermute | solution.py:226
  437.5 235.3 %collective-permute-start.91 = (bf16[1024,1408]{1,0:T(8,128)(2,1)}, bf16[1024,1408]{1,0:T(8,128)(2,1)}, u32[]{:S(2)}, u32[]{:S(2)}) collective-permute-start(bf16[1024,1408]{1,0:T(8,128)(2,1)} %convolution_convert_fusion.1), channel_id=1, source_target_pairs={{0,4},{1,5},{2,6},{3,7},{4,0},{5,1},{6,2},{7,3},{8,12},{9,13},{10,... | collective-permute-start | bytes 8650760 | tf_op jit(solution)/shard_map/ppermute | solution.py:226
  530.7 57.8 %collective-permute-start.64 = (bf16[512,128]{0,1:T(8,128)(2,1)S(1)}, bf16[512,128]{0,1:T(8,128)(2,1)S(1)}, u32[]{:S(2)}, u32[]{:S(2)}) collective-permute-start(bf16[512,128]{0,1:T(8,128)(2,1)S(1)} %get-tuple-element.144), channel_id=1, source_target_pairs={{0,16},{1,17},{2,18},{3,19},{4,20},{5,21},{6,22},{7,23},{8,24},{9,... | collective-permute-start | bytes 393224 | tf_op jit(solution)/shard_map/ppermute | solution.py:226
  647.1 44.1 %collective-permute-start.85 = (bf16[1024,1408]{1,0:T(8,128)(2,1)S(1)}, bf16[1024,1408]{1,0:T(8,128)(2,1)S(1)}, u32[]{:S(2)}, u32[]{:S(2)}) collective-permute-start(bf16[1024,1408]{1,0:T(8,128)(2,1)S(1)} %copy-done.55), channel_id=1, source_target_pairs={{0,4},{1,5},{2,6},{3,7},{4,0},{5,1},{6,2},{7,3},{8,12},{9,13},{10,... | collective-permute-start | bytes 8650760 | tf_op jit(solution)/shard_map/ppermute | solution.py:226
  660.2 34.1 %collective-permute-start.84 = (bf16[64,2048]{1,0:T(8,128)(2,1)S(1)}, bf16[64,2048]{1,0:T(8,128)(2,1)S(1)}, u32[]{:S(2)}, u32[]{:S(2)}) collective-permute-start(bf16[64,2048]{1,0:T(8,128)(2,1)S(1)} %fusion.32), channel_id=1, source_target_pairs={{0,0},{16,1},{2,2},{18,3},{4,4},{20,5},{6,6},{22,7},{1,8},{17,9},{... | collective-permute-start | bytes 786440 | tf_op jit(solution)/shard_map/ppermute | solution.py:443
  668.7 34.6 %collective-permute-start.98 = (bf16[512,1408]{1,0:T(8,128)(2,1)S(1)}, bf16[512,1408]{1,0:T(8,128)(2,1)S(1)}, u32[]{:S(2)}, u32[]{:S(2)}) collective-permute-start(bf16[512,1408]{1,0:T(8,128)(2,1)S(1)} %slice.504), channel_id=1, source_target_pairs={{0,2},{1,3},{2,0},{3,1},{4,6},{5,7},{6,4},{7,5},{8,10},{9,11},{10,... | collective-permute-start | bytes 4325384 | tf_op jit(solution)/shard_map/ppermute | solution.py:226
  694.3 39.8 %collective-permute-start.92 = (bf16[512,1408]{1,0:T(8,128)(2,1)S(1)}, bf16[512,1408]{1,0:T(8,128)(2,1)S(1)}, u32[]{:S(2)}, u32[]{:S(2)}) collective-permute-start(bf16[512,1408]{1,0:T(8,128)(2,1)S(1)} %slice.505), channel_id=1, source_target_pairs={{0,2},{1,3},{2,0},{3,1},{4,6},{5,7},{6,4},{7,5},{8,10},{9,11},{10,... | collective-permute-start | bytes 4325384 | tf_op jit(solution)/shard_map/ppermute | solution.py:226
  697.0 66.8 %collective-permute-start.86 = (bf16[512,1408]{1,0:T(8,128)(2,1)S(1)}, bf16[512,1408]{1,0:T(8,128)(2,1)S(1)}, u32[]{:S(2)}, u32[]{:S(2)}) collective-permute-start(bf16[512,1408]{1,0:T(8,128)(2,1)S(1)} %slice.506), channel_id=1, source_target_pairs={{0,2},{1,3},{2,0},{3,1},{4,6},{5,7},{6,4},{7,5},{8,10},{9,11},{10,... | collective-permute-start | bytes 4325384 | tf_op jit(solution)/shard_map/ppermute | solution.py:226
  703.6 62.7 %collective-permute-start.99 = (bf16[256,1408]{1,0:T(8,128)(2,1)S(1)}, bf16[256,1408]{1,0:T(8,128)(2,1)S(1)}, u32[]{:S(2)}, u32[]{:S(2)}) collective-permute-start(bf16[256,1408]{1,0:T(8,128)(2,1)S(1)} %slice.507), channel_id=1, source_target_pairs={{0,16},{1,17},{2,18},{3,19},{4,20},{5,21},{6,22},{7,23},{8,24},{9,... | collective-permute-start | bytes 2162696 | tf_op jit(solution)/shard_map/ppermute | solution.py:226
  734.4 37.0 %collective-permute-start.93 = (bf16[256,1408]{1,0:T(8,128)(2,1)S(1)}, bf16[256,1408]{1,0:T(8,128)(2,1)S(1)}, u32[]{:S(2)}, u32[]{:S(2)}) collective-permute-start(bf16[256,1408]{1,0:T(8,128)(2,1)S(1)} %slice.508), channel_id=1, source_target_pairs={{0,16},{1,17},{2,18},{3,19},{4,20},{5,21},{6,22},{7,23},{8,24},{9,... | collective-permute-start | bytes 2162696 | tf_op jit(solution)/shard_map/ppermute | solution.py:226
  766.5 32.7 %collective-permute-start.102 = (bf16[64,1408]{1,0:T(8,128)(2,1)S(1)}, bf16[64,1408]{1,0:T(8,128)(2,1)S(1)}, u32[]{:S(2)}, u32[]{:S(2)}) collective-permute-start(bf16[64,1408]{1,0:T(8,128)(2,1)S(1)} %get-tuple-element.96), channel_id=1, source_target_pairs={{0,1},{1,0},{2,3},{3,2},{4,5},{5,4},{6,7},{7,6},{8,9},{9,8},{10,11... | collective-permute-start | bytes 540680 | tf_op jit(solution)/shard_map/ppermute | solution.py:226
  766.6 33.7 %collective-permute-start.101 = (bf16[64,1408]{1,0:T(8,128)(2,1)S(1)}, bf16[64,1408]{1,0:T(8,128)(2,1)S(1)}, u32[]{:S(2)}, u32[]{:S(2)}) collective-permute-start(bf16[64,1408]{1,0:T(8,128)(2,1)S(1)} %get-tuple-element.97), channel_id=1, source_target_pairs={{0,8},{1,9},{2,10},{3,11},{4,12},{5,13},{6,14},{7,15},{8,0},{9,1},... | collective-permute-start | bytes 540680 | tf_op jit(solution)/shard_map/ppermute | solution.py:226
  771.6 32.5 %collective-permute-start.96 = (bf16[64,1408]{1,0:T(8,128)(2,1)S(1)}, bf16[64,1408]{1,0:T(8,128)(2,1)S(1)}, u32[]{:S(2)}, u32[]{:S(2)}) collective-permute-start(bf16[64,1408]{1,0:T(8,128)(2,1)S(1)} %get-tuple-element.99), channel_id=1, source_target_pairs={{0,1},{1,0},{2,3},{3,2},{4,5},{5,4},{6,7},{7,6},{8,9},{9,8},{10,11... | collective-permute-start | bytes 540680 | tf_op jit(solution)/shard_map/ppermute | solution.py:226
  (143 other events, 2171.8 us)

commit v2 on v1

v2 whole, which is shorter than its diff:
```python
import functools
import math

import jax
import jax.numpy as jnp
from jax import lax
from jax.experimental import pallas as pl
from jax.experimental.pallas import tpu as pltpu
from jax.sharding import PartitionSpec as P

H = 32
KV = 4
HD = 64
AXES = ("seq", "fsdp")
norm_eps = 1e-05
rope_base = 10000.0
masked_value = -1e30
score_scale = HD ** (-0.5)
to_log2 = score_scale * math.log2(math.e)
bf16 = jnp.bfloat16
f32 = jnp.float32
KEY_TILE = 512
ONES = 16
LANES = 128
GAIN_ROWS = 16
CHUNKS = 2
HEADS = H // KV
PER_CHUNK = HEADS // CHUNKS
Q_COLS = HEADS * HD
QKV_COLS = Q_COLS + 2 * HD

SMEM_SPEC = pl.BlockSpec(memory_space=pltpu.SMEM)
VMEM_SPEC = pl.BlockSpec(memory_space=pltpu.VMEM)
ANY_SPEC = pl.BlockSpec(memory_space=pl.ANY)


def dot(a, b):
    return lax.dot_general(a, b, (((1,), (0,)), ((), ())), preferred_element_type=f32)


def dot_last(a, b):
    return lax.dot_general(a, b, (((1,), (1,)), ((), ())), preferred_element_type=f32)


def dot_first(a, b):
    return lax.dot_general(a, b, (((0,), (0,)), ((), ())), preferred_element_type=f32)


def inverse_rms(values):
    return lax.rsqrt(jnp.mean(values * values, axis=-1, keepdims=True) + norm_eps)


def rope_tables(positions):
    half = HD // 2
    frequency = rope_base ** (-(jnp.arange(half, dtype=f32) * 2.0) / HD)
    angles = positions.astype(f32)[None, :] * frequency[:, None]
    return (jnp.cos(angles), jnp.sin(angles))


def rotate(values, cosine, sine):
    a, b = values[: HD // 2], values[HD // 2 :]
    return jnp.concatenate([a * cosine - b * sine, b * cosine + a * sine], axis=0)


def unrotate(values, cosine, sine):
    a, b = values[: HD // 2], values[HD // 2 :]
    return jnp.concatenate([a * cosine + b * sine, b * cosine - a * sine], axis=0)


def hold(value, *others):
    return lax.optimization_barrier((value, others))[0]


def call(kernel, name, out, args, specs, flops, scratch=(), exps=0):
    out_shape = tuple(jax.ShapeDtypeStruct(s, d) for s, d in out)
    size = sum(a.size * a.dtype.itemsize for a in args)
    size += sum(math.prod(s.shape) * s.dtype.itemsize for s in out_shape)
    return pl.pallas_call(
        kernel,
        out_shape=out_shape,
        in_specs=specs,
        out_specs=(VMEM_SPEC,) * len(out_shape),
        scratch_shapes=list(scratch),
        compiler_params=pltpu.CompilerParams(vmem_limit_bytes=58 << 20),
        cost_estimate=pl.CostEstimate(flops=flops, bytes_accessed=size, transcendentals=exps),
        name=name,
    )(*args)


def columns_of(ref, starts, k):
    runs = [
        ref[:, pl.ds(pl.multiple_of(starts[2 * k + z], LANES), LANES)] for z in (0, 1)
    ]
    return jnp.concatenate(runs, axis=1)


def pack_kernel(member, q_ref, k_ref, v_ref, ga_ref, gf_ref, out_ref):
    slab = q_ref.shape[0]
    side = member[0]
    row = lax.broadcasted_iota(jnp.int32, (GAIN_ROWS, LANES), 0)
    lane = lax.broadcasted_iota(jnp.int32, (GAIN_ROWS, LANES), 1)
    gains = []
    for ref in (ga_ref, gf_ref):
        gains.append(jnp.concatenate([ref[...].astype(f32)] * (LANES // slab), axis=1))
    block = jnp.where(row == 0, gains[0], jnp.where(row == 1, gains[1], 0.0))
    block = jnp.where(lane // slab == side, block, 0.0).astype(bf16)
    block = jnp.concatenate([block, jnp.zeros((GAIN_ROWS, QKV_COLS - LANES), bf16)], axis=1)
    for i in range(4):
        at = i * (slab + GAIN_ROWS)
        out_ref[at : at + slab, :Q_COLS] = q_ref[:, i * Q_COLS : (i + 1) * Q_COLS]
        kv = [ref[:, i * HD : (i + 1) * HD] for ref in (k_ref, v_ref)]
        out_ref[at : at + slab, Q_COLS:] = jnp.concatenate(kv, axis=1)
        out_ref[at + slab : at + slab + GAIN_ROWS] = block


def pack_attention(side, w_query, w_key, w_value, gain_attn, gain_ffn):
    slab = w_query.shape[0]
    return call(
        pack_kernel,
        "pack_attention",
        [((4 * (slab + GAIN_ROWS), QKV_COLS), bf16)],
        [side, w_query, w_key, w_value, gain_attn.reshape(1, slab), gain_ffn.reshape(1, slab)],
        [SMEM_SPEC] + [VMEM_SPEC] * 5,
        0,
    )[0]


def pack_columns_kernel(cols, *refs):
    ins, out_ref = refs[:-1], refs[-1]
    slab = ins[0].shape[0]
    for i in range(4):
        for w, ref in enumerate(ins):
            out_ref[i * slab : (i + 1) * slab, w * cols : (w + 1) * cols] = ref[
                :, i * cols : (i + 1) * cols
            ]


def pack_columns(weights, name):
    slab, cols = weights[0].shape[0], weights[0].shape[1] // 4
    return call(
        functools.partial(pack_columns_kernel, cols),
        name,
        [((4 * slab, cols * len(weights)), bf16)],
        list(weights),
        [VMEM_SPEC] * len(weights),
        0,
    )[0]


def unpack_columns_kernel(cols, in_ref, *outs):
    slab = outs[0].shape[0]
    for i in range(4):
        for w, ref in enumerate(outs):
            ref[:, i * cols : (i + 1) * cols] = in_ref[
                i * slab : (i + 1) * slab, w * cols : (w + 1) * cols
            ].astype(f32)


def unpack_columns(value, count, name):
    slab, cols = value.shape[0] // 4, value.shape[1] // count
    return call(
        functools.partial(unpack_columns_kernel, cols),
        name,
        [((slab, 4 * cols), f32)] * count,
        [value],
        [VMEM_SPEC],
        0,
    )


def unpack_keys_kernel(member, in_ref, k_ref, v_ref, gain_ref):
    slab = k_ref.shape[0]
    gains = jnp.zeros((2, LANES), f32)
    keys, values = [], []
    for i in range(4):
        at = i * (slab + GAIN_ROWS)
        kv = in_ref[at : at + slab].astype(f32)
        keys.append(kv[:, :HD])
        values.append(kv[:, HD:])
        gains = gains + in_ref[at + slab : at + slab + GAIN_ROWS].astype(f32)[:2]
    k_ref[...] = jnp.concatenate(keys, axis=1)
    v_ref[...] = jnp.concatenate(values, axis=1)
    halves = [gains[:, j * slab : (j + 1) * slab] for j in range(2)]
    gain_ref[...] = jnp.where(member[0] == 0, halves[0], halves[1])


def unpack_keys(side, value):
    slab = value.shape[0] // 4 - GAIN_ROWS
    return call(
        unpack_keys_kernel,
        "unpack_keys",
        [((slab, 4 * HD), f32), ((slab, 4 * HD), f32), ((2, slab), f32)],
        [side, value],
        [SMEM_SPEC, VMEM_SPEC],
        0,
    )


def run_at(starts, j):
    start = starts[j]
    return pl.ds(start if isinstance(start, int) else pl.multiple_of(start, LANES), LANES)


def run_of(j):
    return slice(j * LANES, (j + 1) * LANES)


def sum_of(refs, columns=slice(None)):
    total = refs[0][:, columns].astype(f32)
    for ref in refs[1:]:
        total = total + ref[:, columns].astype(f32)
    return total


def middle_kernel(starts, tok_ref, gain_ref, *rest):
    parts, (mid_ref, h_ref) = rest[:4], rest[4:]
    middle = tok_ref[...].astype(f32) + sum_of(parts)
    mid_ref[...] = middle
    inverse = inverse_rms(middle)
    for j in range(tok_ref.shape[1] // LANES):
        run = run_at(starts, j)
        h_ref[:, run_of(j)] = (mid_ref[:, run] * inverse * gain_ref[:, run]).astype(bf16)


def middle_norm(starts, tokens, gain, parts):
    return call(
        middle_kernel,
        "middle_norm",
        [(tokens.shape, f32), (tokens.shape, bf16)],
        [starts, tokens, gain] + parts,
        [SMEM_SPEC] + [VMEM_SPEC] * 6,
        0,
    )


def arrange_kernel(starts, in_ref, out_ref):
    for j in range(in_ref.shape[1] // LANES):
        out_ref[:, run_of(j)] = in_ref[:, run_at(starts, j)]


def arrange(starts, value):
    return call(
        arrange_kernel,
        "arrange",
        [(value.shape, bf16)],
        [starts, value],
        [SMEM_SPEC, VMEM_SPEC],
        0,
    )[0]


def block_kernel(starts, mid_ref, part_ref, out_ref):
    rows = mid_ref.shape[0]
    parts = [part_ref.at[pl.ds(r * rows, rows)] for r in range(4)]
    for j in range(mid_ref.shape[1] // LANES):
        where = run_at(starts, j)
        out_ref[:, where] = (mid_ref[:, where] + sum_of(parts, run_of(j))).astype(bf16)


def block_output(starts, middle, parts):
    return call(
        block_kernel,
        "block_output",
        [(middle.shape, bf16)],
        [starts, middle, parts],
        [SMEM_SPEC, VMEM_SPEC, VMEM_SPEC],
        0,
    )[0]


def norm_back_kernel(starts, mid_ref, grad_ref, gain_ref, *rest):
    parts, (d_ref, low_ref, term_ref) = rest[:4], rest[4:]
    middle = mid_ref[...]
    inverse = inverse_rms(middle)
    for j in range(mid_ref.shape[1] // LANES):
        d_ref[:, run_at(starts, j)] = sum_of(parts, run_of(j))
    grad = d_ref[...]
    normed = middle * inverse
    term_ref[...] = jnp.sum(grad * normed, axis=0, keepdims=True)
    scaled = grad * gain_ref[...]
    mean = jnp.mean(scaled * normed, axis=-1, keepdims=True)
    d_middle = grad_ref[...].astype(f32) + inverse * (scaled - normed * mean)
    d_ref[...] = d_middle
    low_ref[...] = d_middle.astype(bf16)


def norm_back(starts, middle, out_grad, gain, parts):
    return call(
        norm_back_kernel,
        "norm_back",
        [(middle.shape, f32), (middle.shape, bf16), ((1, middle.shape[1]), f32)],
        [starts, middle, out_grad, gain] + parts,
        [SMEM_SPEC] + [VMEM_SPEC] * 7,
        0,
    )


def query_grad_kernel(count, starts, h_ref, d_ref, own_ref, other_ref):
    for ref, first in ((other_ref, count // 2), (own_ref, 0)):
        for k in range(count // 2):
            ref[k] = dot_first(columns_of(h_ref, starts, first + k), d_ref[...]).astype(bf16)


def query_grads(starts, h, d, count):
    half = (count // 2, 2 * LANES, d.shape[1])
    return call(
        functools.partial(query_grad_kernel, count),
        "query_grads",
        [(half, bf16), (half, bf16)],
        [starts, h, d],
        [SMEM_SPEC] + [VMEM_SPEC] * 2,
        2 * h.shape[0] * h.shape[1] * d.shape[1],
    )


def key_grad_kernel(count, starts, h_ref, d_ref, ga_ref, gf_ref, own_ref, other_ref):
    row = lax.broadcasted_iota(jnp.int32, (GAIN_ROWS, LANES), 0)
    slab = own_ref.shape[1] // 4 - GAIN_ROWS
    for ref, first in ((other_ref, count // 2), (own_ref, 0)):
        for k in range(count // 2):
            grad = dot_first(columns_of(h_ref, starts, first + k), d_ref[...]).astype(bf16)
            for i in range(4):
                where = run_at(starts, 2 * (first + k) + i // 2)
                gains = jnp.where(row == 0, ga_ref[:, where], gf_ref[:, where])
                at = i * (slab + GAIN_ROWS)
                ref[k, at : at + slab] = grad[i * slab : (i + 1) * slab]
                ref[k, at + slab : at + slab + GAIN_ROWS] = jnp.where(row < 2, gains, 0.0).astype(
                    bf16
                )


def key_grads(starts, h, d, gain_a, gain_f, count, slab):
    half = (count // 2, 4 * (slab + GAIN_ROWS), 2 * HD)
    return call(
        functools.partial(key_grad_kernel, count),
        "key_grads",
        [(half, bf16), (half, bf16)],
        [starts, h, d, gain_a, gain_f],
        [SMEM_SPEC] + [VMEM_SPEC] * 4,
        4 * h.shape[0] * h.shape[1] * HD,
    )


def weight_rows(piece):
    slab = piece.shape[0] // 4 - GAIN_ROWS
    at = [i * (slab + GAIN_ROWS) for i in range(4)]
    return jnp.concatenate([piece[a : a + slab] for a in at], axis=0)


def project_kernel(count, rows, starts, cos_ref, sin_ref, *rest):
    toks, pieces = rest[:4], rest[4 : 4 + count]
    h_ref, q_ref, kv_ref, gain_ref = rest[4 + count :]
    stride = pieces[0].shape[0] // 4
    for k in range(count):
        for z in (0, 1):
            gains = None
            for x in (0, 1):
                at = (2 * z + x + 1) * stride - GAIN_ROWS
                part = pieces[k][at : at + GAIN_ROWS, :LANES].astype(f32)
                gains = part if gains is None else gains + part
            gain_ref[:, run_at(starts, 2 * k + z)] = gains[:8]

    for r, tok_ref in enumerate(toks):
        wide = tok_ref[...].astype(f32)
        h_ref[r * rows : (r + 1) * rows] = (wide * inverse_rms(wide) * gain_ref[:1]).astype(bf16)
    total = None
    for k in range(count):
        product = dot(columns_of(h_ref, starts, k), weight_rows(pieces[k]))
        total = product if total is None else total + product
    turned = total.astype(bf16).astype(f32).T
    cosine, sine = cos_ref[...], sin_ref[...]
    for head in range(HEADS):
        q = rotate(turned[head * HD : (head + 1) * HD], cosine, sine).astype(bf16)
        at = head % PER_CHUNK * rows
        for r in range(4):
            q_ref[r, head // PER_CHUNK, :HD, at : at + rows] = q[:, r * rows : (r + 1) * rows]
    q_ref[:, :, HD:, :] = jnp.zeros((4, CHUNKS, HD, PER_CHUNK * rows), bf16)
    kv_ref[:HD] = rotate(turned[Q_COLS : Q_COLS + HD], cosine, sine).astype(bf16)
    kv_ref[HD:] = turned[Q_COLS + HD :].astype(bf16)


def project(starts, toks, cosine, sine, pieces):
    rows, width = toks[0].shape
    tok = 4 * rows
    count = len(pieces)
    return call(
        functools.partial(project_kernel, count, rows),
        "project",
        [
            ((tok, width), bf16),
            ((4, CHUNKS, 2 * HD, PER_CHUNK * rows), bf16),
            ((2 * HD, tok), bf16),
            ((8, width), f32),
        ],
        [starts, cosine, sine] + toks + pieces,
        [SMEM_SPEC] + [VMEM_SPEC] * (6 + count),
        2 * tok * width * QKV_COLS,
    )


def out_kernel(rows, places, attn_a_ref, attn_b_ref, *rest):
    pieces, parts, (attn_t_ref, w_ref) = rest[:-6], rest[-6:-2], rest[-2:]
    count = places.shape[0] // 2
    slab = pieces[0].shape[0] // count
    for k in range(2 * count):
        piece = pieces[k // count][k % count * slab : (k % count + 1) * slab, :]
        w_ref[pl.ds(pl.multiple_of(places[k], slab), slab), :] = piece
    for head in range(HEADS):
        at = head % PER_CHUNK * rows
        for r in range(4):
            block = (attn_a_ref, attn_b_ref)[r % 2][r // 2, head // PER_CHUNK, :, at : at + rows]
            attn_t_ref[head * HD : (head + 1) * HD, r * rows : (r + 1) * rows] = block.astype(bf16)
    step = 512
    for c in range(0, w_ref.shape[1], step):
        part = dot_first(attn_t_ref[...], w_ref[:, c : c + step]).astype(bf16)
        for r in range(4):
            parts[r][:, c : c + step] = part[r * rows : (r + 1) * rows]


def out_products(places, attn, pieces, rows):
    width = pieces[0].shape[1]
    tok = 4 * rows
    return call(
        functools.partial(out_kernel, rows),
        "out_products",
        [((rows, width), bf16)] * 4 + [((Q_COLS, tok), bf16), ((Q_COLS, width), bf16)],
        [places] + attn + pieces,
        [SMEM_SPEC] + [VMEM_SPEC] * (2 + len(pieces)),
        2 * tok * width * Q_COLS,
    )


def out_back_kernel(rows, w_ref, attn_a_ref, attn_b_ref, *rest):
    parts, (g_ref, delta_ref, d_ref) = rest[:4], rest[4:]
    for r in range(4):
        d_ref[r * rows : (r + 1) * rows] = parts[r][...]
    turned = dot_last(w_ref[...], d_ref[...]).astype(bf16)
    g_ref[:, :, :HD, :] = jnp.zeros((4, CHUNKS, HD, PER_CHUNK * rows), bf16)
    for head in range(HEADS):
        at = head % PER_CHUNK * rows
        chunk = head // PER_CHUNK
        for r in range(4):
            g = turned[head * HD : (head + 1) * HD, r * rows : (r + 1) * rows]
            g_ref[r, chunk, HD:, at : at + rows] = g
            attn = (attn_a_ref, attn_b_ref)[r % 2][r // 2, chunk, :, at : at + rows]
            delta = jnp.sum(g.astype(f32) * attn, axis=0, keepdims=True)
            delta_ref[r, chunk, :, at : at + rows] = delta


def out_back(w, attn, parts):
    rows, width = parts[0].shape
    return call(
        functools.partial(out_back_kernel, rows),
        "out_back",
        [
            ((4, CHUNKS, 2 * HD, PER_CHUNK * rows), bf16),
            ((4, CHUNKS, 1, PER_CHUNK * rows), f32),
        ],
        [w] + attn + parts,
        [VMEM_SPEC] * 7,
        8 * rows * width * Q_COLS,
        [pltpu.VMEM((4 * rows, width), bf16)],
    )


def out_grad_kernel(places, attn_t_ref, *rest):
    parts, (own_ref, other_ref, whole_ref, d_ref) = rest[:4], rest[4:]
    rows = parts[0].shape[0]
    for r in range(4):
        d_ref[r * rows : (r + 1) * rows] = parts[r][...]
    whole_ref[...] = dot(attn_t_ref[...], d_ref[...])
    half, slab = own_ref.shape[0], own_ref.shape[1]
    for k in range(half):
        for ref, place in ((own_ref, places[k]), (other_ref, places[half + k])):
            ref[k] = whole_ref[pl.ds(pl.multiple_of(place, slab), slab), :].astype(bf16)


def out_grads(places, attn_t, parts, slab):
    rows, width = parts[0].shape
    half = (places.shape[0] // 2, slab, width)
    return call(
        out_grad_kernel,
        "out_grads",
        [(half, bf16), (half, bf16)],
        [places, attn_t] + parts,
        [SMEM_SPEC] + [VMEM_SPEC] * 5,
        8 * rows * width * Q_COLS,
        [pltpu.VMEM((Q_COLS, width), f32), pltpu.VMEM((4 * rows, width), bf16)],
    )


def back_query_kernel(rows, dq0_ref, dq1_ref, cos_ref, sin_ref, d_ref, turned_ref):
    cosine, sine = cos_ref[...], sin_ref[...]
    for head in range(HEADS):
        at = head % PER_CHUNK * rows
        blocks = [
            (dq0_ref, dq1_ref)[r % 2][r // 2, head // PER_CHUNK, :, at : at + rows]
            for r in range(4)
        ]
        dq = jnp.concatenate(blocks, axis=1) * score_scale
        turned_ref[head * HD : (head + 1) * HD] = unrotate(dq, cosine, sine)
    d_ref[...] = turned_ref[...].T.astype(bf16)


def back_query(dq0, dq1, cosine, sine, rows):
    return call(
        functools.partial(back_query_kernel, rows),
        "back_query",
        [((4 * rows, Q_COLS), bf16)],
        [dq0, dq1, cosine, sine],
        [VMEM_SPEC] * 4,
        0,
        [pltpu.VMEM((Q_COLS, 4 * rows), f32)],
    )[0]


def back_project_kernel(count, rows, starts, dq_ref, kv_ref, cos_ref, sin_ref, *rest):
    toks, pieces, parts = rest[:4], rest[4 : 4 + count], rest[4 + count : 8 + count]
    d_ref, gain_ref, both_ref, inv_ref = rest[8 + count :]
    kv = kv_ref[...].T
    dk = unrotate(kv[:HD] * score_scale, cos_ref[...], sin_ref[...])
    d_ref[...] = jnp.concatenate([dk, kv[HD:]], axis=0).T.astype(bf16)
    both_ref[:, :Q_COLS] = dq_ref[...]
    both_ref[:, Q_COLS:] = d_ref[...]
    for r, tok_ref in enumerate(toks):
        inverse = inverse_rms(tok_ref[...].astype(f32))
        inv_ref[r * rows : (r + 1) * rows] = jnp.broadcast_to(inverse, (rows, LANES))
    for k in range(count):
        product = dot_last(both_ref[...], weight_rows(pieces[k]))
        for z in (0, 1):
            where = run_at(starts, 2 * k + z)
            term = None
            for r in range(4):
                at = slice(r * rows, (r + 1) * rows)
                value = product[at, run_of(z)]
                parts[r][:, where] = value.astype(bf16)
                normed = toks[r][:, where].astype(f32) * inv_ref[at]
                here = jnp.sum(value * normed, axis=0, keepdims=True)
                term = here if term is None else term + here
            gain_ref[:, where] = term


def back_project(starts, dq, kv_sum, cosine, sine, toks, pieces):
    rows, width = toks[0].shape
    tok = 4 * rows
    count = len(pieces)
    return call(
        functools.partial(back_project_kernel, count, rows),
        "back_project",
        [((rows, width), bf16)] * 4 + [((tok, 2 * HD), bf16), ((1, width), f32)],
        [starts, dq, kv_sum, cosine, sine] + toks + pieces,
        [SMEM_SPEC] + [VMEM_SPEC] * (8 + count),
        2 * tok * width * QKV_COLS,
        [pltpu.VMEM((tok, QKV_COLS), bf16), pltpu.VMEM((tok, LANES), f32)],
    )


def rows_of(tile):
    return pl.ds(pl.multiple_of(tile * KEY_TILE, KEY_TILE), KEY_TILE)


def causal(position, rows, columns):
    shape = (KEY_TILE, columns)
    key = lax.broadcasted_iota(jnp.int32, shape, 0)
    row = lax.broadcasted_iota(jnp.int32, shape, 1) % rows
    return key <= row + position % (KEY_TILE // rows) * rows


def fill_keys(place, rows, core, chip, own, all_ref, kvt_ref, kv_ref):
    per_tile = KEY_TILE // rows
    for p, (at, core_bit, member) in enumerate(place):
        where = pl.ds(pl.multiple_of((member ^ own) * rows, rows), rows)
        block = all_ref[core_bit ^ core, at ^ chip, :, where]
        kvt_ref[p // per_tile, :, p % per_tile * rows : (p % per_tile + 1) * rows] = block
        kv_ref[p * rows : (p + 1) * rows, :] = block.T


def forward_kernel(
    offsets, picks, place, rows, me_ref, q_ref, all_ref, o_ref, log_ref, kv_ref, kvt_ref, vt_ref
):
    me, core, chip, own = me_ref[0], me_ref[1], me_ref[2], me_ref[3]
    chunks = q_ref.shape[1]
    fill_keys(place, rows, core, chip, own, all_ref, kvt_ref, kv_ref)
    vt_ref[:, :ONES] = jnp.ones((vt_ref.shape[0], ONES, KEY_TILE), bf16)
    vt_ref[:, ONES:] = kvt_ref[:, HD:]
    for i, (pick, offset) in enumerate(zip(picks, offsets)):
        position = me ^ offset
        last = position // (KEY_TILE // rows)

        def scores(tile):
            kv = kv_ref[rows_of(tile), :]
            return [dot(kv, q_ref[pick, c]) for c in range(chunks)], vt_ref[tile]

        keep = causal(position, rows, q_ref.shape[3])
        found, vt = scores(last)
        state = []
        for s in found:
            s = jnp.where(keep, s, masked_value)
            top = jnp.max(s, axis=0, keepdims=True)
            state.append((top, dot(vt, jnp.exp2((s - top) * to_log2).astype(bf16))))

        def turn(kt, state):
            found, vt = scores(kt)
            out = []
            for s, (top, total) in zip(found, state):
                new_top = jnp.maximum(top, jnp.max(s, axis=0, keepdims=True))
                p = jnp.exp2((s - new_top) * to_log2).astype(bf16)
                out.append((new_top, total * jnp.exp2((top - new_top) * to_log2) + dot(vt, p)))
            return tuple(out)

        state = lax.fori_loop(0, last, turn, tuple(state))
        for c, (top, total) in enumerate(state):
            weight = total[:1]
            o_ref[i, c] = total[ONES:] / weight
            log_ref[i, c] = top * to_log2 + jnp.log2(weight)


def backward_kernel(offsets, picks, place, rows, core_mask, first, *refs):
    me_ref, q_ref, g_ref, all_ref, log_ref, delta_ref = refs[:6]
    kv_ref, kvt_ref = refs[-2:]
    if first:
        dq_ref, dkv_ref = refs[6:8]
        dkv_ref[...] = jnp.zeros_like(dkv_ref)
    else:
        begun_ref, dq_ref, own_ref, other_ref, dkv_ref = refs[6:11]
        dkv_ref[...] = begun_ref[...]
    me, core, chip, own = me_ref[0], me_ref[1], me_ref[2], me_ref[3]
    chunks = q_ref.shape[1]
    fill_keys(place, rows, core, chip, own, all_ref, kvt_ref, kv_ref)
    for i, (pick, offset) in enumerate(zip(picks, offsets)):
        position = me ^ offset
        last = position // (KEY_TILE // rows)

        def turn(tile, keep):
            kv = kv_ref[rows_of(tile), :]
            kvt = kvt_ref[tile]
            pairs = [(dot(kv, q_ref[pick, c]), dot(kv, g_ref[pick, c])) for c in range(chunks)]
            summed, out = None, []
            for c, (s, dp) in enumerate(pairs):
                p = jnp.exp2(s * to_log2 - log_ref[i, c])
                if keep is not None:
                    p = jnp.where(keep, p, 0.0)
                ds = (p * (dp - delta_ref[pick, c])).astype(bf16)
                part = dot_last(p.astype(bf16), g_ref[pick, c]) + dot_last(ds, q_ref[pick, c])
                summed = part if summed is None else summed + part
                out.append(dot(kvt, ds)[:HD])
            dkv_ref[rows_of(tile), :] += summed
            return tuple(out)

        dq = turn(last, causal(position, rows, q_ref.shape[3]))
        dq = lax.fori_loop(
            0, last, lambda tile, dq: tuple(a + b for a, b in zip(dq, turn(tile, None))), dq
        )
        for c in range(chunks):
            dq_ref[i, c] = dq[c]
    if not first:
        for p, (at, core_bit, member) in enumerate(place):
            if core_bit == 0:
                near = (p + core * core_mask) * rows
                far = (p + (1 - core) * core_mask) * rows
                where = pl.ds(pl.multiple_of((member ^ own) * rows, rows), rows)
                own_ref[at ^ chip, where] = dkv_ref[pl.ds(pl.multiple_of(near, rows), rows), :]
                other = dkv_ref[pl.ds(pl.multiple_of(far, rows), rows), :]
                other_ref[at ^ chip, where] = other.astype(bf16)


def attention_forward(me, q, kv_all, offsets, picks, place, rows):
    blocks, chunks, columns = len(picks), q.shape[1], q.shape[3]
    keys = len(place) * rows
    scores = blocks * chunks * columns * keys // 2
    return call(
        functools.partial(forward_kernel, offsets, picks, place, rows),
        "attention_forward",
        [((blocks, chunks, HD, columns), f32), ((blocks, chunks, 1, columns), f32)],
        [me, q, kv_all],
        [SMEM_SPEC, VMEM_SPEC, VMEM_SPEC],
        scores * 8 * HD,
        [
            pltpu.VMEM((keys, 2 * HD), bf16),
            pltpu.VMEM((keys // KEY_TILE, 2 * HD, KEY_TILE), bf16),
            pltpu.VMEM((keys // KEY_TILE, ONES + HD, KEY_TILE), bf16),
        ],
        scores,
    )


def attention_backward(
    me, q, g, kv_all, log_total, delta, dkv, offsets, picks, place, rows, core_mask
):
    chunks, columns = q.shape[1], q.shape[3]
    keys = len(place) * rows
    scores = len(picks) * chunks * columns * keys // 2
    shares = (kv_all.shape[1], kv_all.shape[3], 2 * HD)
    out = [((len(picks), chunks, HD, columns), f32)]
    scratch = [
        pltpu.VMEM((keys, 2 * HD), bf16),
        pltpu.VMEM((keys // KEY_TILE, 2 * HD, KEY_TILE), bf16),
    ]
    args = [me, q, g, kv_all, log_total, delta]
    if dkv is None:
        out = out + [((keys, 2 * HD), f32)]
    else:
        out = out + [(shares, f32), (shares, bf16)]
        scratch = [pltpu.VMEM((keys, 2 * HD), f32)] + scratch
        args = args + [dkv]
    return call(
        functools.partial(backward_kernel, offsets, picks, place, rows, core_mask, dkv is None),
        "attention_backward",
        out,
        args,
        [SMEM_SPEC] + [VMEM_SPEC] * (len(args) - 1),
        scores * 20 * HD,
        scratch,
        scores,
    )


def on_device(
    tokens, gain_attn, w_query, w_key, w_value, w_out, gain_ffn, w_gate, w_up, w_down, out_grad
):
    n_seq = lax.axis_size("seq")
    n_fsdp = lax.axis_size("fsdp")
    n = n_seq * n_fsdp
    me = lax.axis_index(AXES)
    rows, width = tokens.shape
    slab, hidden_width = w_gate.shape
    x_mask, z_mask, core = 1, 2 * n_fsdp, n_fsdp
    t_masks = [0, x_mask, z_mask, x_mask | z_mask]
    far = [n_fsdp << k for k in range(2, n_seq.bit_length() - 1)]
    near = [1 << k for k in range(1, n_fsdp.bit_length() - 1)]
    d_bits = far + near + [core]
    d_masks = [0]
    for bit in d_bits:
        d_masks = d_masks + [m | bit for m in d_masks]
    chips = d_masks[: len(d_masks) // 2]
    d_all = sum(d_bits)
    t_groups = [[b | m for m in t_masks] for b in sorted(d_masks)]

    def swap(value, mask):
        return lax.ppermute(value, AXES, [(i, i ^ mask) for i in range(n)])

    def trade(value, groups):
        return lax.all_to_all(
            value, AXES, split_axis=0, concat_axis=0, tiled=True, axis_index_groups=groups
        )

    def sum_blocks(value, count):
        value = value.reshape((count, -1) + value.shape[1:])
        total = value[0].astype(f32)
        for i in range(1, count):
            total = total + value[i].astype(f32)
        return total

    def spread(pieces, bits):
        pieces = dict(pieces)
        for bit in bits:
            pieces.update({m | bit: swap(v, bit) for m, v in list(pieces.items())})
        return pieces

    def beyond(pieces):
        return {m: v for m, v in pieces.items() if m}

    def joined(own, relayed):
        pieces = {**own, **relayed}
        half = [pieces[m] for m in chips]
        return half + [swap(p, core) for p in half]

    def sum_over(total, bits, after=None):
        for bit in reversed(bits):
            half = total.shape[0] // 2
            got = swap(total[half:].astype(bf16), bit)
            if after is not None:
                got = hold(got, after)
            total = total[:half].astype(f32) + got.astype(f32)
        return total

    def core_sum(pair):
        own, other = pair
        return own.astype(f32) + swap(other, core).astype(f32)

    unit = 2 * slab
    aligned = unit == LANES
    zs = jnp.array([0, z_mask], jnp.int32)
    relative = ((me & d_all) ^ jnp.array(d_masks, jnp.int32))[:, None] + zs[None, :]
    relative = (relative.reshape(-1) // 2 * unit).astype(jnp.int32)
    t = me % 2 + 2 * ((me // z_mask) % 2)
    fixed = [(m | z) // 2 * unit for m in sorted(d_masks) for z in (0, z_mask)]
    fixed = jnp.array(fixed, jnp.int32)
    d_groups = [[b | m for m in sorted(d_masks)] for b in t_masks]
    side = (me % 2).reshape(1).astype(jnp.int32)

    def arranged(value, where):
        return value.reshape(value.shape[0], -1, unit)[:, where // unit].reshape(value.shape)

    def restored(value, where):
        runs = value.reshape(value.shape[0], -1, unit)
        return jnp.zeros_like(runs).at[:, where // unit].set(runs).reshape(value.shape)

    if aligned:
        starts, n_pieces = relative, len(d_masks)
    else:
        starts, n_pieces = jnp.arange(0, width, LANES, dtype=jnp.int32), width // (2 * LANES)

    def copies(value, count):
        shape = (count,) + value.shape
        return jnp.broadcast_to(value[None], shape).reshape((-1,) + value.shape[1:])

    def gather_t(value):
        return [value] + [swap(value, m) for m in t_masks[1:]]

    def relay_t(value):
        along = swap(value, z_mask)
        return [value, swap(value, x_mask), along, swap(along, x_mask)]

    def scatter_t(parts):
        return [parts[0]] + [swap(p, m) for p, m in zip(parts[1:], t_masks[1:])]

    def blocks_of(value):
        return [value[r * rows : (r + 1) * rows] for r in range(4)]

    def send(total, bits):
        total = sum_over(total, bits[1:])
        half = total.shape[0] // 2
        return total[:half].astype(f32), swap(total[half:].astype(bf16), bits[0])

    def give_back(total):
        return trade(total.reshape(4 * slab, -1).astype(bf16), t_groups)

    def by_member(value):
        size = value.shape[0] // 4
        parts = [lax.dynamic_slice_in_dim(value, (t ^ r) * size, size, 0) for r in range(4)]
        return jnp.concatenate(parts, axis=0)

    qkv_shard = trade(pack_attention(side, w_query, w_key, w_value, gain_attn, gain_ffn), t_groups)
    cols = hidden_width // 4
    qkv_far = spread({0: qkv_shard}, far)
    qkv_own = spread({0: qkv_shard}, near)
    near_tokens = hold(tokens, qkv_shard)
    toks = [tokens] + [swap(near_tokens, m) for m in t_masks[1:3]]
    toks = toks + [swap(hold(tokens, qkv_far, qkv_own), t_masks[3])]
    qkv_w = joined(qkv_own, spread(beyond(qkv_far), near))
    if aligned:
        qkv_k = qkv_w
    else:
        parts = jnp.stack(qkv_w).reshape(-1, 2, 2, slab + GAIN_ROWS, QKV_COLS)
        runs = parts[:, :, :, :slab].reshape(-1, unit, QKV_COLS)
        whole = jnp.zeros_like(runs).at[relative // unit].set(runs).reshape(-1, 4, 64, QKV_COLS)
        gains = jnp.stack(
            [parts[:, :, x, slab:, x * slab : (x + 1) * slab] for x in (0, 1)], axis=3
        ).reshape(-1, GAIN_ROWS, unit)
        gains = jnp.zeros_like(gains).at[relative // unit].set(gains)
        gains = jnp.moveaxis(gains, 1, 0).reshape(GAIN_ROWS, -1, 2, 64)
        gains = jnp.moveaxis(gains, 0, 2)
        lane = jnp.arange(QKV_COLS) // 64
        extra = jnp.where(
            lane[None, None, None] == jnp.arange(2)[None, :, None, None],
            jnp.tile(gains, (1, 1, 1, QKV_COLS // 64)),
            jnp.zeros((), bf16),
        ).reshape(-1, 4, GAIN_ROWS, QKV_COLS)
        whole = jnp.concatenate([whole, extra], axis=2).reshape(n_pieces, -1, QKV_COLS)
        qkv_k = [whole[i] for i in range(n_pieces)]

    bits = n.bit_length() - 1
    source = {z_mask.bit_length() - 1: bits - 1, 0: bits - 2}
    free = list(range(bits - 2))
    open_places = [b for b in range(bits) if b not in source]
    for b in list(open_places):
        if b in free:
            source[b] = b
            free.remove(b)
            open_places.remove(b)
    source.update(zip(open_places, free))

    def goes_to(i):
        return sum(((i >> s) & 1) << b for b, s in source.items())

    def came_from(i):
        return sum(((i >> b) & 1) << s for b, s in source.items())

    per_group = n // 4
    out_shard = lax.ppermute(hold(w_out, qkv_shard), AXES, [(i, goes_to(i)) for i in range(n)])
    my_row = came_from(me) % per_group
    out_places = jnp.array([came_from(m) % per_group for m in d_masks], jnp.int32)
    out_places = ((my_row ^ out_places) * slab).astype(jnp.int32)

    out_shard = hold(out_shard, qkv_far)
    out_far = spread({0: out_shard}, far)
    out_own = spread({0: out_shard}, near)
    qkv_k, toks, out_far, out_own = lax.optimization_barrier((qkv_k, toks, out_far, out_own))
    out_all = {**out_own, **spread(beyond(out_far), near)}
    blocks = me ^ jnp.array(t_masks, jnp.int32)
    positions = (blocks[:, None] * rows + jnp.arange(rows, dtype=jnp.int32)).reshape(-1)
    cosine, sine = rope_tables(positions)
    h_attn, q, kv, gains = project(starts, toks, cosine, sine, qkv_k)
    gain_a, gain_f = gains[0:1], gains[1:2]
    pair_shard = trade(hold(pack_columns([w_gate, w_up], "pack_gate_up"), kv), t_groups)
    kv_parts = [kv] + [swap(kv, m) for m in chips[1:]]
    kv_parts, pair_shard, out_all = lax.optimization_barrier((kv_parts, pair_shard, out_all))
    kv = jnp.stack(kv_parts)
    kv_all = jnp.stack([kv, swap(kv, core)])
    place = [
        (
            chips.index(p & sum(far + near)),
            1 if p & core else 0,
            t_masks.index(p & (x_mask | z_mask)),
        )
        for p in range(n)
    ]
    my_chip = sum(((me // bit) % 2) << i for i, bit in enumerate(far + near))
    me_ref = jnp.stack([me, (me // core) % 2, my_chip, t]).astype(jnp.int32)

    pair_w = lax.all_gather(pair_shard, AXES, axis=0, tiled=True, axis_index_groups=d_groups)
    out_half = jnp.concatenate([out_all[m] for m in chips], axis=0)
    out_pieces = [out_half, swap(hold(out_half, kv_all), core)]
    down_shard = trade(pack_columns([hold(w_down, kv_all)], "pack_down"), t_groups)
    g4 = arrange(relative, out_grad) if aligned else arranged(out_grad, relative)

    def forward(x, q):
        return attention_forward(
            me_ref, q, kv_all, [x * x_mask, z_mask + x * x_mask], [x, 2 + x], place, rows
        )

    def backward(x, dkv):
        return attention_backward(
            me_ref,
            q,
            d_heads,
            kv_all,
            log_totals[x],
            delta,
            dkv,
            [x * x_mask, z_mask + x * x_mask],
            [x, 2 + x],
            place,
            rows,
            core,
        )

    attn_a, log_a = forward(0, q)
    attn_a, q_b, out_pieces, down_shard = lax.optimization_barrier(
        (attn_a, q, out_pieces, down_shard)
    )
    down_own = spread({0: hold(down_shard, attn_a)}, near)
    g = trade(copies(hold(g4, attn_a), 4), t_groups)
    attn_b, log_b = forward(1, q_b)
    attn, log_totals = [attn_a, attn_b], [log_a, log_b]
    *middle_parts, attn_t, out_w = out_products(out_places, attn, out_pieces, rows)
    middle_parts = scatter_t(middle_parts)

    def halves(pieces):
        half = jnp.concatenate([pieces[m] for m in chips], axis=0)
        return [half, swap(half, core)]

    middle_parts, down_own, g = lax.optimization_barrier((middle_parts, down_own, g))
    down_far = spread({0: hold(down_shard, middle_parts)}, far)
    g = by_member(hold(g, middle_parts))

    if aligned:
        middle, h = middle_norm(fixed, tokens, gain_f, middle_parts)
    else:
        middle = tokens.astype(f32) + sum([p.astype(f32) for p in middle_parts])
        h = arranged((middle * inverse_rms(middle) * gain_f).astype(bf16), fixed)
    h_parts = gather_t(h)
    h_parts, g = lax.optimization_barrier((h_parts, g))
    down_all = {**down_own, **spread(hold(beyond(down_far), h_parts), near)}
    h_ffn = jnp.concatenate(h_parts, axis=0)
    half_width = width // 2

    def by_halves(left, w):
        return dot(left[:, :half_width], w[0]) + dot(left[:, half_width:], w[1])

    down_w = halves(down_all)
    pair = dot(h_ffn, pair_w)
    gate, up = pair[:, :cols], pair[:, cols:]
    sig = jax.nn.sigmoid(gate)
    act = gate * sig
    hidden = (act * up).astype(bf16)
    d_hidden = by_halves(g, down_w)
    d_gate = (d_hidden * up * sig * (1.0 + gate * (1.0 - sig))).astype(bf16)
    d_up = (d_hidden * act).astype(bf16)
    d_pair = jnp.concatenate([d_gate, d_up], axis=1)
    d_hffn_part = dot_last(d_pair, pair_w).astype(bf16)
    d_hffn_blocks = blocks_of(d_hffn_part)
    d_hffn_parts = scatter_t(d_hffn_blocks)

    def weight_grad(left, right):
        other = dot_first(left[:, half_width:], right).astype(bf16)
        return dot_first(left[:, :half_width], right) + swap(other, core).astype(f32)

    pair_grad = dot_first(hold(h_ffn, d_hffn_blocks), d_pair).astype(bf16)
    pair_total = lax.psum_scatter(
        pair_grad, AXES, scatter_dimension=0, tiled=True, axis_index_groups=d_groups
    )
    block_part = jnp.concatenate(
        [dot_last(hold(hidden, pair_grad), w).astype(bf16) for w in down_w], axis=1
    )
    d_hffn_parts, pair_grad, block_part = lax.optimization_barrier(
        (d_hffn_parts, pair_grad, block_part)
    )
    down_sum = weight_grad(hold(g, d_hffn_parts), hidden)
    block_blocks = by_member(hold(block_part, d_hffn_parts))

    if aligned:
        d_middle, d_low, gain_ffn_term = norm_back(fixed, middle, out_grad, gain_f, d_hffn_parts)
    else:
        d_hffn = restored(sum([p.astype(f32) for p in d_hffn_parts]), fixed)
        inverse = inverse_rms(middle)
        normed = middle * inverse
        scaled = d_hffn * gain_f
        gain_ffn_term = jnp.sum(d_hffn * normed, axis=0, keepdims=True)
        d_middle = out_grad.astype(f32) + inverse * (
            scaled - normed * jnp.mean(scaled * normed, axis=-1, keepdims=True)
        )
        d_low = d_middle.astype(bf16)
    d_branch = relay_t(d_low)
    d_branch, down_sum, block_blocks = lax.optimization_barrier((d_branch, down_sum, block_blocks))
    d_heads, delta = out_back(out_w, attn, d_branch)

    block_parts = trade(hold(block_blocks, d_heads), t_groups)
    down_near = hold(down_sum, d_heads)
    for bit in reversed(near):
        half = down_near.shape[0] // 2
        down_got = swap(down_near[half:].astype(bf16), bit)
        down_near = down_near[:half].astype(f32)
        if bit != near[0]:
            down_near = down_near + down_got.astype(f32)
    out_pair = out_grads(out_places, attn_t, hold(d_branch, d_heads), slab)
    out_sum = core_sum(out_pair)
    dq0, dkv = backward(0, None)
    dkv, out_sum = lax.optimization_barrier((dkv, out_sum))
    out_keep, out_got = send(out_sum, near)
    dq1, own, other = backward(1, dkv)
    other, down_got, block_parts, out_got = lax.optimization_barrier(
        (other, down_got, block_parts, out_got)
    )
    kv_sums = own + swap(other, core).astype(f32)
    kv_sends = [kv_sums[i].astype(bf16) for i in range(len(chips))]
    kv_parts = [swap(kv_sends[i], m) for i, m in enumerate(chips) if m]
    dq0, dq1, block_parts, down_got, out_got, pair_total = hold(
        (dq0, dq1, block_parts, down_got, out_got, pair_total), kv_sends
    )
    d_query = back_query(dq0, dq1, cosine, sine, rows)
    if aligned:
        query_pair = query_grads(starts, h_attn, d_query, n_pieces)
    else:
        grads = dot_first(h_attn, d_query).astype(bf16).reshape(-1, unit, Q_COLS)
        grads = grads[relative // unit].reshape(len(d_masks), -1, Q_COLS)
        query_pair = grads[: len(chips)], grads[len(chips) :]
    query_sum = core_sum(query_pair)
    down_keep, down_got = send(down_near + down_got.astype(f32), far)
    pair_parts = trade(pair_total, t_groups)
    if aligned:
        block_out = block_output(relative, middle, block_parts)
    else:
        block_out = (middle + restored(sum_blocks(block_parts, 4), relative)).astype(bf16)
    kv_parts, query_sum, block_out = lax.optimization_barrier((kv_parts, query_sum, block_out))
    kv_sum = kv_sums[0]
    for part in kv_parts:
        kv_sum = kv_sum + part.astype(f32)
    query_keep, query_got = send(query_sum, near)
    out_keep, out_got = send(out_keep + out_got.astype(f32), far)
    *d_hattn_blocks, d_kv, gain_attn_part = back_project(
        starts, d_query, kv_sum, cosine, sine, toks, qkv_k
    )
    d_hattn_blocks, query_got = lax.optimization_barrier((d_hattn_blocks, query_got))
    query_keep, query_got = send(query_keep + query_got.astype(f32), far)
    d_hattn_parts = scatter_t(d_hattn_blocks)
    d_kv, gain_attn_part = hold((d_kv, gain_attn_part), d_hattn_blocks)
    if aligned:
        own, other = key_grads(starts, h_attn, d_kv, gain_attn_part, gain_ffn_term, n_pieces, slab)
    else:
        grads = dot_first(h_attn, d_kv).astype(bf16).reshape(-1, unit, 2 * HD)
        grads = grads[relative // unit].reshape(-1, 4, slab, 2 * HD)
        terms = jnp.concatenate([gain_attn_part, gain_ffn_term]).astype(bf16)
        terms = terms.reshape(2, -1, unit)[:, relative // unit].reshape(2, -1, 2, 1, unit)
        terms = jnp.moveaxis(jnp.broadcast_to(terms, terms.shape[:3] + (2, unit)), 0, 3)
        terms = terms.reshape(-1, 4, 2, unit)
        terms = jnp.pad(terms, ((0, 0), (0, 0), (0, GAIN_ROWS - 2), (0, 2 * HD - unit)))
        grads = jnp.concatenate([grads, terms], axis=2).reshape(len(d_masks), -1, 2 * HD)
        own, other = grads[: len(chips)], grads[len(chips) :]
    key_sum = core_sum((own, other))
    grad_gate, grad_up = unpack_columns(pair_parts, 2, "unpack_gate_up")
    d_hattn_parts, key_sum, query_got, out_got, down_got, grad_gate, grad_up = (
        lax.optimization_barrier(
            (d_hattn_parts, key_sum, query_got, out_got, down_got, grad_gate, grad_up)
        )
    )
    query_total = query_keep + query_got.astype(f32)
    out_total = (out_keep + out_got.astype(f32)).astype(bf16).reshape(slab, width)
    down_total = down_keep + down_got.astype(f32)
    key_total = sum_over(sum_over(key_sum, near), far)
    grad_query = unpack_columns(give_back(query_total), 1, "unpack_query")[0]
    grad_out_proj = lax.ppermute(out_total, AXES, [(goes_to(i), i) for i in range(n)]).astype(f32)
    grad_down = unpack_columns(give_back(down_total), 1, "unpack_down")[0]
    key_parts = trade(key_total.reshape(-1, 2 * HD).astype(bf16), t_groups)
    grad_key, grad_value, gain_terms = unpack_keys(side, key_parts)

    own = tokens.astype(f32)
    inverse_attn = inverse_rms(own)
    normed_attn = own * inverse_attn
    d_hattn = d_hattn_parts[0].astype(f32)
    for part in d_hattn_parts[1:]:
        d_hattn = d_hattn + part.astype(f32)
    scaled = d_hattn * gain_a
    grad_tokens = d_middle + inverse_attn * (
        scaled - normed_attn * jnp.mean(scaled * normed_attn, axis=-1, keepdims=True)
    )
    return (
        block_out,
        grad_tokens,
        gain_terms[0],
        grad_query,
        grad_key,
        grad_value,
        grad_out_proj,
        gain_terms[1],
        grad_gate,
        grad_up,
        grad_down,
    )


def solution(mesh):
    spec2 = P(AXES, None)
    spec1 = P(AXES)
    return jax.shard_map(
        on_device,
        mesh=mesh,
        in_specs=(
            spec2,
            spec1,
            spec2,
            spec2,
            spec2,
            spec2,
            spec1,
            spec2,
            spec2,
            spec2,
            spec2,
        ),
        out_specs=(
            spec2,
            spec2,
            spec1,
            spec2,
            spec2,
            spec2,
            spec2,
            spec1,
            spec2,
            spec2,
            spec2,
        ),
        check_vma=False,
    )
```

time: 829 us -> 654 us (0.79)
  starting transfers between devices: 197 us -> 111 us
  Pallas kernels: 29.3 us -> 100 us
  local copies, waits for them, and re-layouts: 96.2 us -> 28.4 us
  waiting for transfers between devices: 372 us -> 308 us
  matrix products: 73.8 us -> 49.6 us
  other arithmetic: 46.5 us -> 30.1 us
  between operations: 3.72 us -> 15.3 us
    ppermute x101 -> x53, starting transfers between devices: 187 us -> 60.2 us  [swap(): return lax.ppermute(value, AXES, [(i, i ^ mask) for i in range(n)])]
    ppermute x101 -> x53, waiting for transfers between devices: 359 us -> 271 us  [swap(): return lax.ppermute(value, AXES, [(i, i ^ mask) for i in range(n)])]
    pallas_call x2 -> x23, Pallas kernels: 29.3 us -> 100 us  [call(): pl.pallas_call(kernel, out_shape=out_shape, in_specs=specs, out_specs=(VM...]
    all_to_all x0 -> x9, starting transfers between devices: none -> 45.6 us  [trade(): lax.all_to_all(value, AXES, split_axis=0, concat_axis=0, tiled=True, axis...]
    unnamed x298 -> x109, local copies, waits for them, and re-layouts: 50.9 us -> 15.7 us
    concatenate x19 -> x3, local copies, waits for them, and re-layouts: 18.9 us -> 0.15 us  [the longest x1 0.09 us: halves(): half = jnp.concatenate([pieces[m] for m in chips], axis=0)]
    all_to_all x0 -> x9, waiting for transfers between devices: none -> 15.5 us  [trade(): lax.all_to_all(value, AXES, split_axis=0, concat_axis=0, tiled=True, axis...]
    concatenate x19 -> x3, other arithmetic: 13.8 us -> 1.89 us  [the longest x2 1.71 us: by_member(): return jnp.concatenate(parts, axis=0)]
  transfers between devices with their start and end apart: 103 -> 66, of which waited for: 45 -> 31; matrix products, arithmetic and copies ran while one was open for 20% -> 9% of each run, Pallas kernels for 4% -> 13%
where the time goes in v2:
time: 654 us; the launch traced here: 643 us
  waiting for transfers between devices  308 us (47%)
  starting transfers between devices  111 us (17%)
  Pallas kernels  100 us (15%)
  matrix products  49.6 us (8%)
  other arithmetic  30.1 us (5%)
  local copies, waits for them, and re-layouts  28.4 us (4%)
  between operations  15.3 us (2%)
    ppermute x53, waiting for transfers between devices, swap(): return lax.ppermute(value, AXES, [(i, i ^ mask) for i in range(n)])  271 us
    pallas_call x23, Pallas kernels, call(): pl.pallas_call(kernel, out_shape=out_shape, in_specs=specs, out_specs=(VM...  100 us
    ppermute x53, starting transfers between devices, swap(): return lax.ppermute(value, AXES, [(i, i ^ mask) for i in range(n)])  60.2 us
    all_to_all x9, starting transfers between devices, trade(): lax.all_to_all(value, AXES, split_axis=0, concat_axis=0, tiled=True, axis...  45.6 us
    ppermute x1, waiting for transfers between devices, on_device(): lax.ppermute(hold(w_out, qkv_shard), AXES, [(i, goes_to(i)) for i in rang...  21 us
    dot_general x3, matrix products, dot_first(): lax.dot_general(a, b, (((0,), (0,)), ((), ())), preferred_element_type=f32)  18.7 us
    dot_general x3, matrix products, dot(): lax.dot_general(a, b, (((1,), (0,)), ((), ())), preferred_element_type=f32)  18.1 us
    unnamed x109, local copies, waits for them, and re-layouts  15.7 us
  transfers between devices with their start and end apart: 66, of which 31 were waited for; matrix products, arithmetic and copies ran while one was open for 9% of the time, Pallas kernels for 13%

profile of v2, /device:TPU:8, one launch (start us, length us, event | category | flops | bytes accessed | tf_op | source)
XLA Modules:
  0.0 642.9 jit_solution(4981528813414593931)
XLA Ops:
  13.2 6.2 all-to-all-done
  28.7 21.0 %collective-permute-done.10 = bf16[64,2048]{1,0:T(8,128)(2,1)} collective-permute-done((bf16[64,2048]{1,0:T(8,128)(2,1)}, bf16[64,2048]{1,0:T(8,128)(2,1)}, u32[]{:S(2)}, u32[]{:S(2)}) %collective-permute-start.10) | collective-permute-done | bytes 262176 | tf_op jit(solution)/shard_map/ppermute | solution.py:881
  75.5 6.6 %project.1 = (bf16[512,2048]{1,0:T(8,128)(2,1)}, bf16[4,2,128,512]{3,2,1,0:T(8,128)(2,1)}, bf16[128,512]{1,0:T(8,128)(2,1)}, f32[8,2048]{1,0:T(8,128)}) custom-call(s32[16]{0:T(128)} %fusion.24.starts, f32[32,512]{1,0:T(8,128)} %get-tuple-element.338.cos_ref, f32[32,512]{1,0:T(8,128)} %get-tuple-element.337.sin_ref, bf16[128,2048]{1,0:T(8,128)(2,1)} %rest_0_.1, ...), custom_call_target="tpu_custom_call" | custom-call | flops 1342177280 | bytes 8847424 | tf_op jit(solution)/shard_map/project/pallas_call | solution.py:78
  92.4 14.6 %collective-permute-done.13 = bf16[128,512]{1,0:T(8,128)(2,1)S(1)} collective-permute-done((bf16[128,512]{1,0:T(8,128)(2,1)S(1)}, bf16[128,512]{1,0:T(8,128)(2,1)S(1)}, u32[]{:S(2)}, u32[]{:S(2)}) %collective-permute-start.13) | collective-permute-done | bytes 131104 | tf_op jit(solution)/shard_map/ppermute | solution.py:740
  123.1 6.8 %attention_forward.2 = (f32[2,2,64,512]{3,2,1,0:T(8,128)}, f32[2,2,1,512]{3,2,1,0:T(1,128)}) custom-call(s32[4]{0:T(128)} %pad_add_fusion.me_ref.refs_0_, bf16[4,2,128,512]{3,2,1,0:T(8,128)(2,1)} %get-tuple-element.196.q_ref.refs_1_, bf16[2,4,128,512]{3,2,1,0:T(8,128)(2,1)} %pad_maximum_fusion.6.all_ref.refs_3_), custom_call_target="tpu_custom_call" | custom-call | flops 2147483648 | bytes 2629648 | tf_op jit(solution)/shard_map/attention_forward/pallas_call | solution.py:78
  129.9 6.7 %all-to-all-done.2 = bf16[4,64,1408]{2,1,0:T(8,128)(2,1)S(1)} async-done(((bf16[4,64,1408]{2,1,0:T(8,128)(2,1)}), bf16[4,64,1408]{2,1,0:T(8,128)(2,1)S(1)}, u32[]{:S(2)}, u32[]{:S(2)}) %all-to-all-start.2) | async-done | bytes 720928 | tf_op jit(solution)/shard_map/all_to_all | solution.py:743
  138.2 5.7 all-to-all-start.3
  144.5 7.0 %attention_forward.3 = (f32[2,2,64,512]{3,2,1,0:T(8,128)}, f32[2,2,1,512]{3,2,1,0:T(1,128)}) custom-call(s32[4]{0:T(128)} %pad_add_fusion.me_ref.refs_0_, bf16[4,2,128,512]{3,2,1,0:T(8,128)(2,1)} %get-tuple-element.196.q_ref.refs_1_, bf16[2,4,128,512]{3,2,1,0:T(8,128)(2,1)} %pad_maximum_fusion.6.all_ref.refs_3_), custom_call_target="tpu_custom_call" | custom-call | flops 2147483648 | bytes 2629648 | tf_op jit(solution)/shard_map/attention_forward/pallas_call | solution.py:78
  151.5 5.4 out_products.1
  160.4 19.2 %collective-permute-done.19.rest_1_ = bf16[128,2048]{1,0:T(8,128)(2,1)} collective-permute-done((bf16[128,2048]{1,0:T(8,128)(2,1)}, bf16[128,2048]{1,0:T(8,128)(2,1)}, u32[]{:S(2)}, u32[]{:S(2)}) %collective-permute-start.19) | collective-permute-done | bytes 524320 | tf_op jit(solution)/shard_map/ppermute | solution.py:740
  179.6 33.1 %collective-permute-done.20.rest_2_ = bf16[128,2048]{1,0:T(8,128)(2,1)} collective-permute-done((bf16[128,2048]{1,0:T(8,128)(2,1)}, bf16[128,2048]{1,0:T(8,128)(2,1)}, u32[]{:S(2)}, u32[]{:S(2)}) %collective-permute-start.20) | collective-permute-done | bytes 524320 | tf_op jit(solution)/shard_map/ppermute | solution.py:740
  212.7 14.7 %collective-permute-done.21.rest_3_ = bf16[128,2048]{1,0:T(8,128)(2,1)} collective-permute-done((bf16[128,2048]{1,0:T(8,128)(2,1)}, bf16[128,2048]{1,0:T(8,128)(2,1)}, u32[]{:S(2)}, u32[]{:S(2)}) %collective-permute-start.21) | collective-permute-done | bytes 524320 | tf_op jit(solution)/shard_map/ppermute | solution.py:740
  239.9 10.1 %collective-permute-done.23 = bf16[128,2048]{1,0:T(8,128)(2,1)S(1)} collective-permute-done((bf16[128,2048]{1,0:T(8,128)(2,1)}, bf16[128,2048]{1,0:T(8,128)(2,1)S(1)}, u32[]{:S(2)}, u32[]{:S(2)}) %collective-permute-start.23) | collective-permute-done | bytes 524320 | tf_op jit(solution)/shard_map/ppermute | solution.py:740
  250.0 14.3 %collective-permute-done.24 = bf16[128,2048]{1,0:T(8,128)(2,1)S(1)} collective-permute-done((bf16[128,2048]{1,0:T(8,128)(2,1)}, bf16[128,2048]{1,0:T(8,128)(2,1)S(1)}, u32[]{:S(2)}, u32[]{:S(2)}) %collective-permute-start.24) | collective-permute-done | bytes 524320 | tf_op jit(solution)/shard_map/ppermute | solution.py:740
  264.3 10.1 %collective-permute-done.25 = bf16[128,2048]{1,0:T(8,128)(2,1)S(1)} collective-permute-done((bf16[128,2048]{1,0:T(8,128)(2,1)}, bf16[128,2048]{1,0:T(8,128)(2,1)S(1)}, u32[]{:S(2)}, u32[]{:S(2)}) %collective-permute-start.25) | collective-permute-done | bytes 524320 | tf_op jit(solution)/shard_map/ppermute | solution.py:740
  274.6 16.8 %collective-permute-done.27 = bf16[256,1408]{1,0:T(8,128)(2,1)S(1)} collective-permute-done((bf16[256,1408]{1,0:T(8,128)(2,1)S(1)}, bf16[256,1408]{1,0:T(8,128)(2,1)S(1)}, u32[]{:S(2)}, u32[]{:S(2)}) %collective-permute-start.27) | collective-permute-done | bytes 720928 | tf_op jit(solution)/shard_map/ppermute | solution.py:740
  301.9 10.8 %fusion.31 = f32[512,2816]{1,0:T(8,128)S(1)} fusion(bf16[512,2048]{1,0:T(8,128)(2,1)} %copy-done.39, bf16[2048,2816]{1,0:T(8,128)(2,1)} %all-gather.2.cloned.1.call-done), kind=kOutput, calls=%fused_computation.111 | convolution fusion | flops 5905580032 | bytes 19398656 | tf_op jit(solution)/shard_map/dot_general | solution.py:38
  316.6 6.4 convolution_convert_fusion.2
  325.3 9.2 %convolution_convert_fusion = bf16[2048,2816]{1,0:T(8,128)(2,1)} fusion(bf16[512,2048]{1,0:T(8,128)(2,1)S(1)} %copy-done.40, bf16[512,1408]{1,0:T(8,128)(2,1)S(1)} %get-tuple-element.316, bf16[512,1408]{1,0:T(8,128)(2,1)S(1)} %get-tuple-element.315), kind=kOutput, calls=%fused_computation | convolution fusion | flops 5917114368 | bytes 16515072 | tf_op jit(solution)/shard_map/dot_general | solution.py:46
  351.4 11.7 %collective-permute-done.31.rest_3_ = bf16[128,2048]{1,0:T(8,128)(2,1)S(1)} collective-permute-done((bf16[128,2048]{1,0:T(8,128)(2,1)}, bf16[128,2048]{1,0:T(8,128)(2,1)S(1)}, u32[]{:S(2)}, u32[]{:S(2)}) %collective-permute-start.31) | collective-permute-done | bytes 524320 | tf_op jit(solution)/shard_map/ppermute | solution.py:740
  374.8 22.4 %collective-permute-done.33.rest_2_ = bf16[128,2048]{1,0:T(8,128)(2,1)S(1)} collective-permute-done((bf16[128,2048]{1,0:T(8,128)(2,1)}, bf16[128,2048]{1,0:T(8,128)(2,1)S(1)}, u32[]{:S(2)}, u32[]{:S(2)}) %collective-permute-start.33) | collective-permute-done | bytes 524320 | tf_op jit(solution)/shard_map/ppermute | solution.py:740
  398.9 6.1 convert_add_fusion
  405.0 5.6 collective-permute-done.34.rest_3_
  427.5 10.0 %attention_backward.2 = (f32[2,2,64,512]{3,2,1,0:T(8,128)}, f32[4096,128]{1,0:T(8,128)}) custom-call(s32[4]{0:T(128)} %pad_add_fusion.me_ref.refs_0_, bf16[4,2,128,512]{3,2,1,0:T(8,128)(2,1)} %get-tuple-element.196.q_ref.refs_1_, bf16[4,2,128,512]{3,2,1,0:T(8,128)(2,1)} %get-tuple-element.241.refs_2_, ...), custom_call_target="tpu_custom_call" | custom-call | flops 5368709120 | bytes 5791760 | tf_op jit(solution)/shard_map/attention_backward/pallas_call | solution.py:78
  442.7 10.8 %attention_backward.3 = (f32[2,2,64,512]{3,2,1,0:T(8,128)}, f32[4,512,128]{2,1,0:T(8,128)}, bf16[4,512,128]{2,1,0:T(8,128)(2,1)}) custom-call(s32[4]{0:T(128)} %pad_add_fusion.me_ref.refs_0_, bf16[4,2,128,512]{3,2,1,0:T(8,128)(2,1)} %get-tuple-element.196.q_ref.refs_1_, bf16[4,2,128,512]{3,2,1,0:T(8,128)(2,1)} %get-tuple-element.241.refs_2_, ...), custom_call_target="tpu_custom_call" | custom-call | flops 5368709120 | bytes 7364624 | tf_op jit(solution)/shard_map/attention_backward/pallas_call | solution.py:78
  453.5 23.8 %collective-permute-done.37 = bf16[512,1408]{1,0:T(8,128)(2,1)S(1)} collective-permute-done((bf16[512,1408]{1,0:T(8,128)(2,1)S(1)}, bf16[512,1408]{1,0:T(8,128)(2,1)S(1)}, u32[]{:S(2)}, u32[]{:S(2)}) %collective-permute-start.37) | collective-permute-done | bytes 1441824 | tf_op jit(solution)/shard_map/ppermute | solution.py:740
  478.4 9.9 %collective-permute-done.38 = bf16[2,64,2048]{2,1,0:T(8,128)(2,1)} collective-permute-done((bf16[2,64,2048]{2,1,0:T(8,128)(2,1)S(1)}, bf16[2,64,2048]{2,1,0:T(8,128)(2,1)}, u32[]{:S(2)}, u32[]{:S(2)}) %collective-permute-start.38) | collective-permute-done | bytes 524320 | tf_op jit(solution)/shard_map/ppermute | solution.py:740
  520.5 6.6 %back_project.1 = (bf16[128,2048]{1,0:T(8,128)(2,1)}, bf16[128,2048]{1,0:T(8,128)(2,1)}, bf16[128,2048]{1,0:T(8,128)(2,1)}, bf16[128,2048]{1,0:T(8,128)(2,1)}, b...) custom-call(s32[16]{0:T(128)} %fusion.24.starts, bf16[512,512]{1,0:T(8,128)(2,1)} %back_query.1.d_ref.dq_ref, ...), custom_call_target="tpu_custom_call" | custom-call | flops 1342177280 | bytes 8527936 | tf_op jit(solution)/shard_map/back_project/pallas_call | solution.py:78
  546.6 20.9 %collective-permute-done.51 = bf16[256,1408]{1,0:T(8,128)(2,1)} collective-permute-done((bf16[256,1408]{1,0:T(8,128)(2,1)}, bf16[256,1408]{1,0:T(8,128)(2,1)}, u32[]{:S(2)}, u32[]{:S(2)}) %collective-permute-start.51) | collective-permute-done | bytes 720928 | tf_op jit(solution)/shard_map/ppermute | solution.py:740
  567.5 14.7 %collective-permute-done.49 = bf16[1,256,512]{2,1,0:T(8,128)(2,1)} collective-permute-done((bf16[1,256,512]{2,1,0:T(8,128)(2,1)}, bf16[1,256,512]{2,1,0:T(8,128)(2,1)}, u32[]{:S(2)}, u32[]{:S(2)}) %collective-permute-start.49) | collective-permute-done | bytes 262176 | tf_op jit(solution)/shard_map/ppermute | solution.py:740
  596.4 5.5 all-to-all-start.6
  605.8 5.7 all-to-all-start.7
  (297 shorter events, 249.3 us)
Async XLA Ops:
  19.4 30.3 %collective-permute-start = (bf16[320,640]{1,0:T(8,128)(2,1)S(1)}, bf16[320,640]{1,0:T(8,128)(2,1)S(1)}, u32[]{:S(2)}, u32[]{:S(2)}) collective-permute-start(bf16[320,640]{1,0:T(8,128)(2,1)S(1)} %bitcast.70), channel_id=1, source_target_pairs={{0,16},{1,17},{2,18},{3,19},{4,20},{5,21},{6,22},{7,23},{8,24},{9,... | collective-permute-start | bytes 1228808 | tf_op jit(solution)/shard_map/ppermute | solution.py:740
  22.7 27.0 %collective-permute-start.10 = (bf16[64,2048]{1,0:T(8,128)(2,1)}, bf16[64,2048]{1,0:T(8,128)(2,1)}, u32[]{:S(2)}, u32[]{:S(2)}) collective-permute-start(bf16[64,2048]{1,0:T(8,128)(2,1)} %param.21), channel_id=1, source_target_pairs={{0,0},{1,16},{2,2},{3,18},{4,4},{5,20},{6,6},{7,22},{8,1},{9,17},{... | collective-permute-start | bytes 786440 | tf_op jit(solution)/shard_map/ppermute | solution.py:881
  26.1 25.9 %collective-permute-start.1 = (bf16[320,640]{1,0:T(8,128)(2,1)S(1)}, bf16[320,640]{1,0:T(8,128)(2,1)S(1)}, u32[]{:S(2)}, u32[]{:S(2)}) collective-permute-start(bf16[320,640]{1,0:T(8,128)(2,1)S(1)} %bitcast.71), channel_id=1, source_target_pairs={{0,2},{1,3},{2,0},{3,1},{4,6},{5,7},{6,4},{7,5},{8,10},{9,11},{10,... | collective-permute-start | bytes 1228808 | tf_op jit(solution)/shard_map/ppermute | solution.py:740
  27.7 29.3 %collective-permute-start.7 = (bf16[128,2048]{1,0:T(8,128)(2,1)}, bf16[128,2048]{1,0:T(8,128)(2,1)S(1)}, u32[]{:S(2)}, u32[]{:S(2)}) collective-permute-start(bf16[128,2048]{1,0:T(8,128)(2,1)} %rest_0_.1), channel_id=1, source_target_pairs={{0,1},{1,0},{2,3},{3,2},{4,5},{5,4},{6,7},{7,6},{8,9},{9,8},{10,11... | collective-permute-start | bytes 1572872 | tf_op jit(solution)/shard_map/ppermute | solution.py:740
  27.7 29.3 %collective-permute-start.8 = (bf16[128,2048]{1,0:T(8,128)(2,1)}, bf16[128,2048]{1,0:T(8,128)(2,1)S(1)}, u32[]{:S(2)}, u32[]{:S(2)}) collective-permute-start(bf16[128,2048]{1,0:T(8,128)(2,1)} %rest_0_.1), channel_id=1, source_target_pairs={{0,8},{1,9},{2,10},{3,11},{4,12},{5,13},{6,14},{7,15},{8,0},{9,1},... | collective-permute-start | bytes 1572872 | tf_op jit(solution)/shard_map/ppermute | solution.py:740
  52.1 22.4 %collective-permute-start.9 = (bf16[128,2048]{1,0:T(8,128)(2,1)}, bf16[128,2048]{1,0:T(8,128)(2,1)S(1)}, u32[]{:S(2)}, u32[]{:S(2)}) collective-permute-start(bf16[128,2048]{1,0:T(8,128)(2,1)} %rest_0_.1), channel_id=1, source_target_pairs={{0,9},{1,8},{2,11},{3,10},{4,13},{5,12},{6,15},{7,14},{8,1},{9,0},... | collective-permute-start | bytes 1572872 | tf_op jit(solution)/shard_map/ppermute | solution.py:740
  82.2 26.2 %all-to-all-start.1 = ((bf16[4,64,2816]{2,1,0:T(8,128)(2,1)}), bf16[4,64,2816]{2,1,0:T(8,128)(2,1)S(1)}, u32[]{:S(2)}, u32[]{:S(2)}) async-start(bf16[4,64,2816]{2,1,0:T(8,128)(2,1)} %bitcast.10), calls=%async_computation.1 | async-start | bytes 2883584 | tf_op jit(solution)/shard_map/all_to_all | solution.py:743
  87.5 214.3 %all-gather.2.cloned.1.call-start = ((), (), s32[]{:S(2)}) async-start(), calls=%async_computation.10 | async-start | bytes 12976128 | tf_op jit(solution)/shard_map/all_gather | solution.py:912
  138.2 89.2 %all-to-all-start.3 = ((bf16[4,128,2048]{2,1,0:T(8,128)(2,1)}), bf16[4,128,2048]{2,1,0:T(8,128)(2,1)S(1)}, u32[]{:S(2)}, u32[]{:S(2)}) async-start(bf16[4,128,2048]{2,1,0:T(8,128)(2,1)} %broadcast_in_dim.2), calls=%async_computation.3 | async-start | bytes 4194304 | tf_op jit(solution)/shard_map/all_to_all | solution.py:743
  143.9 348.7 %reduce-scatter.2.cloned.1.call-start = ((), (), s32[]{:S(2)}) async-start(), calls=%async_computation.11 | async-start | bytes 12976128 | tf_op jit(solution)/shard_map/reduce_scatter | solution.py:991
  144.4 82.9 %collective-permute-start.22 = (bf16[256,1408]{1,0:T(8,128)(2,1)S(1)}, bf16[256,1408]{1,0:T(8,128)(2,1)S(1)}, u32[]{:S(2)}, u32[]{:S(2)}) collective-permute-start(bf16[256,1408]{1,0:T(8,128)(2,1)S(1)} %bitcast.75), channel_id=1, source_target_pairs={{0,2},{1,3},{2,0},{3,1},{4,6},{5,7},{6,4},{7,5},{8,10},{9,11},{10,... | collective-permute-start | bytes 2162696 | tf_op jit(solution)/shard_map/ppermute | solution.py:740
  156.9 22.7 %collective-permute-start.19 = (bf16[128,2048]{1,0:T(8,128)(2,1)}, bf16[128,2048]{1,0:T(8,128)(2,1)}, u32[]{:S(2)}, u32[]{:S(2)}) collective-permute-start(bf16[128,2048]{1,0:T(8,128)(2,1)} %get-tuple-element.203), channel_id=1, source_target_pairs={{0,1},{1,0},{2,3},{3,2},{4,5},{5,4},{6,7},{7,6},{8,9},{9,8},{10,11... | collective-permute-start | bytes 1572872 | tf_op jit(solution)/shard_map/ppermute | solution.py:740
  158.4 54.3 %collective-permute-start.20 = (bf16[128,2048]{1,0:T(8,128)(2,1)}, bf16[128,2048]{1,0:T(8,128)(2,1)}, u32[]{:S(2)}, u32[]{:S(2)}) collective-permute-start(bf16[128,2048]{1,0:T(8,128)(2,1)} %get-tuple-element.204), channel_id=1, source_target_pairs={{0,8},{1,9},{2,10},{3,11},{4,12},{5,13},{6,14},{7,15},{8,0},{9,1},... | collective-permute-start | bytes 1572872 | tf_op jit(solution)/shard_map/ppermute | solution.py:740
  158.9 68.4 %collective-permute-start.21 = (bf16[128,2048]{1,0:T(8,128)(2,1)}, bf16[128,2048]{1,0:T(8,128)(2,1)}, u32[]{:S(2)}, u32[]{:S(2)}) collective-permute-start(bf16[128,2048]{1,0:T(8,128)(2,1)} %get-tuple-element.205), channel_id=1, source_target_pairs={{0,9},{1,8},{2,11},{3,10},{4,13},{5,12},{6,15},{7,14},{8,1},{9,0},... | collective-permute-start | bytes 1572872 | tf_op jit(solution)/shard_map/ppermute | solution.py:740
  227.3 47.0 %collective-permute-start.26 = (bf16[256,1408]{1,0:T(8,128)(2,1)S(1)}, bf16[256,1408]{1,0:T(8,128)(2,1)S(1)}, u32[]{:S(2)}, u32[]{:S(2)}) collective-permute-start(bf16[256,1408]{1,0:T(8,128)(2,1)S(1)} %bitcast.76), channel_id=1, source_target_pairs={{0,16},{1,17},{2,18},{3,19},{4,20},{5,21},{6,22},{7,23},{8,24},{9,... | collective-permute-start | bytes 2162696 | tf_op jit(solution)/shard_map/ppermute | solution.py:740
  236.4 27.9 %collective-permute-start.24 = (bf16[128,2048]{1,0:T(8,128)(2,1)}, bf16[128,2048]{1,0:T(8,128)(2,1)S(1)}, u32[]{:S(2)}, u32[]{:S(2)}) collective-permute-start(bf16[128,2048]{1,0:T(8,128)(2,1)} %get-tuple-element.220), channel_id=1, source_target_pairs={{0,8},{1,9},{2,10},{3,11},{4,12},{5,13},{6,14},{7,15},{8,0},{9,1},... | collective-permute-start | bytes 1572872 | tf_op jit(solution)/shard_map/ppermute | solution.py:740
  236.4 38.0 %collective-permute-start.25 = (bf16[128,2048]{1,0:T(8,128)(2,1)}, bf16[128,2048]{1,0:T(8,128)(2,1)S(1)}, u32[]{:S(2)}, u32[]{:S(2)}) collective-permute-start(bf16[128,2048]{1,0:T(8,128)(2,1)} %get-tuple-element.220), channel_id=1, source_target_pairs={{0,9},{1,8},{2,11},{3,10},{4,13},{5,12},{6,15},{7,14},{8,1},{9,0},... | collective-permute-start | bytes 1572872 | tf_op jit(solution)/shard_map/ppermute | solution.py:740
  338.4 24.7 %collective-permute-start.31 = (bf16[128,2048]{1,0:T(8,128)(2,1)}, bf16[128,2048]{1,0:T(8,128)(2,1)S(1)}, u32[]{:S(2)}, u32[]{:S(2)}) collective-permute-start(bf16[128,2048]{1,0:T(8,128)(2,1)} %get-tuple-element.322), channel_id=1, source_target_pairs={{0,9},{1,8},{2,11},{3,10},{4,13},{5,12},{6,15},{7,14},{8,1},{9,0},... | collective-permute-start | bytes 1572872 | tf_op jit(solution)/shard_map/ppermute | solution.py:740
  366.5 32.3 %collective-permute-start.35 = (bf16[1024,1408]{1,0:T(8,128)(2,1)}, bf16[1024,1408]{1,0:T(8,128)(2,1)}, u32[]{:S(2)}, u32[]{:S(2)}) collective-permute-start(bf16[1024,1408]{1,0:T(8,128)(2,1)} %convolution_convert_fusion.1), channel_id=1, source_target_pairs={{0,4},{1,5},{2,6},{3,7},{4,0},{5,1},{6,2},{7,3},{8,12},{9,13},{10,... | collective-permute-start | bytes 8650760 | tf_op jit(solution)/shard_map/ppermute | solution.py:740
  370.9 34.1 %collective-permute-start.32 = (bf16[128,2048]{1,0:T(8,128)(2,1)}, bf16[128,2048]{1,0:T(8,128)(2,1)S(1)}, u32[]{:S(2)}, u32[]{:S(2)}) collective-permute-start(bf16[128,2048]{1,0:T(8,128)(2,1)} %get-tuple-element.247.rest_0_), channel_id=1, source_target_pairs={{0,1},{1,0},{2,3},{3,2},{4,5},{5,4},{6,7},{7,6},{8,9},{9,8},{10,11... | collective-permute-start | bytes 1572872 | tf_op jit(solution)/shard_map/ppermute | solution.py:740
  371.2 26.0 %collective-permute-start.33 = (bf16[128,2048]{1,0:T(8,128)(2,1)}, bf16[128,2048]{1,0:T(8,128)(2,1)S(1)}, u32[]{:S(2)}, u32[]{:S(2)}) collective-permute-start(bf16[128,2048]{1,0:T(8,128)(2,1)} %get-tuple-element.247.rest_0_), channel_id=1, source_target_pairs={{0,8},{1,9},{2,10},{3,11},{4,12},{5,13},{6,14},{7,15},{8,0},{9,1},... | collective-permute-start | bytes 1572872 | tf_op jit(solution)/shard_map/ppermute | solution.py:740
  416.2 72.1 %all-to-all-start.4 = ((bf16[4,128,2048]{2,1,0:T(8,128)(2,1)}), bf16[4,128,2048]{2,1,0:T(8,128)(2,1)S(1)}, u32[]{:S(2)}, u32[]{:S(2)}) async-start(bf16[4,128,2048]{2,1,0:T(8,128)(2,1)} %bitcast.68), calls=%async_computation.4 | async-start | bytes 4194304 | tf_op jit(solution)/shard_map/all_to_all | solution.py:743
  427.4 49.9 %collective-permute-start.37 = (bf16[512,1408]{1,0:T(8,128)(2,1)S(1)}, bf16[512,1408]{1,0:T(8,128)(2,1)S(1)}, u32[]{:S(2)}, u32[]{:S(2)}) collective-permute-start(bf16[512,1408]{1,0:T(8,128)(2,1)S(1)} %slice.226), channel_id=1, source_target_pairs={{0,2},{1,3},{2,0},{3,1},{4,6},{5,7},{6,4},{7,5},{8,10},{9,11},{10,... | collective-permute-start | bytes 4325384 | tf_op jit(solution)/shard_map/ppermute | solution.py:740
  440.6 47.7 %collective-permute-start.38 = (bf16[2,64,2048]{2,1,0:T(8,128)(2,1)S(1)}, bf16[2,64,2048]{2,1,0:T(8,128)(2,1)}, u32[]{:S(2)}, u32[]{:S(2)}) collective-permute-start(bf16[2,64,2048]{2,1,0:T(8,128)(2,1)S(1)} %slice.229), channel_id=1, source_target_pairs={{0,2},{1,3},{2,0},{3,1},{4,6},{5,7},{6,4},{7,5},{8,10},{9,11},{10,... | collective-permute-start | bytes 1572872 | tf_op jit(solution)/shard_map/ppermute | solution.py:740
  506.6 36.8 %all-to-all-start.5 = ((bf16[4,64,2816]{2,1,0:T(8,128)(2,1)}), bf16[4,64,2816]{2,1,0:T(8,128)(2,1)}, u32[]{:S(2)}, u32[]{:S(2)}) async-start(bf16[4,64,2816]{2,1,0:T(8,128)(2,1)} %bitcast.82), calls=%async_computation.6 | async-start | bytes 2883584 | tf_op jit(solution)/shard_map/all_to_all | solution.py:743
  516.6 22.3 %collective-permute-start.50 = (bf16[1,64,2048]{2,1,0:T(8,128)(2,1)}, bf16[1,64,2048]{2,1,0:T(8,128)(2,1)}, u32[]{:S(2)}, u32[]{:S(2)}) collective-permute-start(bf16[1,64,2048]{2,1,0:T(8,128)(2,1)} %slice.230), channel_id=1, source_target_pairs={{0,16},{1,17},{2,18},{3,19},{4,20},{5,21},{6,22},{7,23},{8,24},{9,... | collective-permute-start | bytes 786440 | tf_op jit(solution)/shard_map/ppermute | solution.py:740
  533.8 33.7 %collective-permute-start.51 = (bf16[256,1408]{1,0:T(8,128)(2,1)}, bf16[256,1408]{1,0:T(8,128)(2,1)}, u32[]{:S(2)}, u32[]{:S(2)}) collective-permute-start(bf16[256,1408]{1,0:T(8,128)(2,1)} %slice.227), channel_id=1, source_target_pairs={{0,16},{1,17},{2,18},{3,19},{4,20},{5,21},{6,22},{7,23},{8,24},{9,... | collective-permute-start | bytes 2162696 | tf_op jit(solution)/shard_map/ppermute | solution.py:740
  536.9 45.3 %collective-permute-start.45 = (bf16[128,2048]{1,0:T(8,128)(2,1)}, bf16[128,2048]{1,0:T(8,128)(2,1)}, u32[]{:S(2)}, u32[]{:S(2)}) collective-permute-start(bf16[128,2048]{1,0:T(8,128)(2,1)} %get-tuple-element.284), channel_id=1, source_target_pairs={{0,1},{1,0},{2,3},{3,2},{4,5},{5,4},{6,7},{7,6},{8,9},{9,8},{10,11... | collective-permute-start | bytes 1572872 | tf_op jit(solution)/shard_map/ppermute | solution.py:740
  538.9 43.3 %collective-permute-start.46 = (bf16[128,2048]{1,0:T(8,128)(2,1)}, bf16[128,2048]{1,0:T(8,128)(2,1)}, u32[]{:S(2)}, u32[]{:S(2)}) collective-permute-start(bf16[128,2048]{1,0:T(8,128)(2,1)} %get-tuple-element.285), channel_id=1, source_target_pairs={{0,8},{1,9},{2,10},{3,11},{4,12},{5,13},{6,14},{7,15},{8,0},{9,1},... | collective-permute-start | bytes 1572872 | tf_op jit(solution)/shard_map/ppermute | solution.py:740
  538.9 43.3 %collective-permute-start.47 = (bf16[128,2048]{1,0:T(8,128)(2,1)}, bf16[128,2048]{1,0:T(8,128)(2,1)}, u32[]{:S(2)}, u32[]{:S(2)}) collective-permute-start(bf16[128,2048]{1,0:T(8,128)(2,1)} %get-tuple-element.286), channel_id=1, source_target_pairs={{0,9},{1,8},{2,11},{3,10},{4,13},{5,12},{6,15},{7,14},{8,1},{9,0},... | collective-permute-start | bytes 1572872 | tf_op jit(solution)/shard_map/ppermute | solution.py:740
  542.3 39.9 %collective-permute-start.49 = (bf16[1,256,512]{2,1,0:T(8,128)(2,1)}, bf16[1,256,512]{2,1,0:T(8,128)(2,1)}, u32[]{:S(2)}, u32[]{:S(2)}) collective-permute-start(bf16[1,256,512]{2,1,0:T(8,128)(2,1)} %slice.231), channel_id=1, source_target_pairs={{0,16},{1,17},{2,18},{3,19},{4,20},{5,21},{6,22},{7,23},{8,24},{9,... | collective-permute-start | bytes 786440 | tf_op jit(solution)/shard_map/ppermute | solution.py:740
  603.8 22.2 %collective-permute-start.54 = (bf16[64,2048]{1,0:T(8,128)(2,1)}, bf16[64,2048]{1,0:T(8,128)(2,1)}, u32[]{:S(2)}, u32[]{:S(2)}) collective-permute-start(bf16[64,2048]{1,0:T(8,128)(2,1)} %fusion.19), channel_id=1, source_target_pairs={{0,0},{16,1},{2,2},{18,3},{4,4},{20,5},{6,6},{22,7},{1,8},{17,9},{... | collective-permute-start | bytes 786440 | tf_op jit(solution)/shard_map/ppermute | solution.py:1093
  (84 other events, 994.2 us)
Sparse Core Ops, SparseCore 0:
  109.7 115.1 all-gather.1
  334.7 134.2 reduce-scatter.1

commit v3 on v2

--- a/solution.py
+++ b/solution.py
@@ -162,6 +162,27 @@
         functools.partial(unpack_columns_kernel, cols),
         name,
         [((slab, 4 * cols), f32)] * count,
+        [value],
+        [VMEM_SPEC],
+        0,
+    )
+
+
+def unpack_two_kernel(in_ref, first_ref, second_ref):
+    slab = first_ref.shape[0]
+    wide, cols = first_ref.shape[1] // 4, second_ref.shape[1] // 4
+    for i in range(4):
+        rows = slice(i * slab, (i + 1) * slab)
+        first_ref[:, i * wide : (i + 1) * wide] = in_ref[rows, :wide].astype(f32)
+        second_ref[:, i * cols : (i + 1) * cols] = in_ref[rows, wide:].astype(f32)
+
+
+def unpack_two(value, wide, name):
+    slab, cols = value.shape[0] // 4, value.shape[1] - wide
+    return call(
+        unpack_two_kernel,
+        name,
+        [((slab, 4 * wide), f32), ((slab, 4 * cols), f32)],
         [value],
         [VMEM_SPEC],
         0,
@@ -1079,19 +1100,18 @@
         grads = jnp.concatenate([grads, terms], axis=2).reshape(len(d_masks), -1, 2 * HD)
         own, other = grads[: len(chips)], grads[len(chips) :]
     key_sum = core_sum((own, other))
+    after = d_hattn_parts[1:]
     grad_gate, grad_up = unpack_columns(pair_parts, 2, "unpack_gate_up")
-    d_hattn_parts, key_sum, query_got, out_got, down_got, grad_gate, grad_up = (
-        lax.optimization_barrier(
-            (d_hattn_parts, key_sum, query_got, out_got, down_got, grad_gate, grad_up)
-        )
-    )
+    key_sum, query_got, out_got, down_got = hold((key_sum, query_got, out_got, down_got), after)
+    d_hattn_parts, grad_gate, grad_up = lax.optimization_barrier((d_hattn_parts, grad_gate, grad_up))
     query_total = query_keep + query_got.astype(f32)
     out_total = (out_keep + out_got.astype(f32)).astype(bf16).reshape(slab, width)
     down_total = down_keep + down_got.astype(f32)
     key_total = sum_over(sum_over(key_sum, near), far)
-    grad_query = unpack_columns(give_back(query_total), 1, "unpack_query")[0]
     grad_out_proj = lax.ppermute(out_total, AXES, [(goes_to(i), i) for i in range(n)]).astype(f32)
-    grad_down = unpack_columns(give_back(down_total), 1, "unpack_down")[0]
+    merged = [v.reshape(4 * slab, -1).astype(bf16) for v in (query_total, down_total)]
+    merged = trade(jnp.concatenate(merged, axis=1), t_groups)
+    grad_query, grad_down = unpack_two(merged, Q_COLS, "unpack_query_down")
     key_parts = trade(key_total.reshape(-1, 2 * HD).astype(bf16), t_groups)
     grad_key, grad_value, gain_terms = unpack_keys(side, key_parts)
 

time: 654 us -> 649 us (level)
  waiting for transfers between devices: 308 us -> 319 us
    all_to_all x9 -> x8, starting transfers between devices: 45.6 us -> 39.6 us  [trade(): lax.all_to_all(value, AXES, split_axis=0, concat_axis=0, tiled=True, axis...]
    pallas_call x23 -> x22, Pallas kernels: 100 us -> 99 us  [call(): pl.pallas_call(kernel, out_shape=out_shape, in_specs=specs, out_specs=(VM...]
    unnamed x109 -> x133, local copies, waits for them, and re-layouts: 15.7 us -> 15.8 us
    all_to_all x9 -> x8, waiting for transfers between devices: 15.5 us -> 15.5 us  [trade(): lax.all_to_all(value, AXES, split_axis=0, concat_axis=0, tiled=True, axis...]
  transfers between devices with their start and end apart: 66 -> 65, of which waited for: 31 -> 31; matrix products, arithmetic and copies ran while one was open for 9% -> 9% of each run, Pallas kernels for 13% -> 13%
where the time goes in v3:
time: 649 us; the launch traced here: 639 us
  waiting for transfers between devices  319 us (49%)
  starting transfers between devices  105 us (16%)
  Pallas kernels  99 us (15%)
  matrix products  49.6 us (8%)
  other arithmetic  25.9 us (4%)
  local copies, waits for them, and re-layouts  25.3 us (4%)
  between operations  15.4 us (2%)
    ppermute x53, waiting for transfers between devices, swap(): return lax.ppermute(value, AXES, [(i, i ^ mask) for i in range(n)])  276 us
    pallas_call x22, Pallas kernels, call(): pl.pallas_call(kernel, out_shape=out_shape, in_specs=specs, out_specs=(VM...  99 us
    ppermute x53, starting transfers between devices, swap(): return lax.ppermute(value, AXES, [(i, i ^ mask) for i in range(n)])  60 us
    all_to_all x8, starting transfers between devices, trade(): lax.all_to_all(value, AXES, split_axis=0, concat_axis=0, tiled=True, axis...  39.6 us
    ppermute x1, waiting for transfers between devices, on_device(): lax.ppermute(hold(w_out, qkv_shard), AXES, [(i, goes_to(i)) for i in rang...  21 us
    dot_general x3, matrix products, dot_first(): lax.dot_general(a, b, (((0,), (0,)), ((), ())), preferred_element_type=f32)  18.7 us
    dot_general x3, matrix products, dot(): lax.dot_general(a, b, (((1,), (0,)), ((), ())), preferred_element_type=f32)  18 us
    unnamed x133, local copies, waits for them, and re-layouts  15.8 us
  transfers between devices with their start and end apart: 65, of which 31 were waited for; matrix products, arithmetic and copies ran while one was open for 9% of the time, Pallas kernels for 13%

profile of v3, /device:TPU:8, one launch (start us, length us, event | category | flops | bytes accessed | tf_op | source)
XLA Modules:
  0.0 638.8 jit_solution(2830483793358735541)
XLA Ops:
  13.2 6.2 all-to-all-done
  28.7 21.0 %collective-permute-done.10 = bf16[64,2048]{1,0:T(8,128)(2,1)} collective-permute-done((bf16[64,2048]{1,0:T(8,128)(2,1)}, bf16[64,2048]{1,0:T(8,128)(2,1)}, u32[]{:S(2)}, u32[]{:S(2)}) %collective-permute-start.10) | collective-permute-done | bytes 262176 | tf_op jit(solution)/shard_map/ppermute | solution.py:902
  75.6 6.6 %project.1 = (bf16[512,2048]{1,0:T(8,128)(2,1)}, bf16[4,2,128,512]{3,2,1,0:T(8,128)(2,1)}, bf16[128,512]{1,0:T(8,128)(2,1)}, f32[8,2048]{1,0:T(8,128)}) custom-call(s32[16]{0:T(128)} %fusion.25.starts, f32[32,512]{1,0:T(8,128)} %get-tuple-element.342.cos_ref, f32[32,512]{1,0:T(8,128)} %get-tuple-element.341.sin_ref, bf16[128,2048]{1,0:T(8,128)(2,1)} %rest_0_.1, ...), custom_call_target="tpu_custom_call" | custom-call | flops 1342177280 | bytes 8847424 | tf_op jit(solution)/shard_map/project/pallas_call | solution.py:78
  92.4 14.6 %collective-permute-done.13 = bf16[128,512]{1,0:T(8,128)(2,1)S(1)} collective-permute-done((bf16[128,512]{1,0:T(8,128)(2,1)S(1)}, bf16[128,512]{1,0:T(8,128)(2,1)S(1)}, u32[]{:S(2)}, u32[]{:S(2)}) %collective-permute-start.13) | collective-permute-done | bytes 131104 | tf_op jit(solution)/shard_map/ppermute | solution.py:761
  123.1 6.8 %attention_forward.2 = (f32[2,2,64,512]{3,2,1,0:T(8,128)}, f32[2,2,1,512]{3,2,1,0:T(1,128)}) custom-call(s32[4]{0:T(128)} %pad_add_fusion.me_ref.refs_0_, bf16[4,2,128,512]{3,2,1,0:T(8,128)(2,1)} %get-tuple-element.198.q_ref.refs_1_, bf16[2,4,128,512]{3,2,1,0:T(8,128)(2,1)} %pad_maximum_fusion.6.all_ref.refs_3_), custom_call_target="tpu_custom_call" | custom-call | flops 2147483648 | bytes 2629648 | tf_op jit(solution)/shard_map/attention_forward/pallas_call | solution.py:78
  129.9 6.7 %all-to-all-done.2 = bf16[4,64,1408]{2,1,0:T(8,128)(2,1)S(1)} async-done(((bf16[4,64,1408]{2,1,0:T(8,128)(2,1)}), bf16[4,64,1408]{2,1,0:T(8,128)(2,1)S(1)}, u32[]{:S(2)}, u32[]{:S(2)}) %all-to-all-start.2) | async-done | bytes 720928 | tf_op jit(solution)/shard_map/all_to_all | solution.py:764
  138.2 5.7 all-to-all-start.3
  144.5 7.0 %attention_forward.3 = (f32[2,2,64,512]{3,2,1,0:T(8,128)}, f32[2,2,1,512]{3,2,1,0:T(1,128)}) custom-call(s32[4]{0:T(128)} %pad_add_fusion.me_ref.refs_0_, bf16[4,2,128,512]{3,2,1,0:T(8,128)(2,1)} %get-tuple-element.198.q_ref.refs_1_, bf16[2,4,128,512]{3,2,1,0:T(8,128)(2,1)} %pad_maximum_fusion.6.all_ref.refs_3_), custom_call_target="tpu_custom_call" | custom-call | flops 2147483648 | bytes 2629648 | tf_op jit(solution)/shard_map/attention_forward/pallas_call | solution.py:78
  151.5 5.4 out_products.1
  160.4 19.2 %collective-permute-done.19.rest_1_ = bf16[128,2048]{1,0:T(8,128)(2,1)} collective-permute-done((bf16[128,2048]{1,0:T(8,128)(2,1)}, bf16[128,2048]{1,0:T(8,128)(2,1)}, u32[]{:S(2)}, u32[]{:S(2)}) %collective-permute-start.19) | collective-permute-done | bytes 524320 | tf_op jit(solution)/shard_map/ppermute | solution.py:761
  179.6 33.1 %collective-permute-done.20.rest_2_ = bf16[128,2048]{1,0:T(8,128)(2,1)} collective-permute-done((bf16[128,2048]{1,0:T(8,128)(2,1)}, bf16[128,2048]{1,0:T(8,128)(2,1)}, u32[]{:S(2)}, u32[]{:S(2)}) %collective-permute-start.20) | collective-permute-done | bytes 524320 | tf_op jit(solution)/shard_map/ppermute | solution.py:761
  212.7 14.7 %collective-permute-done.21.rest_3_ = bf16[128,2048]{1,0:T(8,128)(2,1)} collective-permute-done((bf16[128,2048]{1,0:T(8,128)(2,1)}, bf16[128,2048]{1,0:T(8,128)(2,1)}, u32[]{:S(2)}, u32[]{:S(2)}) %collective-permute-start.21) | collective-permute-done | bytes 524320 | tf_op jit(solution)/shard_map/ppermute | solution.py:761
  239.9 10.1 %collective-permute-done.23 = bf16[128,2048]{1,0:T(8,128)(2,1)S(1)} collective-permute-done((bf16[128,2048]{1,0:T(8,128)(2,1)}, bf16[128,2048]{1,0:T(8,128)(2,1)S(1)}, u32[]{:S(2)}, u32[]{:S(2)}) %collective-permute-start.23) | collective-permute-done | bytes 524320 | tf_op jit(solution)/shard_map/ppermute | solution.py:761
  250.0 14.3 %collective-permute-done.24 = bf16[128,2048]{1,0:T(8,128)(2,1)S(1)} collective-permute-done((bf16[128,2048]{1,0:T(8,128)(2,1)}, bf16[128,2048]{1,0:T(8,128)(2,1)S(1)}, u32[]{:S(2)}, u32[]{:S(2)}) %collective-permute-start.24) | collective-permute-done | bytes 524320 | tf_op jit(solution)/shard_map/ppermute | solution.py:761
  264.3 10.1 %collective-permute-done.25 = bf16[128,2048]{1,0:T(8,128)(2,1)S(1)} collective-permute-done((bf16[128,2048]{1,0:T(8,128)(2,1)}, bf16[128,2048]{1,0:T(8,128)(2,1)S(1)}, u32[]{:S(2)}, u32[]{:S(2)}) %collective-permute-start.25) | collective-permute-done | bytes 524320 | tf_op jit(solution)/shard_map/ppermute | solution.py:761
  274.6 16.7 %collective-permute-done.27 = bf16[256,1408]{1,0:T(8,128)(2,1)S(1)} collective-permute-done((bf16[256,1408]{1,0:T(8,128)(2,1)S(1)}, bf16[256,1408]{1,0:T(8,128)(2,1)S(1)}, u32[]{:S(2)}, u32[]{:S(2)}) %collective-permute-start.27) | collective-permute-done | bytes 720928 | tf_op jit(solution)/shard_map/ppermute | solution.py:761
  301.8 10.8 %fusion.32 = f32[512,2816]{1,0:T(8,128)S(1)} fusion(bf16[512,2048]{1,0:T(8,128)(2,1)} %copy-done.46, bf16[2048,2816]{1,0:T(8,128)(2,1)} %all-gather.2.cloned.1.call-done), kind=kOutput, calls=%fused_computation.113 | convolution fusion | flops 5905580032 | bytes 19398656 | tf_op jit(solution)/shard_map/dot_general | solution.py:38
  316.5 6.4 convolution_convert_fusion.2
  325.3 9.2 %convolution_convert_fusion = bf16[2048,2816]{1,0:T(8,128)(2,1)} fusion(bf16[512,2048]{1,0:T(8,128)(2,1)S(1)} %copy-done.47, bf16[512,1408]{1,0:T(8,128)(2,1)S(1)} %get-tuple-element.320, bf16[512,1408]{1,0:T(8,128)(2,1)S(1)} %get-tuple-element.319), kind=kOutput, calls=%fused_computation | convolution fusion | flops 5917114368 | bytes 16515072 | tf_op jit(solution)/shard_map/dot_general | solution.py:46
  351.4 11.7 %collective-permute-done.31.rest_3_ = bf16[128,2048]{1,0:T(8,128)(2,1)S(1)} collective-permute-done((bf16[128,2048]{1,0:T(8,128)(2,1)}, bf16[128,2048]{1,0:T(8,128)(2,1)S(1)}, u32[]{:S(2)}, u32[]{:S(2)}) %collective-permute-start.31) | collective-permute-done | bytes 524320 | tf_op jit(solution)/shard_map/ppermute | solution.py:761
  374.7 22.4 %collective-permute-done.33.rest_2_ = bf16[128,2048]{1,0:T(8,128)(2,1)S(1)} collective-permute-done((bf16[128,2048]{1,0:T(8,128)(2,1)}, bf16[128,2048]{1,0:T(8,128)(2,1)S(1)}, u32[]{:S(2)}, u32[]{:S(2)}) %collective-permute-start.33) | collective-permute-done | bytes 524320 | tf_op jit(solution)/shard_map/ppermute | solution.py:761
  398.8 6.1 convert_add_fusion
  404.9 5.6 collective-permute-done.34.rest_3_
  427.5 10.0 %attention_backward.2 = (f32[2,2,64,512]{3,2,1,0:T(8,128)}, f32[4096,128]{1,0:T(8,128)}) custom-call(s32[4]{0:T(128)} %pad_add_fusion.me_ref.refs_0_, bf16[4,2,128,512]{3,2,1,0:T(8,128)(2,1)} %get-tuple-element.198.q_ref.refs_1_, bf16[4,2,128,512]{3,2,1,0:T(8,128)(2,1)} %get-tuple-element.243.refs_2_, ...), custom_call_target="tpu_custom_call" | custom-call | flops 5368709120 | bytes 5791760 | tf_op jit(solution)/shard_map/attention_backward/pallas_call | solution.py:78
  442.7 10.8 %attention_backward.3 = (f32[2,2,64,512]{3,2,1,0:T(8,128)}, f32[4,512,128]{2,1,0:T(8,128)}, bf16[4,512,128]{2,1,0:T(8,128)(2,1)}) custom-call(s32[4]{0:T(128)} %pad_add_fusion.me_ref.refs_0_, bf16[4,2,128,512]{3,2,1,0:T(8,128)(2,1)} %get-tuple-element.198.q_ref.refs_1_, bf16[4,2,128,512]{3,2,1,0:T(8,128)(2,1)} %get-tuple-element.243.refs_2_, ...), custom_call_target="tpu_custom_call" | custom-call | flops 5368709120 | bytes 7364624 | tf_op jit(solution)/shard_map/attention_backward/pallas_call | solution.py:78
  453.5 23.8 %collective-permute-done.37 = bf16[512,1408]{1,0:T(8,128)(2,1)S(1)} collective-permute-done((bf16[512,1408]{1,0:T(8,128)(2,1)S(1)}, bf16[512,1408]{1,0:T(8,128)(2,1)S(1)}, u32[]{:S(2)}, u32[]{:S(2)}) %collective-permute-start.37) | collective-permute-done | bytes 1441824 | tf_op jit(solution)/shard_map/ppermute | solution.py:761
  478.4 9.9 %collective-permute-done.38 = bf16[2,64,2048]{2,1,0:T(8,128)(2,1)} collective-permute-done((bf16[2,64,2048]{2,1,0:T(8,128)(2,1)S(1)}, bf16[2,64,2048]{2,1,0:T(8,128)(2,1)}, u32[]{:S(2)}, u32[]{:S(2)}) %collective-permute-start.38) | collective-permute-done | bytes 524320 | tf_op jit(solution)/shard_map/ppermute | solution.py:761
  519.8 6.6 %back_project.1 = (bf16[128,2048]{1,0:T(8,128)(2,1)}, bf16[128,2048]{1,0:T(8,128)(2,1)}, bf16[128,2048]{1,0:T(8,128)(2,1)}, bf16[128,2048]{1,0:T(8,128)(2,1)}, b...) custom-call(s32[16]{0:T(128)} %fusion.25.starts, bf16[512,512]{1,0:T(8,128)(2,1)} %back_query.1.d_ref.dq_ref, ...), custom_call_target="tpu_custom_call" | custom-call | flops 1342177280 | bytes 8527936 | tf_op jit(solution)/shard_map/back_project/pallas_call | solution.py:78
  541.9 23.7 %collective-permute-done.51 = bf16[256,1408]{1,0:T(8,128)(2,1)S(1)} collective-permute-done((bf16[256,1408]{1,0:T(8,128)(2,1)S(1)}, bf16[256,1408]{1,0:T(8,128)(2,1)S(1)}, u32[]{:S(2)}, u32[]{:S(2)}) %collective-permute-start.51) | collective-permute-done | bytes 720928 | tf_op jit(solution)/shard_map/ppermute | solution.py:761
  565.6 15.6 %collective-permute-done.49 = bf16[1,256,512]{2,1,0:T(8,128)(2,1)S(1)} collective-permute-done((bf16[1,256,512]{2,1,0:T(8,128)(2,1)S(1)}, bf16[1,256,512]{2,1,0:T(8,128)(2,1)S(1)}, u32[]{:S(2)}, u32[]{:S(2)}) %collective-permute-start.49) | collective-permute-done | bytes 262176 | tf_op jit(solution)/shard_map/ppermute | solution.py:761
  594.3 5.5 all-to-all-start.6
  617.6 5.7 collective-permute-done.54
  (319 shorter events, 241.6 us)
Async XLA Ops:
  19.4 30.3 %collective-permute-start = (bf16[320,640]{1,0:T(8,128)(2,1)S(1)}, bf16[320,640]{1,0:T(8,128)(2,1)S(1)}, u32[]{:S(2)}, u32[]{:S(2)}) collective-permute-start(bf16[320,640]{1,0:T(8,128)(2,1)S(1)} %bitcast.72), channel_id=1, source_target_pairs={{0,16},{1,17},{2,18},{3,19},{4,20},{5,21},{6,22},{7,23},{8,24},{9,... | collective-permute-start | bytes 1228808 | tf_op jit(solution)/shard_map/ppermute | solution.py:761
  22.7 27.0 %collective-permute-start.10 = (bf16[64,2048]{1,0:T(8,128)(2,1)}, bf16[64,2048]{1,0:T(8,128)(2,1)}, u32[]{:S(2)}, u32[]{:S(2)}) collective-permute-start(bf16[64,2048]{1,0:T(8,128)(2,1)} %param.21), channel_id=1, source_target_pairs={{0,0},{1,16},{2,2},{3,18},{4,4},{5,20},{6,6},{7,22},{8,1},{9,17},{... | collective-permute-start | bytes 786440 | tf_op jit(solution)/shard_map/ppermute | solution.py:902
  26.1 25.9 %collective-permute-start.1 = (bf16[320,640]{1,0:T(8,128)(2,1)S(1)}, bf16[320,640]{1,0:T(8,128)(2,1)S(1)}, u32[]{:S(2)}, u32[]{:S(2)}) collective-permute-start(bf16[320,640]{1,0:T(8,128)(2,1)S(1)} %bitcast.73), channel_id=1, source_target_pairs={{0,2},{1,3},{2,0},{3,1},{4,6},{5,7},{6,4},{7,5},{8,10},{9,11},{10,... | collective-permute-start | bytes 1228808 | tf_op jit(solution)/shard_map/ppermute | solution.py:761
  27.7 29.3 %collective-permute-start.7 = (bf16[128,2048]{1,0:T(8,128)(2,1)}, bf16[128,2048]{1,0:T(8,128)(2,1)S(1)}, u32[]{:S(2)}, u32[]{:S(2)}) collective-permute-start(bf16[128,2048]{1,0:T(8,128)(2,1)} %rest_0_.1), channel_id=1, source_target_pairs={{0,1},{1,0},{2,3},{3,2},{4,5},{5,4},{6,7},{7,6},{8,9},{9,8},{10,11... | collective-permute-start | bytes 1572872 | tf_op jit(solution)/shard_map/ppermute | solution.py:761
  27.7 29.3 %collective-permute-start.8 = (bf16[128,2048]{1,0:T(8,128)(2,1)}, bf16[128,2048]{1,0:T(8,128)(2,1)S(1)}, u32[]{:S(2)}, u32[]{:S(2)}) collective-permute-start(bf16[128,2048]{1,0:T(8,128)(2,1)} %rest_0_.1), channel_id=1, source_target_pairs={{0,8},{1,9},{2,10},{3,11},{4,12},{5,13},{6,14},{7,15},{8,0},{9,1},... | collective-permute-start | bytes 1572872 | tf_op jit(solution)/shard_map/ppermute | solution.py:761
  52.1 22.4 %collective-permute-start.9 = (bf16[128,2048]{1,0:T(8,128)(2,1)}, bf16[128,2048]{1,0:T(8,128)(2,1)S(1)}, u32[]{:S(2)}, u32[]{:S(2)}) collective-permute-start(bf16[128,2048]{1,0:T(8,128)(2,1)} %rest_0_.1), channel_id=1, source_target_pairs={{0,9},{1,8},{2,11},{3,10},{4,13},{5,12},{6,15},{7,14},{8,1},{9,0},... | collective-permute-start | bytes 1572872 | tf_op jit(solution)/shard_map/ppermute | solution.py:761
  82.2 26.2 %all-to-all-start.1 = ((bf16[4,64,2816]{2,1,0:T(8,128)(2,1)}), bf16[4,64,2816]{2,1,0:T(8,128)(2,1)S(1)}, u32[]{:S(2)}, u32[]{:S(2)}) async-start(bf16[4,64,2816]{2,1,0:T(8,128)(2,1)} %bitcast.10), calls=%async_computation.1 | async-start | bytes 2883584 | tf_op jit(solution)/shard_map/all_to_all | solution.py:764
  87.5 214.3 %all-gather.2.cloned.1.call-start = ((), (), s32[]{:S(2)}) async-start(), calls=%async_computation.9 | async-start | bytes 12976128 | tf_op jit(solution)/shard_map/all_gather | solution.py:933
  138.2 89.1 %all-to-all-start.3 = ((bf16[4,128,2048]{2,1,0:T(8,128)(2,1)}), bf16[4,128,2048]{2,1,0:T(8,128)(2,1)S(1)}, u32[]{:S(2)}, u32[]{:S(2)}) async-start(bf16[4,128,2048]{2,1,0:T(8,128)(2,1)} %broadcast_in_dim.2), calls=%async_computation.3 | async-start | bytes 4194304 | tf_op jit(solution)/shard_map/all_to_all | solution.py:764
  143.9 347.9 %reduce-scatter.2.cloned.1.call-start = ((), (), s32[]{:S(2)}) async-start(), calls=%async_computation.10 | async-start | bytes 12976128 | tf_op jit(solution)/shard_map/reduce_scatter | solution.py:1012
  144.4 82.9 %collective-permute-start.22 = (bf16[256,1408]{1,0:T(8,128)(2,1)S(1)}, bf16[256,1408]{1,0:T(8,128)(2,1)S(1)}, u32[]{:S(2)}, u32[]{:S(2)}) collective-permute-start(bf16[256,1408]{1,0:T(8,128)(2,1)S(1)} %bitcast.77), channel_id=1, source_target_pairs={{0,2},{1,3},{2,0},{3,1},{4,6},{5,7},{6,4},{7,5},{8,10},{9,11},{10,... | collective-permute-start | bytes 2162696 | tf_op jit(solution)/shard_map/ppermute | solution.py:761
  156.9 22.7 %collective-permute-start.19 = (bf16[128,2048]{1,0:T(8,128)(2,1)}, bf16[128,2048]{1,0:T(8,128)(2,1)}, u32[]{:S(2)}, u32[]{:S(2)}) collective-permute-start(bf16[128,2048]{1,0:T(8,128)(2,1)} %get-tuple-element.205), channel_id=1, source_target_pairs={{0,1},{1,0},{2,3},{3,2},{4,5},{5,4},{6,7},{7,6},{8,9},{9,8},{10,11... | collective-permute-start | bytes 1572872 | tf_op jit(solution)/shard_map/ppermute | solution.py:761
  158.3 54.3 %collective-permute-start.20 = (bf16[128,2048]{1,0:T(8,128)(2,1)}, bf16[128,2048]{1,0:T(8,128)(2,1)}, u32[]{:S(2)}, u32[]{:S(2)}) collective-permute-start(bf16[128,2048]{1,0:T(8,128)(2,1)} %get-tuple-element.206), channel_id=1, source_target_pairs={{0,8},{1,9},{2,10},{3,11},{4,12},{5,13},{6,14},{7,15},{8,0},{9,1},... | collective-permute-start | bytes 1572872 | tf_op jit(solution)/shard_map/ppermute | solution.py:761
  158.9 68.4 %collective-permute-start.21 = (bf16[128,2048]{1,0:T(8,128)(2,1)}, bf16[128,2048]{1,0:T(8,128)(2,1)}, u32[]{:S(2)}, u32[]{:S(2)}) collective-permute-start(bf16[128,2048]{1,0:T(8,128)(2,1)} %get-tuple-element.207), channel_id=1, source_target_pairs={{0,9},{1,8},{2,11},{3,10},{4,13},{5,12},{6,15},{7,14},{8,1},{9,0},... | collective-permute-start | bytes 1572872 | tf_op jit(solution)/shard_map/ppermute | solution.py:761
  227.3 47.0 %collective-permute-start.26 = (bf16[256,1408]{1,0:T(8,128)(2,1)S(1)}, bf16[256,1408]{1,0:T(8,128)(2,1)S(1)}, u32[]{:S(2)}, u32[]{:S(2)}) collective-permute-start(bf16[256,1408]{1,0:T(8,128)(2,1)S(1)} %bitcast.78), channel_id=1, source_target_pairs={{0,16},{1,17},{2,18},{3,19},{4,20},{5,21},{6,22},{7,23},{8,24},{9,... | collective-permute-start | bytes 2162696 | tf_op jit(solution)/shard_map/ppermute | solution.py:761
  236.4 27.8 %collective-permute-start.24 = (bf16[128,2048]{1,0:T(8,128)(2,1)}, bf16[128,2048]{1,0:T(8,128)(2,1)S(1)}, u32[]{:S(2)}, u32[]{:S(2)}) collective-permute-start(bf16[128,2048]{1,0:T(8,128)(2,1)} %get-tuple-element.222), channel_id=1, source_target_pairs={{0,8},{1,9},{2,10},{3,11},{4,12},{5,13},{6,14},{7,15},{8,0},{9,1},... | collective-permute-start | bytes 1572872 | tf_op jit(solution)/shard_map/ppermute | solution.py:761
  236.4 37.9 %collective-permute-start.25 = (bf16[128,2048]{1,0:T(8,128)(2,1)}, bf16[128,2048]{1,0:T(8,128)(2,1)S(1)}, u32[]{:S(2)}, u32[]{:S(2)}) collective-permute-start(bf16[128,2048]{1,0:T(8,128)(2,1)} %get-tuple-element.222), channel_id=1, source_target_pairs={{0,9},{1,8},{2,11},{3,10},{4,13},{5,12},{6,15},{7,14},{8,1},{9,0},... | collective-permute-start | bytes 1572872 | tf_op jit(solution)/shard_map/ppermute | solution.py:761
  338.4 24.7 %collective-permute-start.31 = (bf16[128,2048]{1,0:T(8,128)(2,1)}, bf16[128,2048]{1,0:T(8,128)(2,1)S(1)}, u32[]{:S(2)}, u32[]{:S(2)}) collective-permute-start(bf16[128,2048]{1,0:T(8,128)(2,1)} %get-tuple-element.326), channel_id=1, source_target_pairs={{0,9},{1,8},{2,11},{3,10},{4,13},{5,12},{6,15},{7,14},{8,1},{9,0},... | collective-permute-start | bytes 1572872 | tf_op jit(solution)/shard_map/ppermute | solution.py:761
  366.5 32.3 %collective-permute-start.35 = (bf16[1024,1408]{1,0:T(8,128)(2,1)}, bf16[1024,1408]{1,0:T(8,128)(2,1)}, u32[]{:S(2)}, u32[]{:S(2)}) collective-permute-start(bf16[1024,1408]{1,0:T(8,128)(2,1)} %convolution_convert_fusion.1), channel_id=1, source_target_pairs={{0,4},{1,5},{2,6},{3,7},{4,0},{5,1},{6,2},{7,3},{8,12},{9,13},{10,... | collective-permute-start | bytes 8650760 | tf_op jit(solution)/shard_map/ppermute | solution.py:761
  370.8 34.1 %collective-permute-start.32 = (bf16[128,2048]{1,0:T(8,128)(2,1)}, bf16[128,2048]{1,0:T(8,128)(2,1)S(1)}, u32[]{:S(2)}, u32[]{:S(2)}) collective-permute-start(bf16[128,2048]{1,0:T(8,128)(2,1)} %get-tuple-element.249.rest_0_), channel_id=1, source_target_pairs={{0,1},{1,0},{2,3},{3,2},{4,5},{5,4},{6,7},{7,6},{8,9},{9,8},{10,11... | collective-permute-start | bytes 1572872 | tf_op jit(solution)/shard_map/ppermute | solution.py:761
  371.2 26.0 %collective-permute-start.33 = (bf16[128,2048]{1,0:T(8,128)(2,1)}, bf16[128,2048]{1,0:T(8,128)(2,1)S(1)}, u32[]{:S(2)}, u32[]{:S(2)}) collective-permute-start(bf16[128,2048]{1,0:T(8,128)(2,1)} %get-tuple-element.249.rest_0_), channel_id=1, source_target_pairs={{0,8},{1,9},{2,10},{3,11},{4,12},{5,13},{6,14},{7,15},{8,0},{9,1},... | collective-permute-start | bytes 1572872 | tf_op jit(solution)/shard_map/ppermute | solution.py:761
  416.2 72.0 %all-to-all-start.4 = ((bf16[4,128,2048]{2,1,0:T(8,128)(2,1)}), bf16[4,128,2048]{2,1,0:T(8,128)(2,1)S(1)}, u32[]{:S(2)}, u32[]{:S(2)}) async-start(bf16[4,128,2048]{2,1,0:T(8,128)(2,1)} %bitcast.68), calls=%async_computation.4 | async-start | bytes 4194304 | tf_op jit(solution)/shard_map/all_to_all | solution.py:764
  427.4 49.9 %collective-permute-start.37 = (bf16[512,1408]{1,0:T(8,128)(2,1)S(1)}, bf16[512,1408]{1,0:T(8,128)(2,1)S(1)}, u32[]{:S(2)}, u32[]{:S(2)}) collective-permute-start(bf16[512,1408]{1,0:T(8,128)(2,1)S(1)} %slice.228), channel_id=1, source_target_pairs={{0,2},{1,3},{2,0},{3,1},{4,6},{5,7},{6,4},{7,5},{8,10},{9,11},{10,... | collective-permute-start | bytes 4325384 | tf_op jit(solution)/shard_map/ppermute | solution.py:761
  440.6 47.7 %collective-permute-start.38 = (bf16[2,64,2048]{2,1,0:T(8,128)(2,1)S(1)}, bf16[2,64,2048]{2,1,0:T(8,128)(2,1)}, u32[]{:S(2)}, u32[]{:S(2)}) collective-permute-start(bf16[2,64,2048]{2,1,0:T(8,128)(2,1)S(1)} %slice.231), channel_id=1, source_target_pairs={{0,2},{1,3},{2,0},{3,1},{4,6},{5,7},{6,4},{7,5},{8,10},{9,11},{10,... | collective-permute-start | bytes 1572872 | tf_op jit(solution)/shard_map/ppermute | solution.py:761
  506.1 88.2 %all-to-all-start.5 = ((bf16[4,64,2816]{2,1,0:T(8,128)(2,1)}), bf16[4,64,2816]{2,1,0:T(8,128)(2,1)S(1)}, u32[]{:S(2)}, u32[]{:S(2)}) async-start(bf16[4,64,2816]{2,1,0:T(8,128)(2,1)} %bitcast.82), calls=%async_computation.6 | async-start | bytes 2883584 | tf_op jit(solution)/shard_map/all_to_all | solution.py:764
  515.8 22.6 %collective-permute-start.50 = (bf16[1,64,2048]{2,1,0:T(8,128)(2,1)S(1)}, bf16[1,64,2048]{2,1,0:T(8,128)(2,1)}, u32[]{:S(2)}, u32[]{:S(2)}) collective-permute-start(bf16[1,64,2048]{2,1,0:T(8,128)(2,1)S(1)} %slice.232), channel_id=1, source_target_pairs={{0,16},{1,17},{2,18},{3,19},{4,20},{5,21},{6,22},{7,23},{8,24},{9,... | collective-permute-start | bytes 786440 | tf_op jit(solution)/shard_map/ppermute | solution.py:761
  532.3 33.3 %collective-permute-start.51 = (bf16[256,1408]{1,0:T(8,128)(2,1)S(1)}, bf16[256,1408]{1,0:T(8,128)(2,1)S(1)}, u32[]{:S(2)}, u32[]{:S(2)}) collective-permute-start(bf16[256,1408]{1,0:T(8,128)(2,1)S(1)} %slice.229), channel_id=1, source_target_pairs={{0,16},{1,17},{2,18},{3,19},{4,20},{5,21},{6,22},{7,23},{8,24},{9,... | collective-permute-start | bytes 2162696 | tf_op jit(solution)/shard_map/ppermute | solution.py:761
  536.4 44.8 %collective-permute-start.45 = (bf16[128,2048]{1,0:T(8,128)(2,1)S(1)}, bf16[128,2048]{1,0:T(8,128)(2,1)S(1)}, u32[]{:S(2)}, u32[]{:S(2)}) collective-permute-start(bf16[128,2048]{1,0:T(8,128)(2,1)S(1)} %copy-done.55), channel_id=1, source_target_pairs={{0,1},{1,0},{2,3},{3,2},{4,5},{5,4},{6,7},{7,6},{8,9},{9,8},{10,11... | collective-permute-start | bytes 1572872 | tf_op jit(solution)/shard_map/ppermute | solution.py:761
  538.4 42.8 %collective-permute-start.46 = (bf16[128,2048]{1,0:T(8,128)(2,1)S(1)}, bf16[128,2048]{1,0:T(8,128)(2,1)S(1)}, u32[]{:S(2)}, u32[]{:S(2)}) collective-permute-start(bf16[128,2048]{1,0:T(8,128)(2,1)S(1)} %copy-done.54), channel_id=1, source_target_pairs={{0,8},{1,9},{2,10},{3,11},{4,12},{5,13},{6,14},{7,15},{8,0},{9,1},... | collective-permute-start | bytes 1572872 | tf_op jit(solution)/shard_map/ppermute | solution.py:761
  538.4 42.8 %collective-permute-start.47 = (bf16[128,2048]{1,0:T(8,128)(2,1)S(1)}, bf16[128,2048]{1,0:T(8,128)(2,1)S(1)}, u32[]{:S(2)}, u32[]{:S(2)}) collective-permute-start(bf16[128,2048]{1,0:T(8,128)(2,1)S(1)} %copy-done.53), channel_id=1, source_target_pairs={{0,9},{1,8},{2,11},{3,10},{4,13},{5,12},{6,15},{7,14},{8,1},{9,0},... | collective-permute-start | bytes 1572872 | tf_op jit(solution)/shard_map/ppermute | solution.py:761
  541.1 40.0 %collective-permute-start.49 = (bf16[1,256,512]{2,1,0:T(8,128)(2,1)S(1)}, bf16[1,256,512]{2,1,0:T(8,128)(2,1)S(1)}, u32[]{:S(2)}, u32[]{:S(2)}) collective-permute-start(bf16[1,256,512]{2,1,0:T(8,128)(2,1)S(1)} %slice.233), channel_id=1, source_target_pairs={{0,16},{1,17},{2,18},{3,19},{4,20},{5,21},{6,22},{7,23},{8,24},{9,... | collective-permute-start | bytes 786440 | tf_op jit(solution)/shard_map/ppermute | solution.py:761
  603.4 24.5 %all-to-all-start.7 = ((bf16[4,64,1920]{2,1,0:T(8,128)(2,1)}), bf16[4,64,1920]{2,1,0:T(8,128)(2,1)S(1)}, u32[]{:S(2)}, u32[]{:S(2)}) async-start(bf16[4,64,1920]{2,1,0:T(8,128)(2,1)} %bitcast.34), calls=%async_computation.8 | async-start | bytes 1966080 | tf_op jit(solution)/shard_map/all_to_all | solution.py:764
  (95 other events, 971.4 us)
Sparse Core Ops, SparseCore 0:
  109.7 115.1 all-gather.1
  334.6 134.3 reduce-scatter.1

commit v4 on v3

--- a/solution.py
+++ b/solution.py
@@ -1045,20 +1045,14 @@
         down_near = down_near[:half].astype(f32)
         if bit != near[0]:
             down_near = down_near + down_got.astype(f32)
-    out_pair = out_grads(out_places, attn_t, hold(d_branch, d_heads), slab)
-    out_sum = core_sum(out_pair)
     dq0, dkv = backward(0, None)
-    dkv, out_sum = lax.optimization_barrier((dkv, out_sum))
-    out_keep, out_got = send(out_sum, near)
     dq1, own, other = backward(1, dkv)
-    other, down_got, block_parts, out_got = lax.optimization_barrier(
-        (other, down_got, block_parts, out_got)
-    )
+    other, down_got, block_parts = lax.optimization_barrier((other, down_got, block_parts))
     kv_sums = own + swap(other, core).astype(f32)
     kv_sends = [kv_sums[i].astype(bf16) for i in range(len(chips))]
     kv_parts = [swap(kv_sends[i], m) for i, m in enumerate(chips) if m]
-    dq0, dq1, block_parts, down_got, out_got, pair_total = hold(
-        (dq0, dq1, block_parts, down_got, out_got, pair_total), kv_sends
+    dq0, dq1, block_parts, down_got, pair_total = hold(
+        (dq0, dq1, block_parts, down_got, pair_total), kv_sends
     )
     d_query = back_query(dq0, dq1, cosine, sine, rows)
     if aligned:
@@ -1079,12 +1073,13 @@
     for part in kv_parts:
         kv_sum = kv_sum + part.astype(f32)
     query_keep, query_got = send(query_sum, near)
-    out_keep, out_got = send(out_keep + out_got.astype(f32), far)
     *d_hattn_blocks, d_kv, gain_attn_part = back_project(
         starts, d_query, kv_sum, cosine, sine, toks, qkv_k
     )
-    d_hattn_blocks, query_got = lax.optimization_barrier((d_hattn_blocks, query_got))
-    query_keep, query_got = send(query_keep + query_got.astype(f32), far)
+    d_hattn_blocks, query_got, pair_parts = lax.optimization_barrier(
+        (d_hattn_blocks, query_got, pair_parts)
+    )
+    query_near = query_keep + query_got.astype(f32)
     d_hattn_parts = scatter_t(d_hattn_blocks)
     d_kv, gain_attn_part = hold((d_kv, gain_attn_part), d_hattn_blocks)
     if aligned:
@@ -1102,7 +1097,11 @@
     key_sum = core_sum((own, other))
     after = d_hattn_parts[1:]
     grad_gate, grad_up = unpack_columns(pair_parts, 2, "unpack_gate_up")
-    key_sum, query_got, out_got, down_got = hold((key_sum, query_got, out_got, down_got), after)
+    out_pair = out_grads(out_places, attn_t, hold(d_branch, d_hattn_blocks), slab)
+    out_near = sum_over(core_sum(out_pair), near)
+    key_sum, query_near, down_got, out_near = hold((key_sum, query_near, down_got, out_near), after)
+    query_keep, query_got = send(query_near, far)
+    out_keep, out_got = send(out_near, far)
     d_hattn_parts, grad_gate, grad_up = lax.optimization_barrier((d_hattn_parts, grad_gate, grad_up))
     query_total = query_keep + query_got.astype(f32)
     out_total = (out_keep + out_got.astype(f32)).astype(bf16).reshape(slab, width)

time: 649 us -> 650 us (level)
    unnamed x133 -> x135, local copies, waits for them, and re-layouts: 15.8 us -> 10.4 us
  transfers between devices with their start and end apart: 65 -> 65, of which waited for: 31 -> 35; matrix products, arithmetic and copies ran while one was open for 9% -> 9% of each run, Pallas kernels for 13% -> 13%
where the time goes in v4:
time: 650 us; the launch traced here: 639 us
  waiting for transfers between devices  322 us (50%)
  starting transfers between devices  105 us (16%)
  Pallas kernels  100 us (15%)
  matrix products  49.2 us (8%)
  other arithmetic  25.8 us (4%)
  local copies, waits for them, and re-layouts  21.4 us (3%)
  between operations  15.5 us (2%)
    ppermute x53, waiting for transfers between devices, swap(): return lax.ppermute(value, AXES, [(i, i ^ mask) for i in range(n)])  279 us
    pallas_call x22, Pallas kernels, call(): pl.pallas_call(kernel, out_shape=out_shape, in_specs=specs, out_specs=(VM...  100 us
    ppermute x53, starting transfers between devices, swap(): return lax.ppermute(value, AXES, [(i, i ^ mask) for i in range(n)])  60.8 us
    all_to_all x8, starting transfers between devices, trade(): lax.all_to_all(value, AXES, split_axis=0, concat_axis=0, tiled=True, axis...  39.1 us
    ppermute x1, waiting for transfers between devices, on_device(): lax.ppermute(hold(w_out, qkv_shard), AXES, [(i, goes_to(i)) for i in rang...  20.9 us
    dot_general x3, matrix products, dot_first(): lax.dot_general(a, b, (((0,), (0,)), ((), ())), preferred_element_type=f32)  18.7 us
    dot_general x3, matrix products, dot(): lax.dot_general(a, b, (((1,), (0,)), ((), ())), preferred_element_type=f32)  18.1 us
    all_to_all x8, waiting for transfers between devices, trade(): lax.all_to_all(value, AXES, split_axis=0, concat_axis=0, tiled=True, axis...  14.2 us
  transfers between devices with their start and end apart: 65, of which 35 were waited for; matrix products, arithmetic and copies ran while one was open for 9% of the time, Pallas kernels for 13%

profile of v4, /device:TPU:8, one launch (start us, length us, event | category | flops | bytes accessed | tf_op | source)
XLA Modules:
  0.0 639.5 jit_solution(13908493847190675974)
XLA Ops:
  13.2 6.2 all-to-all-done
  28.7 20.9 %collective-permute-done.10 = bf16[64,2048]{1,0:T(8,128)(2,1)S(1)} collective-permute-done((bf16[64,2048]{1,0:T(8,128)(2,1)}, bf16[64,2048]{1,0:T(8,128)(2,1)S(1)}, u32[]{:S(2)}, u32[]{:S(2)}) %collective-permute-start.10) | collective-permute-done | bytes 262176 | tf_op jit(solution)/shard_map/ppermute | solution.py:902
  75.3 6.6 %project.1 = (bf16[512,2048]{1,0:T(8,128)(2,1)}, bf16[4,2,128,512]{3,2,1,0:T(8,128)(2,1)}, bf16[128,512]{1,0:T(8,128)(2,1)}, f32[8,2048]{1,0:T(8,128)}) custom-call(s32[16]{0:T(128)} %fusion.23.starts, f32[32,512]{1,0:T(8,128)} %get-tuple-element.336.cos_ref, f32[32,512]{1,0:T(8,128)} %get-tuple-element.335.sin_ref, bf16[128,2048]{1,0:T(8,128)(2,1)} %rest_0_.1, ...), custom_call_target="tpu_custom_call" | custom-call | flops 1342177280 | bytes 8847424 | tf_op jit(solution)/shard_map/project/pallas_call | solution.py:78
  92.0 14.5 %collective-permute-done.13 = bf16[128,512]{1,0:T(8,128)(2,1)S(1)} collective-permute-done((bf16[128,512]{1,0:T(8,128)(2,1)S(1)}, bf16[128,512]{1,0:T(8,128)(2,1)S(1)}, u32[]{:S(2)}, u32[]{:S(2)}) %collective-permute-start.13) | collective-permute-done | bytes 131104 | tf_op jit(solution)/shard_map/ppermute | solution.py:761
  122.5 6.8 %attention_forward.2 = (f32[2,2,64,512]{3,2,1,0:T(8,128)}, f32[2,2,1,512]{3,2,1,0:T(1,128)}) custom-call(s32[4]{0:T(128)} %pad_add_fusion.me_ref.refs_0_, bf16[4,2,128,512]{3,2,1,0:T(8,128)(2,1)} %get-tuple-element.195.q_ref.refs_1_, bf16[2,4,128,512]{3,2,1,0:T(8,128)(2,1)} %pad_maximum_fusion.6.all_ref.refs_3_), custom_call_target="tpu_custom_call" | custom-call | flops 2147483648 | bytes 2629648 | tf_op jit(solution)/shard_map/attention_forward/pallas_call | solution.py:78
  129.3 6.6 %all-to-all-done.2 = bf16[4,64,1408]{2,1,0:T(8,128)(2,1)S(1)} async-done(((bf16[4,64,1408]{2,1,0:T(8,128)(2,1)}), bf16[4,64,1408]{2,1,0:T(8,128)(2,1)S(1)}, u32[]{:S(2)}, u32[]{:S(2)}) %all-to-all-start.2) | async-done | bytes 720928 | tf_op jit(solution)/shard_map/all_to_all | solution.py:764
  143.1 6.9 %attention_forward.3 = (f32[2,2,64,512]{3,2,1,0:T(8,128)}, f32[2,2,1,512]{3,2,1,0:T(1,128)}) custom-call(s32[4]{0:T(128)} %pad_add_fusion.me_ref.refs_0_, bf16[4,2,128,512]{3,2,1,0:T(8,128)(2,1)} %get-tuple-element.195.q_ref.refs_1_, bf16[2,4,128,512]{3,2,1,0:T(8,128)(2,1)} %pad_maximum_fusion.6.all_ref.refs_3_), custom_call_target="tpu_custom_call" | custom-call | flops 2147483648 | bytes 2629648 | tf_op jit(solution)/shard_map/attention_forward/pallas_call | solution.py:78
  150.0 5.4 out_products.1
  158.9 18.8 %collective-permute-done.19.rest_1_ = bf16[128,2048]{1,0:T(8,128)(2,1)} collective-permute-done((bf16[128,2048]{1,0:T(8,128)(2,1)}, bf16[128,2048]{1,0:T(8,128)(2,1)}, u32[]{:S(2)}, u32[]{:S(2)}) %collective-permute-start.19) | collective-permute-done | bytes 524320 | tf_op jit(solution)/shard_map/ppermute | solution.py:761
  177.7 34.5 %collective-permute-done.20.rest_2_ = bf16[128,2048]{1,0:T(8,128)(2,1)} collective-permute-done((bf16[128,2048]{1,0:T(8,128)(2,1)}, bf16[128,2048]{1,0:T(8,128)(2,1)}, u32[]{:S(2)}, u32[]{:S(2)}) %collective-permute-start.20) | collective-permute-done | bytes 524320 | tf_op jit(solution)/shard_map/ppermute | solution.py:761
  212.1 13.7 %collective-permute-done.21.rest_3_ = bf16[128,2048]{1,0:T(8,128)(2,1)} collective-permute-done((bf16[128,2048]{1,0:T(8,128)(2,1)}, bf16[128,2048]{1,0:T(8,128)(2,1)}, u32[]{:S(2)}, u32[]{:S(2)}) %collective-permute-start.21) | collective-permute-done | bytes 524320 | tf_op jit(solution)/shard_map/ppermute | solution.py:761
  239.0 10.1 %collective-permute-done.23 = bf16[128,2048]{1,0:T(8,128)(2,1)S(1)} collective-permute-done((bf16[128,2048]{1,0:T(8,128)(2,1)}, bf16[128,2048]{1,0:T(8,128)(2,1)S(1)}, u32[]{:S(2)}, u32[]{:S(2)}) %collective-permute-start.23) | collective-permute-done | bytes 524320 | tf_op jit(solution)/shard_map/ppermute | solution.py:761
  249.1 12.5 %collective-permute-done.24 = bf16[128,2048]{1,0:T(8,128)(2,1)S(1)} collective-permute-done((bf16[128,2048]{1,0:T(8,128)(2,1)}, bf16[128,2048]{1,0:T(8,128)(2,1)S(1)}, u32[]{:S(2)}, u32[]{:S(2)}) %collective-permute-start.24) | collective-permute-done | bytes 524320 | tf_op jit(solution)/shard_map/ppermute | solution.py:761
  261.6 10.3 %collective-permute-done.25 = bf16[128,2048]{1,0:T(8,128)(2,1)S(1)} collective-permute-done((bf16[128,2048]{1,0:T(8,128)(2,1)}, bf16[128,2048]{1,0:T(8,128)(2,1)S(1)}, u32[]{:S(2)}, u32[]{:S(2)}) %collective-permute-start.25) | collective-permute-done | bytes 524320 | tf_op jit(solution)/shard_map/ppermute | solution.py:761
  272.7 16.4 %collective-permute-done.27 = bf16[256,1408]{1,0:T(8,128)(2,1)S(1)} collective-permute-done((bf16[256,1408]{1,0:T(8,128)(2,1)S(1)}, bf16[256,1408]{1,0:T(8,128)(2,1)S(1)}, u32[]{:S(2)}, u32[]{:S(2)}) %collective-permute-start.27) | collective-permute-done | bytes 720928 | tf_op jit(solution)/shard_map/ppermute | solution.py:761
  299.6 10.8 %fusion.30 = f32[512,2816]{1,0:T(8,128)S(1)} fusion(bf16[512,2048]{1,0:T(8,128)(2,1)} %copy-done.49, bf16[2048,2816]{1,0:T(8,128)(2,1)} %all-gather.2.cloned.1.call-done), kind=kOutput, calls=%fused_computation.111 | convolution fusion | flops 5905580032 | bytes 19398656 | tf_op jit(solution)/shard_map/dot_general | solution.py:38
  314.3 6.4 %convolution_convert_fusion.2 = bf16[512,2048]{1,0:T(8,128)(2,1)S(1)} fusion(bf16[2048,2816]{1,0:T(8,128)(2,1)S(1)} %bitcast.94, bf16[512,1408]{1,0:T(8,128)(2,1)S(1)} %get-tuple-element.314, bf16[512,1408]{1,0:T(8,128)(2,1)S(1)} %get-tuple-element.313), kind=kOutput, calls=%fused_computation.4 | convolution fusion | flops 5912395776 | bytes 16515072 | tf_op jit(solution)/shard_map/dot_general | solution.py:42
  323.0 9.1 %convolution_convert_fusion = bf16[2048,2816]{1,0:T(8,128)(2,1)} fusion(bf16[512,2048]{1,0:T(8,128)(2,1)S(1)} %copy-done.50, bf16[512,1408]{1,0:T(8,128)(2,1)S(1)} %get-tuple-element.314, bf16[512,1408]{1,0:T(8,128)(2,1)S(1)} %get-tuple-element.313), kind=kOutput, calls=%fused_computation | convolution fusion | flops 5917114368 | bytes 16515072 | tf_op jit(solution)/shard_map/dot_general | solution.py:46
  349.2 11.7 %collective-permute-done.31.rest_3_ = bf16[128,2048]{1,0:T(8,128)(2,1)S(1)} collective-permute-done((bf16[128,2048]{1,0:T(8,128)(2,1)}, bf16[128,2048]{1,0:T(8,128)(2,1)S(1)}, u32[]{:S(2)}, u32[]{:S(2)}) %collective-permute-start.31) | collective-permute-done | bytes 524320 | tf_op jit(solution)/shard_map/ppermute | solution.py:761
  372.6 22.6 %collective-permute-done.33.rest_2_ = bf16[128,2048]{1,0:T(8,128)(2,1)S(1)} collective-permute-done((bf16[128,2048]{1,0:T(8,128)(2,1)}, bf16[128,2048]{1,0:T(8,128)(2,1)S(1)}, u32[]{:S(2)}, u32[]{:S(2)}) %collective-permute-start.33) | collective-permute-done | bytes 524320 | tf_op jit(solution)/shard_map/ppermute | solution.py:761
  396.7 6.2 convert_add_fusion
  402.9 5.4 collective-permute-done.34.rest_3_
  421.9 10.1 %attention_backward.2 = (f32[2,2,64,512]{3,2,1,0:T(8,128)}, f32[4096,128]{1,0:T(8,128)}) custom-call(s32[4]{0:T(128)} %pad_add_fusion.me_ref.refs_0_, bf16[4,2,128,512]{3,2,1,0:T(8,128)(2,1)} %get-tuple-element.195.q_ref.refs_1_, bf16[4,2,128,512]{3,2,1,0:T(8,128)(2,1)} %get-tuple-element.240.refs_2_, ...), custom_call_target="tpu_custom_call" | custom-call | flops 5368709120 | bytes 5791760 | tf_op jit(solution)/shard_map/attention_backward/pallas_call | solution.py:78
  432.0 11.2 %attention_backward.3 = (f32[2,2,64,512]{3,2,1,0:T(8,128)}, f32[4,512,128]{2,1,0:T(8,128)}, bf16[4,512,128]{2,1,0:T(8,128)(2,1)}) custom-call(s32[4]{0:T(128)} %pad_add_fusion.me_ref.refs_0_, bf16[4,2,128,512]{3,2,1,0:T(8,128)(2,1)} %get-tuple-element.195.q_ref.refs_1_, bf16[4,2,128,512]{3,2,1,0:T(8,128)(2,1)} %get-tuple-element.240.refs_2_, ...), custom_call_target="tpu_custom_call" | custom-call | flops 5368709120 | bytes 7364624 | tf_op jit(solution)/shard_map/attention_backward/pallas_call | solution.py:78
  443.3 24.1 %collective-permute-done.36 = bf16[512,1408]{1,0:T(8,128)(2,1)} collective-permute-done((bf16[512,1408]{1,0:T(8,128)(2,1)S(1)}, bf16[512,1408]{1,0:T(8,128)(2,1)}, u32[]{:S(2)}, u32[]{:S(2)}) %collective-permute-start.36) | collective-permute-done | bytes 1441824 | tf_op jit(solution)/shard_map/ppermute | solution.py:761
  492.5 8.5 %collective-permute-done.38 = bf16[512,128]{1,0:T(8,128)(2,1)S(1)} collective-permute-done((bf16[512,128]{1,0:T(8,128)(2,1)S(1)}, bf16[512,128]{1,0:T(8,128)(2,1)S(1)}, u32[]{:S(2)}, u32[]{:S(2)}) %collective-permute-start.38) | collective-permute-done | bytes 131104 | tf_op jit(solution)/shard_map/ppermute | solution.py:761
  506.2 6.6 %back_project.1 = (bf16[128,2048]{1,0:T(8,128)(2,1)}, bf16[128,2048]{1,0:T(8,128)(2,1)}, bf16[128,2048]{1,0:T(8,128)(2,1)}, bf16[128,2048]{1,0:T(8,128)(2,1)}, b...) custom-call(s32[16]{0:T(128)} %fusion.23.starts, bf16[512,512]{1,0:T(8,128)(2,1)} %back_query.1.d_ref.dq_ref, ...), custom_call_target="tpu_custom_call" | custom-call | flops 1342177280 | bytes 8527936 | tf_op jit(solution)/shard_map/back_project/pallas_call | solution.py:78
  541.2 17.8 %collective-permute-done.45 = bf16[128,2048]{1,0:T(8,128)(2,1)S(1)} collective-permute-done((bf16[128,2048]{1,0:T(8,128)(2,1)}, bf16[128,2048]{1,0:T(8,128)(2,1)S(1)}, u32[]{:S(2)}, u32[]{:S(2)}) %collective-permute-start.45) | collective-permute-done | bytes 524320 | tf_op jit(solution)/shard_map/ppermute | solution.py:761
  559.2 10.8 %collective-permute-done.47 = bf16[256,1408]{1,0:T(8,128)(2,1)S(1)} collective-permute-done((bf16[256,1408]{1,0:T(8,128)(2,1)S(1)}, bf16[256,1408]{1,0:T(8,128)(2,1)S(1)}, u32[]{:S(2)}, u32[]{:S(2)}) %collective-permute-start.47) | collective-permute-done | bytes 720928 | tf_op jit(solution)/shard_map/ppermute | solution.py:761
  580.4 15.0 %collective-permute-done.51 = bf16[1,320,128]{2,1,0:T(8,128)(2,1)S(1)} collective-permute-done((bf16[1,320,128]{2,1,0:T(8,128)(2,1)S(1)}, bf16[1,320,128]{2,1,0:T(8,128)(2,1)S(1)}, u32[]{:S(2)}, u32[]{:S(2)}) %collective-permute-start.51) | collective-permute-done | bytes 81952 | tf_op jit(solution)/shard_map/ppermute | solution.py:761
  596.1 6.2 all-to-all-start.6
  619.6 8.2 %collective-permute-done.54 = bf16[64,2048]{1,0:T(8,128)(2,1)S(1)} collective-permute-done((bf16[64,2048]{1,0:T(8,128)(2,1)S(1)}, bf16[64,2048]{1,0:T(8,128)(2,1)S(1)}, u32[]{:S(2)}, u32[]{:S(2)}) %collective-permute-start.54) | collective-permute-done | bytes 262176 | tf_op jit(solution)/shard_map/ppermute | solution.py:1110
  (321 shorter events, 243.0 us)
Async XLA Ops:
  19.4 30.2 %collective-permute-start = (bf16[320,640]{1,0:T(8,128)(2,1)S(1)}, bf16[320,640]{1,0:T(8,128)(2,1)S(1)}, u32[]{:S(2)}, u32[]{:S(2)}) collective-permute-start(bf16[320,640]{1,0:T(8,128)(2,1)S(1)} %bitcast.72), channel_id=1, source_target_pairs={{0,16},{1,17},{2,18},{3,19},{4,20},{5,21},{6,22},{7,23},{8,24},{9,... | collective-permute-start | bytes 1228808 | tf_op jit(solution)/shard_map/ppermute | solution.py:761
  22.7 26.9 %collective-permute-start.10 = (bf16[64,2048]{1,0:T(8,128)(2,1)}, bf16[64,2048]{1,0:T(8,128)(2,1)S(1)}, u32[]{:S(2)}, u32[]{:S(2)}) collective-permute-start(bf16[64,2048]{1,0:T(8,128)(2,1)} %param.21), channel_id=1, source_target_pairs={{0,0},{1,16},{2,2},{3,18},{4,4},{5,20},{6,6},{7,22},{8,1},{9,17},{... | collective-permute-start | bytes 786440 | tf_op jit(solution)/shard_map/ppermute | solution.py:902
  26.1 25.8 %collective-permute-start.1 = (bf16[320,640]{1,0:T(8,128)(2,1)S(1)}, bf16[320,640]{1,0:T(8,128)(2,1)S(1)}, u32[]{:S(2)}, u32[]{:S(2)}) collective-permute-start(bf16[320,640]{1,0:T(8,128)(2,1)S(1)} %bitcast.73), channel_id=1, source_target_pairs={{0,2},{1,3},{2,0},{3,1},{4,6},{5,7},{6,4},{7,5},{8,10},{9,11},{10,... | collective-permute-start | bytes 1228808 | tf_op jit(solution)/shard_map/ppermute | solution.py:761
  27.7 29.2 %collective-permute-start.7 = (bf16[128,2048]{1,0:T(8,128)(2,1)}, bf16[128,2048]{1,0:T(8,128)(2,1)S(1)}, u32[]{:S(2)}, u32[]{:S(2)}) collective-permute-start(bf16[128,2048]{1,0:T(8,128)(2,1)} %rest_0_.1), channel_id=1, source_target_pairs={{0,1},{1,0},{2,3},{3,2},{4,5},{5,4},{6,7},{7,6},{8,9},{9,8},{10,11... | collective-permute-start | bytes 1572872 | tf_op jit(solution)/shard_map/ppermute | solution.py:761
  27.7 29.2 %collective-permute-start.8 = (bf16[128,2048]{1,0:T(8,128)(2,1)}, bf16[128,2048]{1,0:T(8,128)(2,1)S(1)}, u32[]{:S(2)}, u32[]{:S(2)}) collective-permute-start(bf16[128,2048]{1,0:T(8,128)(2,1)} %rest_0_.1), channel_id=1, source_target_pairs={{0,8},{1,9},{2,10},{3,11},{4,12},{5,13},{6,14},{7,15},{8,0},{9,1},... | collective-permute-start | bytes 1572872 | tf_op jit(solution)/shard_map/ppermute | solution.py:761
  52.0 22.2 %collective-permute-start.9 = (bf16[128,2048]{1,0:T(8,128)(2,1)}, bf16[128,2048]{1,0:T(8,128)(2,1)S(1)}, u32[]{:S(2)}, u32[]{:S(2)}) collective-permute-start(bf16[128,2048]{1,0:T(8,128)(2,1)} %rest_0_.1), channel_id=1, source_target_pairs={{0,9},{1,8},{2,11},{3,10},{4,13},{5,12},{6,15},{7,14},{8,1},{9,0},... | collective-permute-start | bytes 1572872 | tf_op jit(solution)/shard_map/ppermute | solution.py:761
  81.9 26.0 %all-to-all-start.1 = ((bf16[4,64,2816]{2,1,0:T(8,128)(2,1)}), bf16[4,64,2816]{2,1,0:T(8,128)(2,1)S(1)}, u32[]{:S(2)}, u32[]{:S(2)}) async-start(bf16[4,64,2816]{2,1,0:T(8,128)(2,1)} %bitcast.10), calls=%async_computation.1 | async-start | bytes 2883584 | tf_op jit(solution)/shard_map/all_to_all | solution.py:764
  87.0 212.5 %all-gather.2.cloned.1.call-start = ((), (), s32[]{:S(2)}) async-start(), calls=%async_computation.9 | async-start | bytes 12976128 | tf_op jit(solution)/shard_map/all_gather | solution.py:933
  87.0 20.9 %collective-permute-start.16 = (bf16[64,2048]{1,0:T(8,128)(2,1)}, bf16[64,2048]{1,0:T(8,128)(2,1)S(1)}, u32[]{:S(2)}, u32[]{:S(2)}) collective-permute-start(bf16[64,2048]{1,0:T(8,128)(2,1)} %collective-permute-done.11), channel_id=1, source_target_pairs={{0,2},{1,3},{2,0},{3,1},{4,6},{5,7},{6,4},{7,5},{8,10},{9,11},{10,... | collective-permute-start | bytes 786440 | tf_op jit(solution)/shard_map/ppermute | solution.py:761
  114.2 21.8 %all-to-all-start.2 = ((bf16[4,64,1408]{2,1,0:T(8,128)(2,1)}), bf16[4,64,1408]{2,1,0:T(8,128)(2,1)S(1)}, u32[]{:S(2)}, u32[]{:S(2)}) async-start(bf16[4,64,1408]{2,1,0:T(8,128)(2,1)} %bitcast.80), calls=%async_computation.2 | async-start | bytes 1441792 | tf_op jit(solution)/shard_map/all_to_all | solution.py:764
  137.6 88.3 %all-to-all-start.3 = ((bf16[4,128,2048]{2,1,0:T(8,128)(2,1)}), bf16[4,128,2048]{2,1,0:T(8,128)(2,1)S(1)}, u32[]{:S(2)}, u32[]{:S(2)}) async-start(bf16[4,128,2048]{2,1,0:T(8,128)(2,1)} %broadcast_in_dim.2), calls=%async_computation.3 | async-start | bytes 4194304 | tf_op jit(solution)/shard_map/all_to_all | solution.py:764
  142.4 330.3 %reduce-scatter.2.cloned.1.call-start = ((), (), s32[]{:S(2)}) async-start(), calls=%async_computation.10 | async-start | bytes 12976128 | tf_op jit(solution)/shard_map/reduce_scatter | solution.py:1012
  142.9 82.9 %collective-permute-start.22 = (bf16[256,1408]{1,0:T(8,128)(2,1)S(1)}, bf16[256,1408]{1,0:T(8,128)(2,1)S(1)}, u32[]{:S(2)}, u32[]{:S(2)}) collective-permute-start(bf16[256,1408]{1,0:T(8,128)(2,1)S(1)} %bitcast.77), channel_id=1, source_target_pairs={{0,2},{1,3},{2,0},{3,1},{4,6},{5,7},{6,4},{7,5},{8,10},{9,11},{10,... | collective-permute-start | bytes 2162696 | tf_op jit(solution)/shard_map/ppermute | solution.py:761
  155.4 22.2 %collective-permute-start.19 = (bf16[128,2048]{1,0:T(8,128)(2,1)}, bf16[128,2048]{1,0:T(8,128)(2,1)}, u32[]{:S(2)}, u32[]{:S(2)}) collective-permute-start(bf16[128,2048]{1,0:T(8,128)(2,1)} %get-tuple-element.202), channel_id=1, source_target_pairs={{0,1},{1,0},{2,3},{3,2},{4,5},{5,4},{6,7},{7,6},{8,9},{9,8},{10,11... | collective-permute-start | bytes 1572872 | tf_op jit(solution)/shard_map/ppermute | solution.py:761
  156.9 55.3 %collective-permute-start.20 = (bf16[128,2048]{1,0:T(8,128)(2,1)}, bf16[128,2048]{1,0:T(8,128)(2,1)}, u32[]{:S(2)}, u32[]{:S(2)}) collective-permute-start(bf16[128,2048]{1,0:T(8,128)(2,1)} %get-tuple-element.203), channel_id=1, source_target_pairs={{0,8},{1,9},{2,10},{3,11},{4,12},{5,13},{6,14},{7,15},{8,0},{9,1},... | collective-permute-start | bytes 1572872 | tf_op jit(solution)/shard_map/ppermute | solution.py:761
  157.5 68.4 %collective-permute-start.21 = (bf16[128,2048]{1,0:T(8,128)(2,1)}, bf16[128,2048]{1,0:T(8,128)(2,1)}, u32[]{:S(2)}, u32[]{:S(2)}) collective-permute-start(bf16[128,2048]{1,0:T(8,128)(2,1)} %get-tuple-element.204), channel_id=1, source_target_pairs={{0,9},{1,8},{2,11},{3,10},{4,13},{5,12},{6,15},{7,14},{8,1},{9,0},... | collective-permute-start | bytes 1572872 | tf_op jit(solution)/shard_map/ppermute | solution.py:761
  225.8 46.0 %collective-permute-start.26 = (bf16[256,1408]{1,0:T(8,128)(2,1)S(1)}, bf16[256,1408]{1,0:T(8,128)(2,1)S(1)}, u32[]{:S(2)}, u32[]{:S(2)}) collective-permute-start(bf16[256,1408]{1,0:T(8,128)(2,1)S(1)} %bitcast.78), channel_id=1, source_target_pairs={{0,16},{1,17},{2,18},{3,19},{4,20},{5,21},{6,22},{7,23},{8,24},{9,... | collective-permute-start | bytes 2162696 | tf_op jit(solution)/shard_map/ppermute | solution.py:761
  235.3 26.3 %collective-permute-start.24 = (bf16[128,2048]{1,0:T(8,128)(2,1)}, bf16[128,2048]{1,0:T(8,128)(2,1)S(1)}, u32[]{:S(2)}, u32[]{:S(2)}) collective-permute-start(bf16[128,2048]{1,0:T(8,128)(2,1)} %get-tuple-element.219), channel_id=1, source_target_pairs={{0,8},{1,9},{2,10},{3,11},{4,12},{5,13},{6,14},{7,15},{8,0},{9,1},... | collective-permute-start | bytes 1572872 | tf_op jit(solution)/shard_map/ppermute | solution.py:761
  235.4 36.5 %collective-permute-start.25 = (bf16[128,2048]{1,0:T(8,128)(2,1)}, bf16[128,2048]{1,0:T(8,128)(2,1)S(1)}, u32[]{:S(2)}, u32[]{:S(2)}) collective-permute-start(bf16[128,2048]{1,0:T(8,128)(2,1)} %get-tuple-element.219), channel_id=1, source_target_pairs={{0,9},{1,8},{2,11},{3,10},{4,13},{5,12},{6,15},{7,14},{8,1},{9,0},... | collective-permute-start | bytes 1572872 | tf_op jit(solution)/shard_map/ppermute | solution.py:761
  336.1 24.8 %collective-permute-start.31 = (bf16[128,2048]{1,0:T(8,128)(2,1)}, bf16[128,2048]{1,0:T(8,128)(2,1)S(1)}, u32[]{:S(2)}, u32[]{:S(2)}) collective-permute-start(bf16[128,2048]{1,0:T(8,128)(2,1)} %get-tuple-element.320), channel_id=1, source_target_pairs={{0,9},{1,8},{2,11},{3,10},{4,13},{5,12},{6,15},{7,14},{8,1},{9,0},... | collective-permute-start | bytes 1572872 | tf_op jit(solution)/shard_map/ppermute | solution.py:761
  364.3 32.4 %collective-permute-start.35 = (bf16[1024,1408]{1,0:T(8,128)(2,1)}, bf16[1024,1408]{1,0:T(8,128)(2,1)}, u32[]{:S(2)}, u32[]{:S(2)}) collective-permute-start(bf16[1024,1408]{1,0:T(8,128)(2,1)} %convolution_convert_fusion.1), channel_id=1, source_target_pairs={{0,4},{1,5},{2,6},{3,7},{4,0},{5,1},{6,2},{7,3},{8,12},{9,13},{10,... | collective-permute-start | bytes 8650760 | tf_op jit(solution)/shard_map/ppermute | solution.py:761
  368.7 34.2 %collective-permute-start.32 = (bf16[128,2048]{1,0:T(8,128)(2,1)}, bf16[128,2048]{1,0:T(8,128)(2,1)S(1)}, u32[]{:S(2)}, u32[]{:S(2)}) collective-permute-start(bf16[128,2048]{1,0:T(8,128)(2,1)} %get-tuple-element.294.rest_0_), channel_id=1, source_target_pairs={{0,1},{1,0},{2,3},{3,2},{4,5},{5,4},{6,7},{7,6},{8,9},{9,8},{10,11... | collective-permute-start | bytes 1572872 | tf_op jit(solution)/shard_map/ppermute | solution.py:761
  369.3 25.9 %collective-permute-start.33 = (bf16[128,2048]{1,0:T(8,128)(2,1)}, bf16[128,2048]{1,0:T(8,128)(2,1)S(1)}, u32[]{:S(2)}, u32[]{:S(2)}) collective-permute-start(bf16[128,2048]{1,0:T(8,128)(2,1)} %get-tuple-element.294.rest_0_), channel_id=1, source_target_pairs={{0,8},{1,9},{2,10},{3,11},{4,12},{5,13},{6,14},{7,15},{8,0},{9,1},... | collective-permute-start | bytes 1572872 | tf_op jit(solution)/shard_map/ppermute | solution.py:761
  413.9 53.5 %all-to-all-start.4 = ((bf16[4,128,2048]{2,1,0:T(8,128)(2,1)}), bf16[4,128,2048]{2,1,0:T(8,128)(2,1)S(1)}, u32[]{:S(2)}, u32[]{:S(2)}) async-start(bf16[4,128,2048]{2,1,0:T(8,128)(2,1)} %bitcast.68), calls=%async_computation.4 | async-start | bytes 4194304 | tf_op jit(solution)/shard_map/all_to_all | solution.py:764
  420.3 47.1 %collective-permute-start.36 = (bf16[512,1408]{1,0:T(8,128)(2,1)S(1)}, bf16[512,1408]{1,0:T(8,128)(2,1)}, u32[]{:S(2)}, u32[]{:S(2)}) collective-permute-start(bf16[512,1408]{1,0:T(8,128)(2,1)S(1)} %slice.223), channel_id=1, source_target_pairs={{0,2},{1,3},{2,0},{3,1},{4,6},{5,7},{6,4},{7,5},{8,10},{9,11},{10,... | collective-permute-start | bytes 4325384 | tf_op jit(solution)/shard_map/ppermute | solution.py:761
  472.6 43.4 %all-to-all-start.5 = ((bf16[4,64,2816]{2,1,0:T(8,128)(2,1)}), bf16[4,64,2816]{2,1,0:T(8,128)(2,1)S(1)}, u32[]{:S(2)}, u32[]{:S(2)}) async-start(bf16[4,64,2816]{2,1,0:T(8,128)(2,1)} %bitcast.82), calls=%async_computation.6 | async-start | bytes 2883584 | tf_op jit(solution)/shard_map/all_to_all | solution.py:764
  526.3 32.8 %collective-permute-start.45 = (bf16[128,2048]{1,0:T(8,128)(2,1)}, bf16[128,2048]{1,0:T(8,128)(2,1)S(1)}, u32[]{:S(2)}, u32[]{:S(2)}) collective-permute-start(bf16[128,2048]{1,0:T(8,128)(2,1)} %get-tuple-element.276), channel_id=1, source_target_pairs={{0,9},{1,8},{2,11},{3,10},{4,13},{5,12},{6,15},{7,14},{8,1},{9,0},... | collective-permute-start | bytes 1572872 | tf_op jit(solution)/shard_map/ppermute | solution.py:761
  536.5 22.5 %collective-permute-start.49 = (bf16[2,64,2048]{2,1,0:T(8,128)(2,1)S(1)}, bf16[2,64,2048]{2,1,0:T(8,128)(2,1)S(1)}, u32[]{:S(2)}, u32[]{:S(2)}) collective-permute-start(bf16[2,64,2048]{2,1,0:T(8,128)(2,1)S(1)} %slice.225), channel_id=1, source_target_pairs={{0,2},{1,3},{2,0},{3,1},{4,6},{5,7},{6,4},{7,5},{8,10},{9,11},{10,... | collective-permute-start | bytes 1572872 | tf_op jit(solution)/shard_map/ppermute | solution.py:761
  538.4 31.6 %collective-permute-start.47 = (bf16[256,1408]{1,0:T(8,128)(2,1)S(1)}, bf16[256,1408]{1,0:T(8,128)(2,1)S(1)}, u32[]{:S(2)}, u32[]{:S(2)}) collective-permute-start(bf16[256,1408]{1,0:T(8,128)(2,1)S(1)} %copy-done.30), channel_id=1, source_target_pairs={{0,16},{1,17},{2,18},{3,19},{4,20},{5,21},{6,22},{7,23},{8,24},{9,... | collective-permute-start | bytes 2162696 | tf_op jit(solution)/shard_map/ppermute | solution.py:761
  572.4 29.8 %collective-permute-start.52 = (bf16[1,256,512]{2,1,0:T(8,128)(2,1)}, bf16[1,256,512]{2,1,0:T(8,128)(2,1)}, u32[]{:S(2)}, u32[]{:S(2)}) collective-permute-start(bf16[1,256,512]{2,1,0:T(8,128)(2,1)} %slice.228), channel_id=1, source_target_pairs={{0,16},{1,17},{2,18},{3,19},{4,20},{5,21},{6,22},{7,23},{8,24},{9,... | collective-permute-start | bytes 786440 | tf_op jit(solution)/shard_map/ppermute | solution.py:761
  580.3 30.3 %collective-permute-start.53 = (bf16[1,64,2048]{2,1,0:T(8,128)(2,1)S(1)}, bf16[1,64,2048]{2,1,0:T(8,128)(2,1)}, u32[]{:S(2)}, u32[]{:S(2)}) collective-permute-start(bf16[1,64,2048]{2,1,0:T(8,128)(2,1)S(1)} %slice.227), channel_id=1, source_target_pairs={{0,16},{1,17},{2,18},{3,19},{4,20},{5,21},{6,22},{7,23},{8,24},{9,... | collective-permute-start | bytes 786440 | tf_op jit(solution)/shard_map/ppermute | solution.py:761
  605.9 22.8 %all-to-all-start.7 = ((bf16[4,64,1920]{2,1,0:T(8,128)(2,1)}), bf16[4,64,1920]{2,1,0:T(8,128)(2,1)S(1)}, u32[]{:S(2)}, u32[]{:S(2)}) async-start(bf16[4,64,1920]{2,1,0:T(8,128)(2,1)} %bitcast.34), calls=%async_computation.8 | async-start | bytes 1966080 | tf_op jit(solution)/shard_map/all_to_all | solution.py:764
  (96 other events, 1169.3 us)
Sparse Core Ops, SparseCore 0:
  109.1 114.7 all-gather.1
  332.3 134.7 reduce-scatter.1

commit v5 on v3

--- a/solution.py
+++ b/solution.py
@@ -1084,7 +1084,7 @@
         starts, d_query, kv_sum, cosine, sine, toks, qkv_k
     )
     d_hattn_blocks, query_got = lax.optimization_barrier((d_hattn_blocks, query_got))
-    query_keep, query_got = send(query_keep + query_got.astype(f32), far)
+    query_near = query_keep + query_got.astype(f32)
     d_hattn_parts = scatter_t(d_hattn_blocks)
     d_kv, gain_attn_part = hold((d_kv, gain_attn_part), d_hattn_blocks)
     if aligned:
@@ -1102,7 +1102,8 @@
     key_sum = core_sum((own, other))
     after = d_hattn_parts[1:]
     grad_gate, grad_up = unpack_columns(pair_parts, 2, "unpack_gate_up")
-    key_sum, query_got, out_got, down_got = hold((key_sum, query_got, out_got, down_got), after)
+    key_sum, query_near, out_got, down_got = hold((key_sum, query_near, out_got, down_got), after)
+    query_keep, query_got = send(query_near, far)
     d_hattn_parts, grad_gate, grad_up = lax.optimization_barrier((d_hattn_parts, grad_gate, grad_up))
     query_total = query_keep + query_got.astype(f32)
     out_total = (out_keep + out_got.astype(f32)).astype(bf16).reshape(slab, width)

time: 649 us -> 648 us (level)
    ppermute x53, starting transfers between devices: 60 us -> 66.7 us  [swap(): return lax.ppermute(value, AXES, [(i, i ^ mask) for i in range(n)])]
  transfers between devices with their start and end apart: 65 -> 65, of which waited for: 31 -> 31; matrix products, arithmetic and copies ran while one was open for 9% -> 8% of each run, Pallas kernels for 13% -> 13%
where the time goes in v5:
time: 648 us; the launch traced here: 637 us
  waiting for transfers between devices  314 us (48%)
  starting transfers between devices  110 us (17%)
  Pallas kernels  99.1 us (15%)
  matrix products  49.3 us (8%)
  other arithmetic  25.3 us (4%)
  local copies, waits for them, and re-layouts  23.9 us (4%)
  between operations  15.5 us (2%)
    ppermute x53, waiting for transfers between devices, swap(): return lax.ppermute(value, AXES, [(i, i ^ mask) for i in range(n)])  271 us
    pallas_call x22, Pallas kernels, call(): pl.pallas_call(kernel, out_shape=out_shape, in_specs=specs, out_specs=(VM...  99.1 us
    ppermute x53, starting transfers between devices, swap(): return lax.ppermute(value, AXES, [(i, i ^ mask) for i in range(n)])  66.7 us
    all_to_all x8, starting transfers between devices, trade(): lax.all_to_all(value, AXES, split_axis=0, concat_axis=0, tiled=True, axis...  37 us
    ppermute x1, waiting for transfers between devices, on_device(): lax.ppermute(hold(w_out, qkv_shard), AXES, [(i, goes_to(i)) for i in rang...  20.9 us
    dot_general x3, matrix products, dot_first(): lax.dot_general(a, b, (((0,), (0,)), ((), ())), preferred_element_type=f32)  18.9 us
    dot_general x3, matrix products, dot(): lax.dot_general(a, b, (((1,), (0,)), ((), ())), preferred_element_type=f32)  18 us
    all_to_all x8, waiting for transfers between devices, trade(): lax.all_to_all(value, AXES, split_axis=0, concat_axis=0, tiled=True, axis...  15.5 us
  transfers between devices with their start and end apart: 65, of which 31 were waited for; matrix products, arithmetic and copies ran while one was open for 8% of the time, Pallas kernels for 13%

profile of v5, /device:TPU:8, one launch (start us, length us, event | category | flops | bytes accessed | tf_op | source)
XLA Modules:
  0.0 637.0 jit_solution(8973945373554506062)
XLA Ops:
  13.2 6.2 all-to-all-done
  28.7 20.9 %collective-permute-done.10 = bf16[64,2048]{1,0:T(8,128)(2,1)S(1)} collective-permute-done((bf16[64,2048]{1,0:T(8,128)(2,1)}, bf16[64,2048]{1,0:T(8,128)(2,1)S(1)}, u32[]{:S(2)}, u32[]{:S(2)}) %collective-permute-start.10) | collective-permute-done | bytes 262176 | tf_op jit(solution)/shard_map/ppermute | solution.py:902
  75.3 6.6 %project.1 = (bf16[512,2048]{1,0:T(8,128)(2,1)}, bf16[4,2,128,512]{3,2,1,0:T(8,128)(2,1)}, bf16[128,512]{1,0:T(8,128)(2,1)}, f32[8,2048]{1,0:T(8,128)}) custom-call(s32[16]{0:T(128)} %fusion.24.starts, f32[32,512]{1,0:T(8,128)} %get-tuple-element.342.cos_ref, f32[32,512]{1,0:T(8,128)} %get-tuple-element.341.sin_ref, bf16[128,2048]{1,0:T(8,128)(2,1)} %rest_0_.1, ...), custom_call_target="tpu_custom_call" | custom-call | flops 1342177280 | bytes 8847424 | tf_op jit(solution)/shard_map/project/pallas_call | solution.py:78
  91.8 14.7 %collective-permute-done.13 = bf16[128,512]{1,0:T(8,128)(2,1)S(1)} collective-permute-done((bf16[128,512]{1,0:T(8,128)(2,1)S(1)}, bf16[128,512]{1,0:T(8,128)(2,1)S(1)}, u32[]{:S(2)}, u32[]{:S(2)}) %collective-permute-start.13) | collective-permute-done | bytes 131104 | tf_op jit(solution)/shard_map/ppermute | solution.py:761
  122.3 6.8 %attention_forward.2 = (f32[2,2,64,512]{3,2,1,0:T(8,128)}, f32[2,2,1,512]{3,2,1,0:T(1,128)}) custom-call(s32[4]{0:T(128)} %pad_add_fusion.me_ref.refs_0_, bf16[4,2,128,512]{3,2,1,0:T(8,128)(2,1)} %get-tuple-element.198.q_ref.refs_1_, bf16[2,4,128,512]{3,2,1,0:T(8,128)(2,1)} %pad_maximum_fusion.6.all_ref.refs_3_), custom_call_target="tpu_custom_call" | custom-call | flops 2147483648 | bytes 2629648 | tf_op jit(solution)/shard_map/attention_forward/pallas_call | solution.py:78
  129.1 6.6 %all-to-all-done.2 = bf16[4,64,1408]{2,1,0:T(8,128)(2,1)S(1)} async-done(((bf16[4,64,1408]{2,1,0:T(8,128)(2,1)}), bf16[4,64,1408]{2,1,0:T(8,128)(2,1)S(1)}, u32[]{:S(2)}, u32[]{:S(2)}) %all-to-all-start.2) | async-done | bytes 720928 | tf_op jit(solution)/shard_map/all_to_all | solution.py:764
  143.0 7.0 %attention_forward.3 = (f32[2,2,64,512]{3,2,1,0:T(8,128)}, f32[2,2,1,512]{3,2,1,0:T(1,128)}) custom-call(s32[4]{0:T(128)} %pad_add_fusion.me_ref.refs_0_, bf16[4,2,128,512]{3,2,1,0:T(8,128)(2,1)} %get-tuple-element.198.q_ref.refs_1_, bf16[2,4,128,512]{3,2,1,0:T(8,128)(2,1)} %pad_maximum_fusion.6.all_ref.refs_3_), custom_call_target="tpu_custom_call" | custom-call | flops 2147483648 | bytes 2629648 | tf_op jit(solution)/shard_map/attention_forward/pallas_call | solution.py:78
  149.9 5.6 out_products.1
  159.0 18.6 %collective-permute-done.19.rest_1_ = bf16[128,2048]{1,0:T(8,128)(2,1)} collective-permute-done((bf16[128,2048]{1,0:T(8,128)(2,1)}, bf16[128,2048]{1,0:T(8,128)(2,1)}, u32[]{:S(2)}, u32[]{:S(2)}) %collective-permute-start.19) | collective-permute-done | bytes 524320 | tf_op jit(solution)/shard_map/ppermute | solution.py:761
  177.6 34.4 %collective-permute-done.20.rest_2_ = bf16[128,2048]{1,0:T(8,128)(2,1)} collective-permute-done((bf16[128,2048]{1,0:T(8,128)(2,1)}, bf16[128,2048]{1,0:T(8,128)(2,1)}, u32[]{:S(2)}, u32[]{:S(2)}) %collective-permute-start.20) | collective-permute-done | bytes 524320 | tf_op jit(solution)/shard_map/ppermute | solution.py:761
  212.0 13.8 %collective-permute-done.21.rest_3_ = bf16[128,2048]{1,0:T(8,128)(2,1)} collective-permute-done((bf16[128,2048]{1,0:T(8,128)(2,1)}, bf16[128,2048]{1,0:T(8,128)(2,1)}, u32[]{:S(2)}, u32[]{:S(2)}) %collective-permute-start.21) | collective-permute-done | bytes 524320 | tf_op jit(solution)/shard_map/ppermute | solution.py:761
  239.0 10.1 %collective-permute-done.23 = bf16[128,2048]{1,0:T(8,128)(2,1)S(1)} collective-permute-done((bf16[128,2048]{1,0:T(8,128)(2,1)}, bf16[128,2048]{1,0:T(8,128)(2,1)S(1)}, u32[]{:S(2)}, u32[]{:S(2)}) %collective-permute-start.23) | collective-permute-done | bytes 524320 | tf_op jit(solution)/shard_map/ppermute | solution.py:761
  249.1 12.6 %collective-permute-done.24 = bf16[128,2048]{1,0:T(8,128)(2,1)S(1)} collective-permute-done((bf16[128,2048]{1,0:T(8,128)(2,1)}, bf16[128,2048]{1,0:T(8,128)(2,1)S(1)}, u32[]{:S(2)}, u32[]{:S(2)}) %collective-permute-start.24) | collective-permute-done | bytes 524320 | tf_op jit(solution)/shard_map/ppermute | solution.py:761
  261.7 10.3 %collective-permute-done.25 = bf16[128,2048]{1,0:T(8,128)(2,1)S(1)} collective-permute-done((bf16[128,2048]{1,0:T(8,128)(2,1)}, bf16[128,2048]{1,0:T(8,128)(2,1)S(1)}, u32[]{:S(2)}, u32[]{:S(2)}) %collective-permute-start.25) | collective-permute-done | bytes 524320 | tf_op jit(solution)/shard_map/ppermute | solution.py:761
  272.5 16.7 %collective-permute-done.27 = bf16[256,1408]{1,0:T(8,128)(2,1)S(1)} collective-permute-done((bf16[256,1408]{1,0:T(8,128)(2,1)S(1)}, bf16[256,1408]{1,0:T(8,128)(2,1)S(1)}, u32[]{:S(2)}, u32[]{:S(2)}) %collective-permute-start.27) | collective-permute-done | bytes 720928 | tf_op jit(solution)/shard_map/ppermute | solution.py:761
  299.7 10.8 %fusion.31 = f32[512,2816]{1,0:T(8,128)S(1)} fusion(bf16[512,2048]{1,0:T(8,128)(2,1)} %copy-done.44, bf16[2048,2816]{1,0:T(8,128)(2,1)} %all-gather.2.cloned.1.call-done), kind=kOutput, calls=%fused_computation.112 | convolution fusion | flops 5905580032 | bytes 19398656 | tf_op jit(solution)/shard_map/dot_general | solution.py:38
  314.4 6.4 %convolution_convert_fusion.2 = bf16[512,2048]{1,0:T(8,128)(2,1)S(1)} fusion(bf16[2048,2816]{1,0:T(8,128)(2,1)S(1)} %bitcast.92, bf16[512,1408]{1,0:T(8,128)(2,1)S(1)} %get-tuple-element.320, bf16[512,1408]{1,0:T(8,128)(2,1)S(1)} %get-tuple-element.319), kind=kOutput, calls=%fused_computation.4 | convolution fusion | flops 5912395776 | bytes 16515072 | tf_op jit(solution)/shard_map/dot_general | solution.py:42
  323.1 9.1 %convolution_convert_fusion = bf16[2048,2816]{1,0:T(8,128)(2,1)} fusion(bf16[512,2048]{1,0:T(8,128)(2,1)S(1)} %copy-done.45, bf16[512,1408]{1,0:T(8,128)(2,1)S(1)} %get-tuple-element.320, bf16[512,1408]{1,0:T(8,128)(2,1)S(1)} %get-tuple-element.319), kind=kOutput, calls=%fused_computation | convolution fusion | flops 5917114368 | bytes 16515072 | tf_op jit(solution)/shard_map/dot_general | solution.py:46
  349.3 11.7 %collective-permute-done.31.rest_3_ = bf16[128,2048]{1,0:T(8,128)(2,1)S(1)} collective-permute-done((bf16[128,2048]{1,0:T(8,128)(2,1)}, bf16[128,2048]{1,0:T(8,128)(2,1)S(1)}, u32[]{:S(2)}, u32[]{:S(2)}) %collective-permute-start.31) | collective-permute-done | bytes 524320 | tf_op jit(solution)/shard_map/ppermute | solution.py:761
  372.6 22.7 %collective-permute-done.33.rest_2_ = bf16[128,2048]{1,0:T(8,128)(2,1)S(1)} collective-permute-done((bf16[128,2048]{1,0:T(8,128)(2,1)}, bf16[128,2048]{1,0:T(8,128)(2,1)S(1)}, u32[]{:S(2)}, u32[]{:S(2)}) %collective-permute-start.33) | collective-permute-done | bytes 524320 | tf_op jit(solution)/shard_map/ppermute | solution.py:761
  396.7 6.3 convert_add_fusion
  403.0 5.5 collective-permute-done.34.rest_3_
  426.2 10.0 %attention_backward.2 = (f32[2,2,64,512]{3,2,1,0:T(8,128)}, f32[4096,128]{1,0:T(8,128)}) custom-call(s32[4]{0:T(128)} %pad_add_fusion.me_ref.refs_0_, bf16[4,2,128,512]{3,2,1,0:T(8,128)(2,1)} %get-tuple-element.198.q_ref.refs_1_, bf16[4,2,128,512]{3,2,1,0:T(8,128)(2,1)} %get-tuple-element.243.refs_2_, ...), custom_call_target="tpu_custom_call" | custom-call | flops 5368709120 | bytes 5791760 | tf_op jit(solution)/shard_map/attention_backward/pallas_call | solution.py:78
  440.2 10.8 %attention_backward.3 = (f32[2,2,64,512]{3,2,1,0:T(8,128)}, f32[4,512,128]{2,1,0:T(8,128)}, bf16[4,512,128]{2,1,0:T(8,128)(2,1)}) custom-call(s32[4]{0:T(128)} %pad_add_fusion.me_ref.refs_0_, bf16[4,2,128,512]{3,2,1,0:T(8,128)(2,1)} %get-tuple-element.198.q_ref.refs_1_, bf16[4,2,128,512]{3,2,1,0:T(8,128)(2,1)} %get-tuple-element.243.refs_2_, ...), custom_call_target="tpu_custom_call" | custom-call | flops 5368709120 | bytes 7364624 | tf_op jit(solution)/shard_map/attention_backward/pallas_call | solution.py:78
  450.9 23.9 %collective-permute-done.37 = bf16[512,1408]{1,0:T(8,128)(2,1)S(1)} collective-permute-done((bf16[512,1408]{1,0:T(8,128)(2,1)S(1)}, bf16[512,1408]{1,0:T(8,128)(2,1)S(1)}, u32[]{:S(2)}, u32[]{:S(2)}) %collective-permute-start.37) | collective-permute-done | bytes 1441824 | tf_op jit(solution)/shard_map/ppermute | solution.py:761
  476.0 9.9 %collective-permute-done.38 = bf16[2,64,2048]{2,1,0:T(8,128)(2,1)} collective-permute-done((bf16[2,64,2048]{2,1,0:T(8,128)(2,1)S(1)}, bf16[2,64,2048]{2,1,0:T(8,128)(2,1)}, u32[]{:S(2)}, u32[]{:S(2)}) %collective-permute-start.38) | collective-permute-done | bytes 524320 | tf_op jit(solution)/shard_map/ppermute | solution.py:761
  520.9 6.6 %back_project.1 = (bf16[128,2048]{1,0:T(8,128)(2,1)}, bf16[128,2048]{1,0:T(8,128)(2,1)}, bf16[128,2048]{1,0:T(8,128)(2,1)}, bf16[128,2048]{1,0:T(8,128)(2,1)}, b...) custom-call(s32[16]{0:T(128)} %fusion.24.starts, bf16[512,512]{1,0:T(8,128)(2,1)} %back_query.1.d_ref.dq_ref, ...), custom_call_target="tpu_custom_call" | custom-call | flops 1342177280 | bytes 8527936 | tf_op jit(solution)/shard_map/back_project/pallas_call | solution.py:78
  539.6 22.4 %collective-permute-done.49 = bf16[1,64,2048]{2,1,0:T(8,128)(2,1)S(1)} collective-permute-done((bf16[1,64,2048]{2,1,0:T(8,128)(2,1)S(1)}, bf16[1,64,2048]{2,1,0:T(8,128)(2,1)S(1)}, u32[]{:S(2)}, u32[]{:S(2)}) %collective-permute-start.49) | collective-permute-done | bytes 262176 | tf_op jit(solution)/shard_map/ppermute | solution.py:761
  561.9 10.2 %collective-permute-done.47 = bf16[128,2048]{1,0:T(8,128)(2,1)S(1)} collective-permute-done((bf16[128,2048]{1,0:T(8,128)(2,1)S(1)}, bf16[128,2048]{1,0:T(8,128)(2,1)S(1)}, u32[]{:S(2)}, u32[]{:S(2)}) %collective-permute-start.47) | collective-permute-done | bytes 524320 | tf_op jit(solution)/shard_map/ppermute | solution.py:761
  573.3 6.8 %collective-permute-start.53 = (bf16[1,256,512]{2,1,0:T(8,128)(2,1)S(1)}, bf16[1,256,512]{2,1,0:T(8,128)(2,1)S(1)}, u32[]{:S(2)}, u32[]{:S(2)}) collective-permute-start(bf16[1,256,512]{2,1,0:T(8,128)(2,1)S(1)} %slice.229), channel_id=1, source_target_pairs={{0,16},{1,17},{2,18},{3,19},{4,20},{5,21},{6,22},{7,23},{8,24},{9,... | collective-permute-start | bytes 786440 | tf_op jit(solution)/shard_map/ppermute | solution.py:761
  585.3 7.5 %collective-permute-done.52 = bf16[1,320,128]{2,1,0:T(8,128)(2,1)S(1)} collective-permute-done((bf16[1,320,128]{2,1,0:T(8,128)(2,1)S(1)}, bf16[1,320,128]{2,1,0:T(8,128)(2,1)S(1)}, u32[]{:S(2)}, u32[]{:S(2)}) %collective-permute-start.52) | collective-permute-done | bytes 81952 | tf_op jit(solution)/shard_map/ppermute | solution.py:761
  615.4 7.0 %collective-permute-done.54 = bf16[64,2048]{1,0:T(8,128)(2,1)S(1)} collective-permute-done((bf16[64,2048]{1,0:T(8,128)(2,1)}, bf16[64,2048]{1,0:T(8,128)(2,1)S(1)}, u32[]{:S(2)}, u32[]{:S(2)}) %collective-permute-start.54) | collective-permute-done | bytes 262176 | tf_op jit(solution)/shard_map/ppermute | solution.py:1112
  (319 shorter events, 242.9 us)
Async XLA Ops:
  19.4 30.2 %collective-permute-start = (bf16[320,640]{1,0:T(8,128)(2,1)S(1)}, bf16[320,640]{1,0:T(8,128)(2,1)S(1)}, u32[]{:S(2)}, u32[]{:S(2)}) collective-permute-start(bf16[320,640]{1,0:T(8,128)(2,1)S(1)} %bitcast.71), channel_id=1, source_target_pairs={{0,16},{1,17},{2,18},{3,19},{4,20},{5,21},{6,22},{7,23},{8,24},{9,... | collective-permute-start | bytes 1228808 | tf_op jit(solution)/shard_map/ppermute | solution.py:761
  22.7 26.9 %collective-permute-start.10 = (bf16[64,2048]{1,0:T(8,128)(2,1)}, bf16[64,2048]{1,0:T(8,128)(2,1)S(1)}, u32[]{:S(2)}, u32[]{:S(2)}) collective-permute-start(bf16[64,2048]{1,0:T(8,128)(2,1)} %param.21), channel_id=1, source_target_pairs={{0,0},{1,16},{2,2},{3,18},{4,4},{5,20},{6,6},{7,22},{8,1},{9,17},{... | collective-permute-start | bytes 786440 | tf_op jit(solution)/shard_map/ppermute | solution.py:902
  26.1 25.8 %collective-permute-start.1 = (bf16[320,640]{1,0:T(8,128)(2,1)S(1)}, bf16[320,640]{1,0:T(8,128)(2,1)S(1)}, u32[]{:S(2)}, u32[]{:S(2)}) collective-permute-start(bf16[320,640]{1,0:T(8,128)(2,1)S(1)} %bitcast.72), channel_id=1, source_target_pairs={{0,2},{1,3},{2,0},{3,1},{4,6},{5,7},{6,4},{7,5},{8,10},{9,11},{10,... | collective-permute-start | bytes 1228808 | tf_op jit(solution)/shard_map/ppermute | solution.py:761
  27.7 29.2 %collective-permute-start.7 = (bf16[128,2048]{1,0:T(8,128)(2,1)}, bf16[128,2048]{1,0:T(8,128)(2,1)S(1)}, u32[]{:S(2)}, u32[]{:S(2)}) collective-permute-start(bf16[128,2048]{1,0:T(8,128)(2,1)} %rest_0_.1), channel_id=1, source_target_pairs={{0,1},{1,0},{2,3},{3,2},{4,5},{5,4},{6,7},{7,6},{8,9},{9,8},{10,11... | collective-permute-start | bytes 1572872 | tf_op jit(solution)/shard_map/ppermute | solution.py:761
  27.7 29.2 %collective-permute-start.8 = (bf16[128,2048]{1,0:T(8,128)(2,1)}, bf16[128,2048]{1,0:T(8,128)(2,1)S(1)}, u32[]{:S(2)}, u32[]{:S(2)}) collective-permute-start(bf16[128,2048]{1,0:T(8,128)(2,1)} %rest_0_.1), channel_id=1, source_target_pairs={{0,8},{1,9},{2,10},{3,11},{4,12},{5,13},{6,14},{7,15},{8,0},{9,1},... | collective-permute-start | bytes 1572872 | tf_op jit(solution)/shard_map/ppermute | solution.py:761
  52.0 22.2 %collective-permute-start.9 = (bf16[128,2048]{1,0:T(8,128)(2,1)}, bf16[128,2048]{1,0:T(8,128)(2,1)S(1)}, u32[]{:S(2)}, u32[]{:S(2)}) collective-permute-start(bf16[128,2048]{1,0:T(8,128)(2,1)} %rest_0_.1), channel_id=1, source_target_pairs={{0,9},{1,8},{2,11},{3,10},{4,13},{5,12},{6,15},{7,14},{8,1},{9,0},... | collective-permute-start | bytes 1572872 | tf_op jit(solution)/shard_map/ppermute | solution.py:761
  81.9 25.9 %all-to-all-start.1 = ((bf16[4,64,2816]{2,1,0:T(8,128)(2,1)}), bf16[4,64,2816]{2,1,0:T(8,128)(2,1)S(1)}, u32[]{:S(2)}, u32[]{:S(2)}) async-start(bf16[4,64,2816]{2,1,0:T(8,128)(2,1)} %bitcast.10), calls=%async_computation.1 | async-start | bytes 2883584 | tf_op jit(solution)/shard_map/all_to_all | solution.py:764
  86.9 212.8 %all-gather.2.cloned.1.call-start = ((), (), s32[]{:S(2)}) async-start(), calls=%async_computation.9 | async-start | bytes 12976128 | tf_op jit(solution)/shard_map/all_gather | solution.py:933
  114.2 21.6 %all-to-all-start.2 = ((bf16[4,64,1408]{2,1,0:T(8,128)(2,1)}), bf16[4,64,1408]{2,1,0:T(8,128)(2,1)S(1)}, u32[]{:S(2)}, u32[]{:S(2)}) async-start(bf16[4,64,1408]{2,1,0:T(8,128)(2,1)} %bitcast.79), calls=%async_computation.2 | async-start | bytes 1441792 | tf_op jit(solution)/shard_map/all_to_all | solution.py:764
  137.4 88.4 %all-to-all-start.3 = ((bf16[4,128,2048]{2,1,0:T(8,128)(2,1)}), bf16[4,128,2048]{2,1,0:T(8,128)(2,1)S(1)}, u32[]{:S(2)}, u32[]{:S(2)}) async-start(bf16[4,128,2048]{2,1,0:T(8,128)(2,1)} %broadcast_in_dim.2), calls=%async_computation.3 | async-start | bytes 4194304 | tf_op jit(solution)/shard_map/all_to_all | solution.py:764
  142.2 347.2 %reduce-scatter.2.cloned.1.call-start = ((), (), s32[]{:S(2)}) async-start(), calls=%async_computation.10 | async-start | bytes 12976128 | tf_op jit(solution)/shard_map/reduce_scatter | solution.py:1012
  142.7 83.1 %collective-permute-start.22 = (bf16[256,1408]{1,0:T(8,128)(2,1)S(1)}, bf16[256,1408]{1,0:T(8,128)(2,1)S(1)}, u32[]{:S(2)}, u32[]{:S(2)}) collective-permute-start(bf16[256,1408]{1,0:T(8,128)(2,1)S(1)} %bitcast.76), channel_id=1, source_target_pairs={{0,2},{1,3},{2,0},{3,1},{4,6},{5,7},{6,4},{7,5},{8,10},{9,11},{10,... | collective-permute-start | bytes 2162696 | tf_op jit(solution)/shard_map/ppermute | solution.py:761
  155.5 22.1 %collective-permute-start.19 = (bf16[128,2048]{1,0:T(8,128)(2,1)}, bf16[128,2048]{1,0:T(8,128)(2,1)}, u32[]{:S(2)}, u32[]{:S(2)}) collective-permute-start(bf16[128,2048]{1,0:T(8,128)(2,1)} %get-tuple-element.205), channel_id=1, source_target_pairs={{0,1},{1,0},{2,3},{3,2},{4,5},{5,4},{6,7},{7,6},{8,9},{9,8},{10,11... | collective-permute-start | bytes 1572872 | tf_op jit(solution)/shard_map/ppermute | solution.py:761
  157.0 55.0 %collective-permute-start.20 = (bf16[128,2048]{1,0:T(8,128)(2,1)}, bf16[128,2048]{1,0:T(8,128)(2,1)}, u32[]{:S(2)}, u32[]{:S(2)}) collective-permute-start(bf16[128,2048]{1,0:T(8,128)(2,1)} %get-tuple-element.206), channel_id=1, source_target_pairs={{0,8},{1,9},{2,10},{3,11},{4,12},{5,13},{6,14},{7,15},{8,0},{9,1},... | collective-permute-start | bytes 1572872 | tf_op jit(solution)/shard_map/ppermute | solution.py:761
  157.6 68.2 %collective-permute-start.21 = (bf16[128,2048]{1,0:T(8,128)(2,1)}, bf16[128,2048]{1,0:T(8,128)(2,1)}, u32[]{:S(2)}, u32[]{:S(2)}) collective-permute-start(bf16[128,2048]{1,0:T(8,128)(2,1)} %get-tuple-element.207), channel_id=1, source_target_pairs={{0,9},{1,8},{2,11},{3,10},{4,13},{5,12},{6,15},{7,14},{8,1},{9,0},... | collective-permute-start | bytes 1572872 | tf_op jit(solution)/shard_map/ppermute | solution.py:761
  225.8 46.2 %collective-permute-start.26 = (bf16[256,1408]{1,0:T(8,128)(2,1)S(1)}, bf16[256,1408]{1,0:T(8,128)(2,1)S(1)}, u32[]{:S(2)}, u32[]{:S(2)}) collective-permute-start(bf16[256,1408]{1,0:T(8,128)(2,1)S(1)} %bitcast.77), channel_id=1, source_target_pairs={{0,16},{1,17},{2,18},{3,19},{4,20},{5,21},{6,22},{7,23},{8,24},{9,... | collective-permute-start | bytes 2162696 | tf_op jit(solution)/shard_map/ppermute | solution.py:761
  235.3 26.4 %collective-permute-start.24 = (bf16[128,2048]{1,0:T(8,128)(2,1)}, bf16[128,2048]{1,0:T(8,128)(2,1)S(1)}, u32[]{:S(2)}, u32[]{:S(2)}) collective-permute-start(bf16[128,2048]{1,0:T(8,128)(2,1)} %get-tuple-element.222), channel_id=1, source_target_pairs={{0,8},{1,9},{2,10},{3,11},{4,12},{5,13},{6,14},{7,15},{8,0},{9,1},... | collective-permute-start | bytes 1572872 | tf_op jit(solution)/shard_map/ppermute | solution.py:761
  235.3 36.7 %collective-permute-start.25 = (bf16[128,2048]{1,0:T(8,128)(2,1)}, bf16[128,2048]{1,0:T(8,128)(2,1)S(1)}, u32[]{:S(2)}, u32[]{:S(2)}) collective-permute-start(bf16[128,2048]{1,0:T(8,128)(2,1)} %get-tuple-element.222), channel_id=1, source_target_pairs={{0,9},{1,8},{2,11},{3,10},{4,13},{5,12},{6,15},{7,14},{8,1},{9,0},... | collective-permute-start | bytes 1572872 | tf_op jit(solution)/shard_map/ppermute | solution.py:761
  336.2 24.8 %collective-permute-start.31 = (bf16[128,2048]{1,0:T(8,128)(2,1)}, bf16[128,2048]{1,0:T(8,128)(2,1)S(1)}, u32[]{:S(2)}, u32[]{:S(2)}) collective-permute-start(bf16[128,2048]{1,0:T(8,128)(2,1)} %get-tuple-element.326), channel_id=1, source_target_pairs={{0,9},{1,8},{2,11},{3,10},{4,13},{5,12},{6,15},{7,14},{8,1},{9,0},... | collective-permute-start | bytes 1572872 | tf_op jit(solution)/shard_map/ppermute | solution.py:761
  364.4 32.4 %collective-permute-start.35 = (bf16[1024,1408]{1,0:T(8,128)(2,1)}, bf16[1024,1408]{1,0:T(8,128)(2,1)}, u32[]{:S(2)}, u32[]{:S(2)}) collective-permute-start(bf16[1024,1408]{1,0:T(8,128)(2,1)} %convolution_convert_fusion.1), channel_id=1, source_target_pairs={{0,4},{1,5},{2,6},{3,7},{4,0},{5,1},{6,2},{7,3},{8,12},{9,13},{10,... | collective-permute-start | bytes 8650760 | tf_op jit(solution)/shard_map/ppermute | solution.py:761
  368.7 34.3 %collective-permute-start.32 = (bf16[128,2048]{1,0:T(8,128)(2,1)}, bf16[128,2048]{1,0:T(8,128)(2,1)S(1)}, u32[]{:S(2)}, u32[]{:S(2)}) collective-permute-start(bf16[128,2048]{1,0:T(8,128)(2,1)} %get-tuple-element.249.rest_0_), channel_id=1, source_target_pairs={{0,1},{1,0},{2,3},{3,2},{4,5},{5,4},{6,7},{7,6},{8,9},{9,8},{10,11... | collective-permute-start | bytes 1572872 | tf_op jit(solution)/shard_map/ppermute | solution.py:761
  369.4 25.9 %collective-permute-start.33 = (bf16[128,2048]{1,0:T(8,128)(2,1)}, bf16[128,2048]{1,0:T(8,128)(2,1)S(1)}, u32[]{:S(2)}, u32[]{:S(2)}) collective-permute-start(bf16[128,2048]{1,0:T(8,128)(2,1)} %get-tuple-element.249.rest_0_), channel_id=1, source_target_pairs={{0,8},{1,9},{2,10},{3,11},{4,12},{5,13},{6,14},{7,15},{8,0},{9,1},... | collective-permute-start | bytes 1572872 | tf_op jit(solution)/shard_map/ppermute | solution.py:761
  414.2 71.6 %all-to-all-start.4 = ((bf16[4,128,2048]{2,1,0:T(8,128)(2,1)}), bf16[4,128,2048]{2,1,0:T(8,128)(2,1)S(1)}, u32[]{:S(2)}, u32[]{:S(2)}) async-start(bf16[4,128,2048]{2,1,0:T(8,128)(2,1)} %bitcast.68), calls=%async_computation.4 | async-start | bytes 4194304 | tf_op jit(solution)/shard_map/all_to_all | solution.py:764
  425.0 49.9 %collective-permute-start.37 = (bf16[512,1408]{1,0:T(8,128)(2,1)S(1)}, bf16[512,1408]{1,0:T(8,128)(2,1)S(1)}, u32[]{:S(2)}, u32[]{:S(2)}) collective-permute-start(bf16[512,1408]{1,0:T(8,128)(2,1)S(1)} %slice.225), channel_id=1, source_target_pairs={{0,2},{1,3},{2,0},{3,1},{4,6},{5,7},{6,4},{7,5},{8,10},{9,11},{10,... | collective-permute-start | bytes 4325384 | tf_op jit(solution)/shard_map/ppermute | solution.py:761
  439.3 46.5 %collective-permute-start.38 = (bf16[2,64,2048]{2,1,0:T(8,128)(2,1)S(1)}, bf16[2,64,2048]{2,1,0:T(8,128)(2,1)}, u32[]{:S(2)}, u32[]{:S(2)}) collective-permute-start(bf16[2,64,2048]{2,1,0:T(8,128)(2,1)S(1)} %slice.228), channel_id=1, source_target_pairs={{0,2},{1,3},{2,0},{3,1},{4,6},{5,7},{6,4},{7,5},{8,10},{9,11},{10,... | collective-permute-start | bytes 1572872 | tf_op jit(solution)/shard_map/ppermute | solution.py:761
  504.1 89.4 %all-to-all-start.5 = ((bf16[4,64,2816]{2,1,0:T(8,128)(2,1)}), bf16[4,64,2816]{2,1,0:T(8,128)(2,1)}, u32[]{:S(2)}, u32[]{:S(2)}) async-start(bf16[4,64,2816]{2,1,0:T(8,128)(2,1)} %bitcast.27), calls=%async_computation.6 | async-start | bytes 2883584 | tf_op jit(solution)/shard_map/all_to_all | solution.py:764
  517.2 44.7 %collective-permute-start.50 = (bf16[256,1408]{1,0:T(8,128)(2,1)}, bf16[256,1408]{1,0:T(8,128)(2,1)}, u32[]{:S(2)}, u32[]{:S(2)}) collective-permute-start(bf16[256,1408]{1,0:T(8,128)(2,1)} %slice.226), channel_id=1, source_target_pairs={{0,16},{1,17},{2,18},{3,19},{4,20},{5,21},{6,22},{7,23},{8,24},{9,... | collective-permute-start | bytes 2162696 | tf_op jit(solution)/shard_map/ppermute | solution.py:761
  532.4 29.5 %collective-permute-start.49 = (bf16[1,64,2048]{2,1,0:T(8,128)(2,1)S(1)}, bf16[1,64,2048]{2,1,0:T(8,128)(2,1)S(1)}, u32[]{:S(2)}, u32[]{:S(2)}) collective-permute-start(bf16[1,64,2048]{2,1,0:T(8,128)(2,1)S(1)} %slice.230), channel_id=1, source_target_pairs={{0,16},{1,17},{2,18},{3,19},{4,20},{5,21},{6,22},{7,23},{8,24},{9,... | collective-permute-start | bytes 786440 | tf_op jit(solution)/shard_map/ppermute | solution.py:761
  534.8 27.2 %collective-permute-start.45 = (bf16[128,2048]{1,0:T(8,128)(2,1)}, bf16[128,2048]{1,0:T(8,128)(2,1)S(1)}, u32[]{:S(2)}, u32[]{:S(2)}) collective-permute-start(bf16[128,2048]{1,0:T(8,128)(2,1)} %get-tuple-element.286), channel_id=1, source_target_pairs={{0,1},{1,0},{2,3},{3,2},{4,5},{5,4},{6,7},{7,6},{8,9},{9,8},{10,11... | collective-permute-start | bytes 1572872 | tf_op jit(solution)/shard_map/ppermute | solution.py:761
  536.7 25.2 %collective-permute-start.46 = (bf16[128,2048]{1,0:T(8,128)(2,1)S(1)}, bf16[128,2048]{1,0:T(8,128)(2,1)S(1)}, u32[]{:S(2)}, u32[]{:S(2)}) collective-permute-start(bf16[128,2048]{1,0:T(8,128)(2,1)S(1)} %copy-done.55), channel_id=1, source_target_pairs={{0,8},{1,9},{2,10},{3,11},{4,12},{5,13},{6,14},{7,15},{8,0},{9,1},... | collective-permute-start | bytes 1572872 | tf_op jit(solution)/shard_map/ppermute | solution.py:761
  536.8 35.4 %collective-permute-start.47 = (bf16[128,2048]{1,0:T(8,128)(2,1)S(1)}, bf16[128,2048]{1,0:T(8,128)(2,1)S(1)}, u32[]{:S(2)}, u32[]{:S(2)}) collective-permute-start(bf16[128,2048]{1,0:T(8,128)(2,1)S(1)} %copy-done.54), channel_id=1, source_target_pairs={{0,9},{1,8},{2,11},{3,10},{4,13},{5,12},{6,15},{7,14},{8,1},{9,0},... | collective-permute-start | bytes 1572872 | tf_op jit(solution)/shard_map/ppermute | solution.py:761
  601.8 24.4 %all-to-all-start.7 = ((bf16[4,64,1920]{2,1,0:T(8,128)(2,1)}), bf16[4,64,1920]{2,1,0:T(8,128)(2,1)S(1)}, u32[]{:S(2)}, u32[]{:S(2)}) async-start(bf16[4,64,1920]{2,1,0:T(8,128)(2,1)} %bitcast.34), calls=%async_computation.8 | async-start | bytes 1966080 | tf_op jit(solution)/shard_map/all_to_all | solution.py:764
  (95 other events, 1002.4 us)
Sparse Core Ops, SparseCore 0:
  109.1 114.6 all-gather.1
  332.4 135.6 reduce-scatter.1
